TPU v7x, 128 devices: a whole 4x4x4 slice. The times are simulated.
128 devices in a mesh: row: 8 (over y_hi, z), col: 16 (over y_lo, x, core).
Axes of the slice: x: 4, y: 4 (y_hi: 2, y_lo: 2; y = y_hi * 2 + y_lo), z: 4, core: 2. Of those that a mesh axis runs over, the one named last changes fastest.
Arguments:
- tokens: bfloat16 [256, 256, 512], P('row', 'col'), may hold values from -6 to 6
- norm_gains: float32 [4, 512], replicated, may hold values from 0.1 to 1.9
- qkv_weight: bfloat16 [2, 512, 1536], replicated, may hold values from -1 to 1
- rel_bias: float32 [2, 16, 13, 13], replicated, may hold values from -4 to 4
- proj_weight: bfloat16 [2, 512, 512], replicated, may hold values from -0.5 to 0.5
- up_weight: bfloat16 [2, 512, 2048], replicated, may hold values from -0.25 to 0.25
- down_weight: bfloat16 [2, 2048, 512], replicated, may hold values from -0.125 to 0.125
Outputs:
- features: bfloat16 [256, 256, 512], P('row', 'col')
All inputs are finite; a program needn't handle non-finite values.
Results may differ from a plain program's by a relative error of at most 0.014.
Values may be sent and summed in bfloat16 or wider, within the bound.
No kernel may reach another device: no remote copies, remote signals or barrier semaphores. Data moves between devices by JAX's collectives and lax.ppermute only.
A program may use at most 320 MiB of HBM per device.

v0:
```python
import jax
import jax.numpy as jnp
from jax import lax
from jax.sharding import PartitionSpec as P

DILATION = 16


def padded_2(cells, sides, width):
    for axis, dim in sides:
        count = lax.axis_size(axis)
        ends = count - 1
        head = lax.slice_in_dim(cells, 0, width, axis=dim)
        tail = lax.slice_in_dim(cells, cells.shape[dim] - width, cells.shape[dim], axis=dim)
        cells = jnp.concatenate(
            [
                lax.ppermute(tail, axis, [(i, (i + 1) % count) for i in range(ends)]),
                cells,
                lax.ppermute(head, axis, [((i + 1) % count, i) for i in range(ends)]),
            ],
            axis=dim,
        )
    return cells


def window_starts(positions, extent):
    return jnp.clip(positions - 3, 0, extent - 7)


def layer_norm(rows_in, norm_gain):
    values_f = rows_in.astype(jnp.float32)
    mean_value = jnp.mean(values_f, axis=-1, keepdims=True)
    centred = values_f - mean_value
    variance = jnp.mean(centred * centred, axis=-1, keepdims=True)
    return (centred * lax.rsqrt(variance + 1e-05) * norm_gain).astype(jnp.bfloat16)


def window_attend(
    queries, key_block, value_block, row_start, col_start, row_shift, col_shift, rel_table
):
    query_rows, query_cols, group_count, feature_width = queries.shape
    head_count = rel_table.shape[0]
    head_size = feature_width // head_count
    token_count = query_rows * query_cols * group_count
    query_flat = queries.reshape(token_count, feature_width)
    head_ones = (
        jnp.arange(feature_width, dtype=jnp.int32)[None, :] // head_size
        == jnp.arange(head_count, dtype=jnp.int32)[:, None]
    ).astype(jnp.float32)
    head_mask = head_ones.astype(jnp.bfloat16)
    classes = jnp.arange(13, dtype=jnp.int32)
    col_hots = [
        ((col_shift + across + 6)[:, None] == classes).astype(jnp.float32) for across in range(7)
    ]
    scaling = head_size ** (-0.5)
    score_list = []
    for offset in range(7):
        key_rows = jnp.take(key_block, row_start + offset, axis=0)
        row_hot = ((row_shift + offset + 6)[:, None] == classes).astype(jnp.float32)
        for across in range(7):
            window = jnp.take(key_rows, col_start + across, axis=1).reshape(
                token_count, feature_width
            )
            product = query_flat.astype(jnp.float32) * window.astype(jnp.float32)
            partial_score = jnp.einsum(
                "nd,td->nt", head_ones, product, precision=lax.Precision.HIGHEST
            )
            bias_term = jnp.einsum(
                "iy,cz,nyz->nic",
                row_hot,
                col_hots[across],
                rel_table,
                precision=lax.Precision.HIGHEST,
            )
            bias_full = jnp.broadcast_to(
                bias_term[:, :, :, None], (head_count, query_rows, query_cols, group_count)
            ).reshape(head_count, token_count)
            score_list.append(partial_score * scaling + bias_full)
    scores = jnp.stack(score_list)
    row_max = jnp.max(scores, axis=0, keepdims=True)
    exponent = jnp.exp(scores - row_max)
    weights = (exponent / jnp.sum(exponent, axis=0, keepdims=True)).astype(jnp.bfloat16)
    running = jnp.zeros((token_count, feature_width), jnp.float32)
    for offset in range(7):
        value_rows = jnp.take(value_block, row_start + offset, axis=0)
        for across in range(7):
            window = jnp.take(value_rows, col_start + across, axis=1).reshape(
                token_count, feature_width
            )
            spread = jnp.einsum(
                "nt,nd->td",
                weights[offset * 7 + across],
                head_mask,
                preferred_element_type=jnp.float32,
            )
            running = running + spread * window.astype(jnp.float32)
    return running.reshape(query_rows, query_cols, group_count, feature_width).astype(jnp.bfloat16)


def finish_layer(attended, stream, norm_gain, proj, up_proj, down_proj):
    mixed = (
        jnp.dot(attended, proj, preferred_element_type=jnp.float32) + stream.astype(jnp.float32)
    ).astype(jnp.bfloat16)
    normed = layer_norm(mixed, norm_gain)
    hidden = jax.nn.gelu(
        jnp.dot(normed, up_proj, preferred_element_type=jnp.float32), approximate=True
    ).astype(jnp.bfloat16)
    return (
        jnp.dot(hidden, down_proj, preferred_element_type=jnp.float32) + mixed.astype(jnp.float32)
    ).astype(jnp.bfloat16)


def body(tokens, norm_gains, qkv_weight, rel_bias, proj_weight, up_weight, down_weight):
    tile_rows, tile_cols, feature_width = tokens.shape
    row_count = lax.axis_size("row")
    col_count = lax.axis_size("col")
    map_rows = tile_rows * row_count
    map_cols = tile_cols * col_count
    stream_rows = tokens.reshape(-1, feature_width)
    normed = layer_norm(stream_rows, norm_gains[0])
    packed = jnp.dot(normed, qkv_weight[0], preferred_element_type=jnp.float32).astype(jnp.bfloat16)
    queries = packed[:, :feature_width]
    kv_pair = packed[:, feature_width:].reshape(tile_rows, tile_cols, 2 * feature_width)
    padded = padded_2(kv_pair, (("row", 0), ("col", 1)), 3)
    key_block = padded[:, :, None, :feature_width]
    value_block = padded[:, :, None, feature_width:]
    first_row = lax.axis_index("row") * tile_rows
    first_col = lax.axis_index("col") * tile_cols
    row_global = first_row + jnp.arange(tile_rows, dtype=jnp.int32)
    col_global = first_col + jnp.arange(tile_cols, dtype=jnp.int32)
    row_begin = window_starts(row_global, map_rows)
    col_begin = window_starts(col_global, map_cols)
    attended = window_attend(
        queries.reshape(tile_rows, tile_cols, 1, feature_width),
        key_block,
        value_block,
        row_begin - first_row + 3,
        col_begin - first_col + 3,
        row_begin - row_global,
        col_begin - col_global,
        rel_bias[0],
    )
    stream_rows = finish_layer(
        attended.reshape(-1, feature_width),
        stream_rows,
        norm_gains[1],
        proj_weight[0],
        up_weight[0],
        down_weight[0],
    )
    residue_rows = DILATION // row_count
    residue_cols = DILATION // col_count
    block_rows = tile_rows // DILATION
    block_cols = tile_cols // DILATION
    group_rows = block_rows * row_count
    group_cols = block_cols * col_count
    group_count = residue_rows * residue_cols
    shaped = stream_rows.reshape(
        block_rows, row_count, residue_rows, block_cols, col_count, residue_cols, feature_width
    )
    shaped = shaped.transpose(1, 4, 2, 5, 0, 3, 6).reshape(
        row_count * col_count, residue_rows, residue_cols, block_rows * block_cols, feature_width
    )
    arrived = lax.all_to_all(shaped, ("row", "col"), split_axis=0, concat_axis=0, tiled=True)
    grouped = arrived.reshape(
        row_count, col_count, residue_rows, residue_cols, block_rows, block_cols, feature_width
    )
    grouped = grouped.transpose(0, 4, 1, 5, 2, 3, 6).reshape(
        group_rows, group_cols, group_count, feature_width
    )
    grouped_rows = grouped.reshape(-1, feature_width)
    packed_two = jnp.dot(
        layer_norm(grouped_rows, norm_gains[2]), qkv_weight[1], preferred_element_type=jnp.float32
    ).astype(jnp.bfloat16)
    packed_two = packed_two.reshape(group_rows, group_cols, group_count, 3 * feature_width)
    bordered = jnp.pad(packed_two[..., feature_width:], ((3, 3), (3, 3), (0, 0), (0, 0)))
    grow_places = jnp.arange(group_rows, dtype=jnp.int32)
    gcol_places = jnp.arange(group_cols, dtype=jnp.int32)
    grow_begin = window_starts(grow_places, group_rows)
    gcol_begin = window_starts(gcol_places, group_cols)
    attended_two = window_attend(
        packed_two[..., :feature_width],
        bordered[..., :feature_width],
        bordered[..., feature_width:],
        grow_begin + 3,
        gcol_begin + 3,
        grow_begin - grow_places,
        gcol_begin - gcol_places,
        rel_bias[1],
    )
    final_rows = finish_layer(
        attended_two.reshape(-1, feature_width),
        grouped_rows,
        norm_gains[3],
        proj_weight[1],
        up_weight[1],
        down_weight[1],
    )
    shaped = final_rows.reshape(
        row_count, block_rows, col_count, block_cols, residue_rows, residue_cols, feature_width
    )
    shaped = shaped.transpose(0, 2, 4, 5, 1, 3, 6).reshape(
        row_count * col_count, residue_rows, residue_cols, block_rows * block_cols, feature_width
    )
    arrived = lax.all_to_all(shaped, ("row", "col"), split_axis=0, concat_axis=0, tiled=True)
    restored = arrived.reshape(
        row_count, col_count, residue_rows, residue_cols, block_rows, block_cols, feature_width
    )
    restored = restored.transpose(4, 0, 2, 5, 1, 3, 6).reshape(tile_rows, tile_cols, feature_width)
    return restored


def solution(mesh):
    placed = (P("row", "col", None), P(), P(), P(), P(), P(), P())
    return jax.shard_map(
        body, mesh=mesh, in_specs=placed, out_specs=P("row", "col", None), check_vma=False
    )
```

profile of v0, /device:TPU:1, one launch (start us, length us, event | category | flops | bytes accessed | tf_op | source)
XLA Modules:
  0.0 1566.3 jit_solution(5357733896260968912)
XLA Ops:
  9.7 5.6 collective-permute-start
  595.3 6.5 fusion.285
  604.9 7.2 fusion.284
  613.8 8.1 fusion.283
  624.8 8.5 fusion.282
  636.2 8.3 fusion.281
  647.3 8.6 fusion.280
  658.7 8.2 fusion.279
  802.9 5.1 fusion.142
  809.5 11.7 all-to-all-start
  821.3 14.0 all-to-all-done
  1104.3 9.1 convert_multiply_fusion.6
  1116.4 9.6 convert_multiply_fusion.5
  1128.9 9.2 convert_multiply_fusion.4
  1141.2 9.3 convert_multiply_fusion.3
  1153.4 9.7 convert_multiply_fusion.2
  1166.1 9.4 convert_multiply_fusion.1
  1178.6 9.5 convert_multiply_fusion
  1328.8 4.9 bitcast_convert_fusion.4
  1336.2 4.8 bitcast_convert_fusion.3
  1343.5 4.8 bitcast_convert_fusion.2
  1350.8 4.9 bitcast_convert_fusion.1
  1541.7 5.1 fusion.145
  1547.7 17.5 %all_to_all.10 = bf16[128,2,1,2,512]{4,3,1,2,0:T(2,128)(2,1)S(1)} all-to-all(bf16[128,2,1,2,512]{4,3,1,2,0:T(2,128)(2,1)S(1)} %copy.2293), channel_id=1, replica_groups=mesh['row'=8,'col'=16] {'row','col'}, dimensions={0} | all-to-all | bytes 1048576 | tf_op jit(solution)/shard_map/all_to_all | solution.py:205
  (2040 shorter events, 1359.5 us)
Async XLA Ops:
  7.7 19.4 %copy-start.305 = (f32[2,16,13,13]{1,0,3,2:T(2,128)S(1)}, f32[2,16,13,13]{1,0,3,2:T(2,128)}, u32[]{:S(2)}) copy-start(f32[2,16,13,13]{1,0,3,2:T(2,128)} %param.18) | copy-start | bytes 64900
  8.4 183.6 %collective-permute-start.1 = (bf16[3,16,1024]{2,1,0:T(8,128)(2,1)}, bf16[3,16,1024]{2,1,0:T(8,128)(2,1)}, u32[]{:S(2)}, u32[]{:S(2)}) collective-permute-start(bf16[3,16,1024]{2,1,0:T(8,128)(2,1)} %bitcast.5), channel_id=1, source_target_pairs={{16,0},{32,16},{48,32},{64,48},{80,64},{96,80},{112,96},{17,1},{33... | collective-permute-start | bytes 294920 | tf_op jit(solution)/shard_map/ppermute | solution.py:19
  9.7 182.3 %collective-permute-start = (bf16[3,16,1024]{2,1,0:T(8,128)(2,1)}, bf16[3,16,1024]{2,1,0:T(8,128)(2,1)}, u32[]{:S(2)}, u32[]{:S(2)}) collective-permute-start(bf16[3,16,1024]{2,1,0:T(8,128)(2,1)} %bitcast.3), channel_id=1, source_target_pairs={{0,16},{16,32},{32,48},{48,64},{64,80},{80,96},{96,112},{1,17},{17... | collective-permute-start | bytes 294920 | tf_op jit(solution)/shard_map/ppermute | solution.py:17
  122.1 7.3 copy-start.435
  122.1 7.9 copy-start.438
  122.1 8.5 copy-start.436
  122.1 9.1 copy-start.440
  122.1 9.7 copy-start.439
  122.1 10.2 copy-start.434
  122.1 10.8 copy-start.437
  182.0 8.2 copy-start.432
  182.0 8.2 copy-start.433
  193.9 119.1 %collective-permute-start.3 = (bf16[38,3,1024]{2,1,0:T(4,128)(2,1)}, bf16[38,3,1024]{2,1,0:T(4,128)(2,1)}, u32[]{:S(2)}, u32[]{:S(2)}) collective-permute-start(bf16[38,3,1024]{2,1,0:T(4,128)(2,1)} %get-tuple-element.63), channel_id=1, source_target_pairs={{1,0},{2,1},{3,2},{4,3},{5,4},{6,5},{7,6},{8,7},{9,8},{10,9},{11,1... | collective-permute-start | bytes 700424 | tf_op jit(solution)/shard_map/ppermute | solution.py:19
  196.8 116.2 %collective-permute-start.2 = (bf16[38,3,1024]{2,1,0:T(4,128)(2,1)}, bf16[38,3,1024]{2,1,0:T(4,128)(2,1)}, u32[]{:S(2)}, u32[]{:S(2)}) collective-permute-start(bf16[38,3,1024]{2,1,0:T(4,128)(2,1)} %get-tuple-element.62), channel_id=1, source_target_pairs={{0,1},{1,2},{2,3},{3,4},{4,5},{5,6},{6,7},{7,8},{8,9},{9,10},{10,1... | collective-permute-start | bytes 700424 | tf_op jit(solution)/shard_map/ppermute | solution.py:17
  382.1 7.2 copy-start.442
  564.4 7.5 copy-start.406
  808.0 13.2 copy-start.426
  808.0 13.2 copy-start.427
  808.0 13.2 copy-start.424
  808.1 13.2 copy-start.425
  808.1 13.2 copy-start.422
  808.1 13.2 copy-start.423
  809.5 25.9 %all-to-all-start = ((bf16[128,2,1,2,512]{4,3,1,2,0:T(2,128)(2,1)}), bf16[128,2,1,2,512]{4,3,1,2,0:T(2,128)(2,1)S(1)}, u32[]{:S(2)}, u32[]{:S(2)}) async-start(bf16[128,2,1,2,512]{4,3,1,2,0:T(2,128)(2,1)} %copy.1944), calls=%async_computation | async-start | bytes 1048576 | tf_op jit(solution)/shard_map/all_to_all | solution.py:164
  1284.3 6.4 copy-start.352
  (429 other events, 875.9 us)
where the time goes:
time: 1590 us; the launch traced here: 1570 us
  local copies, waits for them, and re-layouts  1070 us (67%)
  other arithmetic  230 us (14%)
  matrix products  204 us (13%)
  starting transfers between devices  24.8 us (2%)
  blocking collectives  17.5 us (1%)
    gather x98, local copies, waits for them, and re-layouts, window_attend(): jnp.take(key_rows, col_start + across, axis=1)  198 us
    gather x98, local copies, waits for them, and re-layouts, window_attend(): jnp.take(value_rows, col_start + across, axis=1)  197 us
    convert_element_type x147, local copies, waits for them, and re-layouts, window_attend(): running = running + spread * window.astype(jnp.float32)  169 us
    mul x49, local copies, waits for them, and re-layouts, window_attend(): product = query_flat.astype(jnp.float32) * window.astype(jnp.float32)  118 us
    dot_general x112, matrix products, window_attend(): jnp.einsum('iy,cz,nyz->nic', row_hot, col_hots[across], rel_table, precis...  91.5 us
    convert_element_type x14, other arithmetic, window_attend(): running = running + spread * window.astype(jnp.float32)  86.1 us
    mul x7, other arithmetic, window_attend(): product = query_flat.astype(jnp.float32) * window.astype(jnp.float32)  65.8 us
    dot_general x98, matrix products, window_attend(): jnp.einsum('nd,td->nt', head_ones, product, precision=lax.Precision.HIGHEST)  61.3 us
  transfers between devices with their start and end apart: 5, of which 1 were waited for; matrix products, arithmetic and copies ran while one was open for 18% of the time, Pallas kernels for 0%

commit v1 on v0

v1 whole, which is shorter than its diff:
```python
import jax
import jax.numpy as jnp
from jax import lax
from jax.experimental import pallas as pl
from jax.experimental.pallas import tpu as pltpu
from jax.sharding import PartitionSpec as P

D = 512
HEADS = 16
FF = 2048
TR = 32
TC = 16
MAP = 256
LOG2E = 1.4426950408889634
QSCALE = LOG2E * 32.0 ** -0.5
NEG = -1e30
F32 = jnp.float32
BF16 = jnp.bfloat16
VMEM_LIMIT = 56 * 1024 * 1024


def iota(shape, dim):
    return lax.broadcasted_iota(jnp.int32, shape, dim)


def layer_norm(rows, gain):
    x = rows.astype(F32)
    centred = x - jnp.mean(x, axis=-1, keepdims=True)
    variance = jnp.mean(centred * centred, axis=-1, keepdims=True)
    return (centred * lax.rsqrt(variance + 1e-5) * gain).astype(BF16)


def dot(a, b):
    return jnp.dot(a, b, preferred_element_type=F32)


def dot_t(a, b):
    return lax.dot_general(a, b, (((1,), (1,)), ((), ())), preferred_element_type=F32)


def gelu(z):
    inner = 0.7978845608028654 * (z + 0.044715 * (z * z * z))
    return 0.5 * z * (1.0 + jnp.tanh(inner))


def head_masks(count):
    lane = iota((count, 128), 1) // 32
    return [lane == h for h in range(4)]


def attend_unit(q, k, v_ones, bias):
    n = q.shape[0]
    masks = head_masks(n)
    zero = jnp.zeros_like(q)
    stacked = jnp.concatenate([jnp.where(m, q, zero) for m in masks], axis=0)
    scores = dot_t(stacked, k) + bias
    top = jnp.max(scores, axis=-1, keepdims=True)
    probs = jnp.exp2(scores - top).astype(BF16)
    both = dot(probs, v_ones)
    out = both[:n]
    for h in range(1, 4):
        part = both[h * n : (h + 1) * n]
        wide = jnp.concatenate([masks[h], masks[h]], axis=1)
        out = jnp.where(wide, part, out)
    return (out[:, :128] / out[:, 128:]).astype(BF16)


def finish_rows(attended, stream, gain, wp, wu, wd):
    mixed = (dot(attended, wp) + stream.astype(F32)).astype(BF16)
    normed = layer_norm(mixed, gain)
    acc = mixed.astype(F32)
    for c in range(4):
        hidden = gelu(dot(normed, wu[:, c * 512 : (c + 1) * 512])).astype(BF16)
        acc = acc + dot(hidden, wd[c * 512 : (c + 1) * 512, :])
    return acc.astype(BF16)


def query_kernel(x_ref, gains_ref, w_ref, q_ref):
    q_ref[...] = (dot(layer_norm(x_ref[...], gains_ref[0:1, :]), w_ref[0]) * QSCALE).astype(BF16)


def query_call(x, gains, qkv_weight):
    return pl.pallas_call(
        query_kernel,
        grid=(1,),
        in_specs=[
            pl.BlockSpec((512, 512), lambda i: (0, 0)),
            pl.BlockSpec((4, 512), lambda i: (0, 0)),
            pl.BlockSpec((1, 512, 512), lambda i: (0, 0, 0)),
        ],
        out_specs=pl.BlockSpec((512, 512), lambda i: (0, 0)),
        out_shape=jax.ShapeDtypeStruct((512, 512), BF16),
        compiler_params=pltpu.CompilerParams(vmem_limit_bytes=VMEM_LIMIT),
        cost_estimate=pl.CostEstimate(flops=2 * 512 ** 3, transcendentals=0, bytes_accessed=3 * 512 * 1024),
        name="query",
    )(x, gains, qkv_weight)


def spread(table, n):
    base = jnp.broadcast_to(table[n : n + 1, :], (16, table.shape[1]))
    return pltpu.roll(base, 0, 1, stride=1, stride_axis=0)


def local_bias_kernel(place_ref, table_ref, bias_ref):
    first_row = place_ref[0]
    first_col = place_ref[1]
    row = iota((64, 256), 0)
    lane = iota((64, 256), 1)
    qi = row // 16
    qj = row % 16
    kr = lane // 24
    kc = lane - kr * 24
    col_q = first_col + qj
    col_a = jnp.clip(col_q - 3, 0, MAP - 7)
    col_k = first_col + kc - 3
    col_ok = (col_k >= col_a) & (col_k <= col_a + 6)
    oks = []
    for block in (0, 1, 7):
        row_q = first_row + 4 * block + qi
        row_a = jnp.clip(row_q - 3, 0, MAP - 7)
        row_k = first_row + 4 * block - 3 + kr
        oks.append(col_ok & (row_k >= row_a) & (row_k <= row_a + 6))
    rolled = [pltpu.roll(table_ref[...], 512 - (24 * (3 - i) + 3), 1) for i in range(4)]
    for n in range(HEADS):
        parts = [spread(rolled[i], n)[:, :256] for i in range(4)]
        full = jnp.concatenate(parts, axis=0)
        at = (n % 4) * 64
        for c in range(3):
            bias_ref[c, n // 4, at : at + 64, :] = jnp.where(oks[c], full, NEG)


def local_bias_call(place, table):
    return pl.pallas_call(
        local_bias_kernel,
        in_specs=[pl.BlockSpec(memory_space=pltpu.SMEM), pl.BlockSpec(memory_space=pltpu.VMEM)],
        out_specs=pl.BlockSpec(memory_space=pltpu.VMEM),
        out_shape=jax.ShapeDtypeStruct((3, 4, 256, 256), F32),
        compiler_params=pltpu.CompilerParams(vmem_limit_bytes=VMEM_LIMIT),
        cost_estimate=pl.CostEstimate(flops=4_000_000, transcendentals=0, bytes_accessed=3 * 1024 * 1024),
        name="local_bias",
    )(place, table)


def group_bias_kernel(table_ref, bias_ref):
    row = iota((32, 128), 0)
    lane = iota((32, 128), 1)
    qi = row // 16
    qj = row % 16
    kr = lane // 16
    kc = lane % 16
    col_a = jnp.clip(qj - 3, 0, 9)
    col_ok = (kc >= col_a) & (kc <= col_a + 6)
    classes = ((0, 0), (1, 0), (2, 1), (6, 8), (7, 8))
    rolled = [pltpu.roll(table_ref[...], 256 - (step * 16 + 6), 1) for step in range(8)]
    for n in range(HEADS):
        at = (n % 4) * 32
        for c, (block, start) in enumerate(classes):
            parts = [spread(rolled[start - 2 * block - i + 7], n)[:, :128] for i in range(2)]
            row_a = jnp.clip(2 * block + qi - 3, 0, 9)
            row_k = start + kr
            ok = col_ok & (row_k >= row_a) & (row_k <= row_a + 6)
            bias_ref[c, n // 4, at : at + 32, :] = jnp.where(ok, jnp.concatenate(parts, axis=0), NEG)


def group_bias_call(table):
    return pl.pallas_call(
        group_bias_kernel,
        in_specs=[pl.BlockSpec(memory_space=pltpu.VMEM)],
        out_specs=pl.BlockSpec(memory_space=pltpu.VMEM),
        out_shape=jax.ShapeDtypeStruct((5, 4, 128, 128), F32),
        compiler_params=pltpu.CompilerParams(vmem_limit_bytes=VMEM_LIMIT),
        cost_estimate=pl.CostEstimate(flops=4_000_000, transcendentals=0, bytes_accessed=1_300_000),
        name="group_bias",
    )(table)


def local_kernel(
    xpad_ref, x_ref, q_ref, gains_ref, bias_hbm, wqkv_hbm, wp_hbm, wu_hbm, wd_hbm, out_ref,
    bias, wkv, wp, wu, wd, k_s, v_s, a_s, sems,
):
    copies = [
        pltpu.make_async_copy(wqkv_hbm.at[0, :, pl.ds(512, 1024)], wkv, sems.at[0]),
        pltpu.make_async_copy(bias_hbm, bias, sems.at[1]),
        pltpu.make_async_copy(wp_hbm.at[0], wp, sems.at[2]),
        pltpu.make_async_copy(wu_hbm.at[0], wu, sems.at[3]),
        pltpu.make_async_copy(wd_hbm.at[0], wd, sems.at[4]),
    ]
    for c in copies:
        c.start()
    k_s[912:928, :] = jnp.zeros((16, 512), BF16)
    v_s[...] = jnp.ones((928, 1024), BF16)
    for g in range(4):
        v_s[912:928, g * 256 : g * 256 + 128] = jnp.zeros((16, 128), BF16)
    copies[0].wait()
    for r in range(3):
        rows = slice(r * 304, (r + 1) * 304)
        normed = layer_norm(xpad_ref[rows, :], gains_ref[0:1, :])
        k_s[rows, :] = dot(normed, wkv[:, :512]).astype(BF16)
        value = dot(normed, wkv[:, 512:]).astype(BF16)
        for g in range(4):
            v_s[rows, g * 256 : g * 256 + 128] = value[:, g * 128 : (g + 1) * 128]
    copies[1].wait()

    def attend(b, carry):
        at_q = pl.multiple_of(b * 64, 64)
        at_k = pl.multiple_of(b * 96, 32)
        kind = jnp.where(b == 0, 0, jnp.where(b == 7, 2, 1))
        for g in range(4):
            lanes = slice(g * 128, (g + 1) * 128)
            a_s[pl.ds(at_q, 64), lanes] = attend_unit(
                q_ref[pl.ds(at_q, 64), lanes],
                k_s[pl.ds(at_k, 256), lanes],
                v_s[pl.ds(at_k, 256), g * 256 : (g + 1) * 256],
                bias[kind, g],
            )
        return carry

    lax.fori_loop(0, 8, attend, 0)
    for c in copies[2:]:
        c.wait()
    for half in range(2):
        rows = slice(half * 256, (half + 1) * 256)
        done = finish_rows(a_s[rows, :], x_ref[rows, :], gains_ref[1:2, :], wp[...], wu, wd)
        for r in range(8):
            for g in range(2):
                at = (2 * r + g) * 16
                lane = (g * 2 + half) * 512
                out_ref[r * 16 : (r + 1) * 16, lane : lane + 512] = done[at : at + 16, :]


def local_call(xpad, x, q, gains, bias, wqkv, wp, wu, wd):
    vmem = pl.BlockSpec(memory_space=pltpu.VMEM)
    hbm = pl.BlockSpec(memory_space=pl.ANY)
    return pl.pallas_call(
        local_kernel,
        in_specs=[vmem] * 4 + [hbm] * 5,
        out_specs=vmem,
        out_shape=jax.ShapeDtypeStruct((128, 2048), BF16),
        scratch_shapes=[
            pltpu.VMEM((3, 4, 256, 256), F32),
            pltpu.VMEM((512, 1024), BF16),
            pltpu.VMEM((512, 512), BF16),
            pltpu.VMEM((512, 2048), BF16),
            pltpu.VMEM((2048, 512), BF16),
            pltpu.VMEM((928, 512), BF16),
            pltpu.VMEM((928, 1024), BF16),
            pltpu.VMEM((512, 512), BF16),
            pltpu.SemaphoreType.DMA((5,)),
        ],
        compiler_params=pltpu.CompilerParams(vmem_limit_bytes=VMEM_LIMIT),
        cost_estimate=pl.CostEstimate(flops=8_000_000_000, transcendentals=3_000_000, bytes_accessed=12_000_000),
        name="local_layer",
    )(xpad, x, q, gains, bias, wqkv, wp, wu, wd)


def group_kernel(
    in_ref, gains_ref, bias_hbm, wqkv_hbm, wp_hbm, wu_hbm, wd_hbm, out_ref,
    bias, wqkv, wp, wu, wd, x_s, q_s, k_s, v_s, a_s, sems,
):
    copies = [
        pltpu.make_async_copy(wqkv_hbm.at[1], wqkv, sems.at[0]),
        pltpu.make_async_copy(bias_hbm, bias, sems.at[1]),
        pltpu.make_async_copy(wp_hbm.at[1], wp, sems.at[2]),
        pltpu.make_async_copy(wu_hbm.at[1], wu, sems.at[3]),
        pltpu.make_async_copy(wd_hbm.at[1], wd, sems.at[4]),
    ]
    for c in copies:
        c.start()
    for g in range(2):
        for p in range(16):
            r, half = p // 2, p % 2
            lane = (g * 2 + half) * 512
            at = g * 256 + p * 16
            x_s[at : at + 16, :] = in_ref[r * 16 : (r + 1) * 16, lane : lane + 512]
    v_s[...] = jnp.ones((512, 1024), BF16)
    copies[0].wait()
    for g in range(2):
        rows = slice(g * 256, (g + 1) * 256)
        normed = layer_norm(x_s[rows, :], gains_ref[2:3, :])
        q_s[rows, :] = (dot(normed, wqkv[:, :512]) * QSCALE).astype(BF16)
        k_s[rows, :] = dot(normed, wqkv[:, 512:1024]).astype(BF16)
        value = dot(normed, wqkv[:, 1024:]).astype(BF16)
        for h in range(4):
            v_s[rows, h * 256 : h * 256 + 128] = value[:, h * 128 : (h + 1) * 128]
    copies[1].wait()

    def attend(b, carry):
        start = jnp.clip(2 * b - 3, 0, 8)
        kind = jnp.where(b < 2, b, jnp.where(b < 6, 2, b - 3))
        for g in range(2):
            at_q = pl.multiple_of(g * 256 + b * 32, 32)
            at_k = pl.multiple_of(g * 256 + start * 16, 16)
            for h in range(4):
                lanes = slice(h * 128, (h + 1) * 128)
                a_s[pl.ds(at_q, 32), lanes] = attend_unit(
                    q_s[pl.ds(at_q, 32), lanes],
                    k_s[pl.ds(at_k, 128), lanes],
                    v_s[pl.ds(at_k, 128), h * 256 : (h + 1) * 256],
                    bias[kind, h],
                )
        return carry

    lax.fori_loop(0, 8, attend, 0)
    for c in copies[2:]:
        c.wait()
    for g in range(2):
        rows = slice(g * 256, (g + 1) * 256)
        done = finish_rows(a_s[rows, :], x_s[rows, :], gains_ref[3:4, :], wp[...], wu, wd)
        for p in range(16):
            r, half = p // 2, p % 2
            lane = (g * 2 + half) * 512
            out_ref[r * 16 : (r + 1) * 16, lane : lane + 512] = done[p * 16 : (p + 1) * 16, :]


def group_call(rows, gains, bias, wqkv, wp, wu, wd):
    vmem = pl.BlockSpec(memory_space=pltpu.VMEM)
    hbm = pl.BlockSpec(memory_space=pl.ANY)
    return pl.pallas_call(
        group_kernel,
        in_specs=[vmem] * 2 + [hbm] * 5,
        out_specs=vmem,
        out_shape=jax.ShapeDtypeStruct((128, 2048), BF16),
        scratch_shapes=[
            pltpu.VMEM((5, 4, 128, 128), F32),
            pltpu.VMEM((512, 1536), BF16),
            pltpu.VMEM((512, 512), BF16),
            pltpu.VMEM((512, 2048), BF16),
            pltpu.VMEM((2048, 512), BF16),
            pltpu.VMEM((512, 512), BF16),
            pltpu.VMEM((512, 512), BF16),
            pltpu.VMEM((512, 512), BF16),
            pltpu.VMEM((512, 1024), BF16),
            pltpu.VMEM((512, 512), BF16),
            pltpu.SemaphoreType.DMA((5,)),
        ],
        compiler_params=pltpu.CompilerParams(vmem_limit_bytes=VMEM_LIMIT),
        cost_estimate=pl.CostEstimate(flops=7_000_000_000, transcendentals=3_000_000, bytes_accessed=10_000_000),
        name="group_layer",
    )(rows, gains, bias, wqkv, wp, wu, wd)


def place_kernel(in_ref, out_ref):
    for r in range(8):
        for g in range(2):
            for half in range(2):
                lane = (g * 2 + half) * 512
                out_ref[half * 16 + 2 * r + g] = in_ref[r * 16 : (r + 1) * 16, lane : lane + 512]


def place_call(rows):
    return pl.pallas_call(
        place_kernel,
        in_specs=[pl.BlockSpec(memory_space=pltpu.VMEM)],
        out_specs=pl.BlockSpec(memory_space=pltpu.VMEM),
        out_shape=jax.ShapeDtypeStruct((TR, TC, D), BF16),
        compiler_params=pltpu.CompilerParams(vmem_limit_bytes=VMEM_LIMIT),
        name="place",
    )(rows)


def edges(cells, axis, dim):
    count = lax.axis_size(axis)
    ends = count - 1
    size = cells.shape[dim]
    head = lax.slice_in_dim(cells, 0, 3, axis=dim)
    tail = lax.slice_in_dim(cells, size - 3, size, axis=dim)
    before = lax.ppermute(tail, axis, [(i, i + 1) for i in range(ends)])
    after = lax.ppermute(head, axis, [(i + 1, i) for i in range(ends)])
    return before, after


def exchange(rows):
    shaped = rows.reshape(128, 16, 128)
    return lax.all_to_all(shaped, ("row", "col"), 0, 0, tiled=True).reshape(128, 2048)


def body(tokens, norm_gains, qkv_weight, rel_bias, proj_weight, up_weight, down_weight):
    x = tokens.reshape(TR * TC, D)
    top, bottom = edges(tokens, "row", 0)
    tall = jnp.concatenate([top, tokens, bottom], axis=0)
    left, right = edges(tall, "col", 1)
    xpad = jnp.concatenate([left, tall, right, jnp.zeros((TR + 6, 2, D), BF16)], axis=1)
    xpad = xpad.reshape((TR + 6) * 24, D)

    table = rel_bias * LOG2E
    local_table = jnp.pad(table[0], ((0, 0), (0, 0), (0, 11))).reshape(HEADS, 312)
    local_table = jnp.pad(local_table, ((0, 0), (0, 200)))
    group_table = jnp.pad(table[1], ((0, 0), (1, 2), (0, 3))).reshape(HEADS, 256)
    place = jnp.stack([lax.axis_index("row") * TR, lax.axis_index("col") * TC]).astype(jnp.int32)

    q = query_call(x, norm_gains, qkv_weight)
    local_bias = local_bias_call(place, local_table)
    group_bias = group_bias_call(group_table)
    sent = local_call(xpad, x, q, norm_gains, local_bias, qkv_weight, proj_weight, up_weight, down_weight)
    got = exchange(sent)
    back = group_call(got, norm_gains, group_bias, qkv_weight, proj_weight, up_weight, down_weight)
    return place_call(exchange(back))


def solution(mesh):
    placed = (P("row", "col", None), P(), P(), P(), P(), P(), P())
    return jax.shard_map(
        body, mesh=mesh, in_specs=placed, out_specs=P("row", "col", None), check_vma=False
    )
```

time: 1590 us -> 115 us (0.07); the launches traced: 1570 us -> 115 us
  local copies, waits for them, and re-layouts: 1070 us -> 8.8 us
  other arithmetic: 230 us -> 2.22 us
  matrix products: 204 us -> 0 us
  Pallas kernels: 0 us -> 49.5 us
    gather x224 -> x0, local copies, waits for them, and re-layouts: 456 us -> none  [the longest x98 198 us: window_attend(): jnp.take(key_rows, col_start + across, axis=1)]
    convert_element_type x200 -> x0, local copies, waits for them, and re-layouts: 225 us -> none  [the longest x147 169 us: window_attend(): running = running + spread * window.astype(jnp.float32)]
    dot_general x312 -> x0, matrix products: 204 us -> none  [the longest x112 91.5 us: window_attend(): jnp.einsum('iy,cz,nyz->nic', row_hot, col_hots[across], rel_table, precis...]
    mul x49 -> x0, local copies, waits for them, and re-layouts: 118 us -> none  [window_attend(): product = query_flat.astype(jnp.float32) * window.astype(jnp.float32)]
    convert_element_type x19 -> x0, other arithmetic: 90.1 us -> none  [the longest x14 86.1 us: window_attend(): running = running + spread * window.astype(jnp.float32)]
    mul x7 -> x1, other arithmetic: 65.8 us -> 0.02 us  [body(): table = rel_bias * LOG2E]
    another operation x63 -> x0, local copies, waits for them, and re-layouts: 58.7 us -> none  [the longest x49 37.3 us: window_attend(): bias_full = jnp.broadcast_to(bias_term[:, :, :, None], (head_count, query...]
    transpose x50 -> x0, local copies, waits for them, and re-layouts: 51 us -> none  [the longest x49 50.2 us: window_attend(): jnp.einsum('iy,cz,nyz->nic', row_hot, col_hots[across], rel_table, precis...]
  transfers between devices with their start and end apart: 5 -> 5, of which waited for: 1 -> 2; matrix products, arithmetic and copies ran while one was open for 18% -> 3% of each run, Pallas kernels for 0% -> 7%
where the time goes in v1:
time: 115 us
  Pallas kernels  49.5 us (43%)
  starting transfers between devices  24.1 us (21%)
  blocking collectives  17.5 us (15%)
  waiting for transfers between devices  12.5 us (11%)
  local copies, waits for them, and re-layouts  8.8 us (8%)
  other arithmetic  2.22 us (2%)
    pallas_call x1, Pallas kernels, group_call(): pl.pallas_call(group_kernel, in_specs=[vmem] * 2 + [hbm] * 5, out_specs=v...  25.1 us
    all_to_all x1, blocking collectives, exchange(): lax.all_to_all(shaped, ('row', 'col'), 0, 0, tiled=True).reshape(128, 2048)  17.5 us
    pallas_call x1, Pallas kernels, local_call(): pl.pallas_call(local_kernel, in_specs=[vmem] * 4 + [hbm] * 5, out_specs=v...  14.4 us
    all_to_all x1, starting transfers between devices, exchange(): lax.all_to_all(shaped, ('row', 'col'), 0, 0, tiled=True).reshape(128, 2048)  11.6 us
    all_to_all x1, waiting for transfers between devices, exchange(): lax.all_to_all(shaped, ('row', 'col'), 0, 0, tiled=True).reshape(128, 2048)  10.9 us
    ppermute x2, starting transfers between devices, edges(): before = lax.ppermute(tail, axis, [(i, i + 1) for i in range(ends)])  9.29 us
    unnamed x11, local copies, waits for them, and re-layouts  6.23 us
    ppermute x2, starting transfers between devices, edges(): after = lax.ppermute(head, axis, [(i + 1, i) for i in range(ends)])  3.21 us
  transfers between devices with their start and end apart: 5, of which 2 were waited for; matrix products, arithmetic and copies ran while one was open for 3% of the time, Pallas kernels for 7%

profile of v1, /device:TPU:1, one launch (start us, length us, event | category | flops | bytes accessed | tf_op | source)
XLA Modules:
  0.0 114.8 jit_solution(15487955922611371210)
XLA Ops:
  0.0 0.9 fusion.1
  0.9 4.4 %collective-permute-start = (bf16[3,16,512]{2,1,0:T(8,128)(2,1)S(1)}, bf16[3,16,512]{2,1,0:T(8,128)(2,1)S(1)}, u32[]{:S(2)}, u32[]{:S(2)}) collective-permute-start(bf16[3,16,512]{2,1,0:T(8,128)(2,1)S(1)} %get-tuple-element.8), channel_id=1, source_target_pairs={{0,16},{16,32},{32,48},{48,64},{64,80},{80,96},{96,112},{1,17},{17... | collective-permute-start | bytes 147464 | tf_op jit(solution)/shard_map/ppermute | solution.py:367
  5.3 1.3 %collective-permute-start.1 = (bf16[3,16,512]{2,1,0:T(8,128)(2,1)S(1)}, bf16[3,16,512]{2,1,0:T(8,128)(2,1)S(1)}, u32[]{:S(2)}, u32[]{:S(2)}) collective-permute-start(bf16[3,16,512]{2,1,0:T(8,128)(2,1)S(1)} %get-tuple-element.7), channel_id=1, source_target_pairs={{16,0},{32,16},{48,32},{64,48},{80,64},{96,80},{112,96},{17,1},{33... | collective-permute-start | bytes 147464 | tf_op jit(solution)/shard_map/ppermute | solution.py:368
  6.6 1.1 copy.10
  7.9 0.6 pad.13.table_ref
  8.7 1.6 %collective-permute-done.1 = bf16[3,16,512]{2,1,0:T(8,128)(2,1)S(1)} collective-permute-done((bf16[3,16,512]{2,1,0:T(8,128)(2,1)S(1)}, bf16[3,16,512]{2,1,0:T(8,128)(2,1)S(1)}, u32[]{:S(2)}, u32[]{:S(2)}) %collective-permute-start.1) | collective-permute-done | bytes 49184 | tf_op jit(solution)/shard_map/ppermute | solution.py:368
  10.4 4.9 %collective-permute-start.2 = (bf16[38,3,512]{2,1,0:T(4,128)(2,1)S(1)}, bf16[38,3,512]{2,1,0:T(4,128)(2,1)S(1)}, u32[]{:S(2)}, u32[]{:S(2)}) collective-permute-start(bf16[38,3,512]{2,1,0:T(4,128)(2,1)S(1)} %get-tuple-element.5), channel_id=1, source_target_pairs={{0,1},{1,2},{2,3},{3,4},{4,5},{5,6},{6,7},{7,8},{8,9},{9,10},{10,1... | collective-permute-start | bytes 350216 | tf_op jit(solution)/shard_map/ppermute | solution.py:367
  15.3 1.9 %collective-permute-start.3 = (bf16[38,3,512]{2,1,0:T(4,128)(2,1)S(1)}, bf16[38,3,512]{2,1,0:T(4,128)(2,1)S(1)}, u32[]{:S(2)}, u32[]{:S(2)}) collective-permute-start(bf16[38,3,512]{2,1,0:T(4,128)(2,1)S(1)} %get-tuple-element.6), channel_id=1, source_target_pairs={{1,0},{2,1},{3,2},{4,3},{5,4},{6,5},{7,6},{8,7},{9,8},{10,9},{11,1... | collective-permute-start | bytes 350216 | tf_op jit(solution)/shard_map/ppermute | solution.py:368
  17.3 0.6 pad_add_fusion.place_ref
  17.9 3.0 %local_bias.1.bias_hbm = f32[3,4,256,256]{3,2,1,0:T(8,128)} custom-call(s32[2]{0:T(128)} %pad_add_fusion.place_ref, f32[16,512]{1,0:T(8,128)} %pad.13.table_ref), custom_call_target="tpu_custom_call" | custom-call | flops 4000000 | bytes 3145728 | tf_op jit(solution)/shard_map/local_bias/pallas_call | solution.py:133
  20.9 2.7 %query.1.q_ref = bf16[512,512]{1,0:T(8,128)(2,1)} custom-call(bf16[512,512]{1,0:T(8,128)(2,1)} %bitcast.20, f32[4,512]{1,0:T(4,128)} %gains_ref.5, bf16[2,512,1536]{2,1,0:T(8,128)(2,1)} %wqkv_hbm.3), custom_call_target="tpu_custom_call" | custom-call | flops 268435456 | bytes 1572864 | tf_op jit(solution)/shard_map/query/pallas_call | solution.py:83
  23.6 1.6 %maximum_maximum_fusion = bf16[38,24,512]{2,1,0:T(8,128)(2,1)} fusion(bf16[38,3,512]{2,1,0:T(4,128)(2,1)S(1)} %collective-permute-done.3, bf16[38,16,512]{2,1,0:T(8,128)(2,1)S(1)} %constant_dynamic-update-slice_fusion, bf16[38,3,512]{2,1,0:T(4,128)(2,1)S(1)} %collective-permute-done.2, bf16[24]{0:T(256)(128)(2,1)S(1)} %pad.20.clone), kind=kLoop, calls=%fused_computation | loop fusion | flops 3735552 | bytes 1790000 | tf_op jit(solution)/shard_map/concatenate | solution.py:382
  25.2 14.4 %local_layer.1 = bf16[128,2048]{1,0:T(8,128)(2,1)} custom-call(bf16[912,512]{1,0:T(8,128)(2,1)} %bitcast.26, bf16[512,512]{1,0:T(8,128)(2,1)} %bitcast.21, bf16[512,512]{1,0:T(8,128)(2,1)} %query.1.q_ref, f32[4,512]{1,0:T(4,128)} %gains_ref.5, f32[3,4,256,256]{3,2,1,0:T(8,128)} %local_bias.1.bias_hbm, bf16[2,512,1536]{2,1,0:T(8,128)(2,1)} %wqkv_hbm.3, ...), custom_call_target="tpu_custom_call" | custom-call | flops 8000000000 | bytes 12000000 | tf_op jit(solution)/shard_map/local_layer/pallas_call | solution.py:234
  39.6 1.9 %copy.15 = bf16[16,8,16,128]{3,2,1,0:T(8,128)(2,1)} copy(bf16[16,8,16,128]{3,1,2,0:T(8,128)(2,1)} %bitcast.27) | data formatting | bytes 1048576
  41.5 11.6 %all-to-all-start = ((bf16[128,16,128]{2,1,0:T(8,128)(2,1)}), bf16[128,16,128]{2,1,0:T(8,128)(2,1)S(1)}, u32[]{:S(2)}, u32[]{:S(2)}) async-start(bf16[128,16,128]{2,1,0:T(8,128)(2,1)} %bitcast.7), calls=%async_computation | async-start | bytes 1048576 | tf_op jit(solution)/shard_map/all_to_all | solution.py:374
  53.2 0.7 reshape.29.table_ref
  53.9 2.5 %group_bias.1.bias_hbm = f32[5,4,128,128]{3,2,1,0:T(8,128)} custom-call(f32[16,256]{1,0:T(8,128)} %reshape.29.table_ref), custom_call_target="tpu_custom_call" | custom-call | flops 4000000 | bytes 1300000 | tf_op jit(solution)/shard_map/group_bias/pallas_call | solution.py:166
  56.4 10.9 %all-to-all-done = bf16[128,16,128]{2,1,0:T(8,128)(2,1)S(1)} async-done(((bf16[128,16,128]{2,1,0:T(8,128)(2,1)}), bf16[128,16,128]{2,1,0:T(8,128)(2,1)S(1)}, u32[]{:S(2)}, u32[]{:S(2)}) %all-to-all-start) | async-done | bytes 524320 | tf_op jit(solution)/shard_map/all_to_all | solution.py:374
  67.3 0.9 copy.22
  68.2 25.1 %group_layer.1 = bf16[128,2048]{1,0:T(8,128)(2,1)} custom-call(bf16[128,2048]{1,0:T(8,128)(2,1)} %bitcast.28, f32[4,512]{1,0:T(4,128)} %gains_ref.5, f32[5,4,128,128]{3,2,1,0:T(8,128)} %group_bias.1.bias_hbm, bf16[2,512,1536]{2,1,0:T(8,128)(2,1)} %wqkv_hbm.3, bf16[2,512,512]{2,1,0:T(8,128)(2,1)} %wp_hbm.3, bf16[2,512,2048]{2,1,0:T(8,128)(2,1)} %wu_hbm.3, ...), custom_call_target="tpu_custom_call" | custom-call | flops 7000000000 | bytes 10000000 | tf_op jit(solution)/shard_map/group_layer/pallas_call | solution.py:318
  93.3 1.1 copy.17
  94.5 17.5 %all_to_all.10 = bf16[128,16,128]{2,1,0:T(8,128)(2,1)S(1)} all-to-all(bf16[128,16,128]{2,1,0:T(8,128)(2,1)S(1)} %bitcast.23), channel_id=1, replica_groups=mesh['row'=8,'col'=16] {'row','col'}, dimensions={0} | all-to-all | bytes 1048576 | tf_op jit(solution)/shard_map/all_to_all | solution.py:374
  112.0 0.9 copy.21
  112.9 1.9 %place.1 = bf16[32,16,512]{2,1,0:T(8,128)(2,1)} custom-call(bf16[128,2048]{1,0:T(8,128)(2,1)} %bitcast.25), custom_call_target="tpu_custom_call" | custom-call | tf_op jit(solution)/shard_map/place/pallas_call | solution.py:351
  (18 shorter events, 0.5 us)
Async XLA Ops:
  0.0 8.6 %copy-start = (bf16[32,16,512]{2,1,0:T(8,128)(2,1)S(1)}, bf16[32,16,512]{2,1,0:T(8,128)(2,1)}, u32[]{:S(2)}) copy-start(bf16[32,16,512]{2,1,0:T(8,128)(2,1)} %param.7) | copy-start | bytes 1572868
  0.9 7.7 %collective-permute-start = (bf16[3,16,512]{2,1,0:T(8,128)(2,1)S(1)}, bf16[3,16,512]{2,1,0:T(8,128)(2,1)S(1)}, u32[]{:S(2)}, u32[]{:S(2)}) collective-permute-start(bf16[3,16,512]{2,1,0:T(8,128)(2,1)S(1)} %get-tuple-element.8), channel_id=1, source_target_pairs={{0,16},{16,32},{32,48},{48,64},{64,80},{80,96},{96,112},{1,17},{17... | collective-permute-start | bytes 147464 | tf_op jit(solution)/shard_map/ppermute | solution.py:367
  5.3 5.0 %collective-permute-start.1 = (bf16[3,16,512]{2,1,0:T(8,128)(2,1)S(1)}, bf16[3,16,512]{2,1,0:T(8,128)(2,1)S(1)}, u32[]{:S(2)}, u32[]{:S(2)}) collective-permute-start(bf16[3,16,512]{2,1,0:T(8,128)(2,1)S(1)} %get-tuple-element.7), channel_id=1, source_target_pairs={{16,0},{32,16},{48,32},{64,48},{80,64},{96,80},{112,96},{17,1},{33... | collective-permute-start | bytes 147464 | tf_op jit(solution)/shard_map/ppermute | solution.py:368
  10.4 13.2 %collective-permute-start.2 = (bf16[38,3,512]{2,1,0:T(4,128)(2,1)S(1)}, bf16[38,3,512]{2,1,0:T(4,128)(2,1)S(1)}, u32[]{:S(2)}, u32[]{:S(2)}) collective-permute-start(bf16[38,3,512]{2,1,0:T(4,128)(2,1)S(1)} %get-tuple-element.5), channel_id=1, source_target_pairs={{0,1},{1,2},{2,3},{3,4},{4,5},{5,6},{6,7},{7,8},{8,9},{9,10},{10,1... | collective-permute-start | bytes 350216 | tf_op jit(solution)/shard_map/ppermute | solution.py:367
  15.3 8.3 %collective-permute-start.3 = (bf16[38,3,512]{2,1,0:T(4,128)(2,1)S(1)}, bf16[38,3,512]{2,1,0:T(4,128)(2,1)S(1)}, u32[]{:S(2)}, u32[]{:S(2)}) collective-permute-start(bf16[38,3,512]{2,1,0:T(4,128)(2,1)S(1)} %get-tuple-element.6), channel_id=1, source_target_pairs={{1,0},{2,1},{3,2},{4,3},{5,4},{6,5},{7,6},{8,7},{9,8},{10,9},{11,1... | collective-permute-start | bytes 350216 | tf_op jit(solution)/shard_map/ppermute | solution.py:368
  41.5 25.8 %all-to-all-start = ((bf16[128,16,128]{2,1,0:T(8,128)(2,1)}), bf16[128,16,128]{2,1,0:T(8,128)(2,1)S(1)}, u32[]{:S(2)}, u32[]{:S(2)}) async-start(bf16[128,16,128]{2,1,0:T(8,128)(2,1)} %bitcast.7), calls=%async_computation | async-start | bytes 1048576 | tf_op jit(solution)/shard_map/all_to_all | solution.py:374

commit v2 on v1

--- a/solution.py
+++ b/solution.py
@@ -48,21 +48,26 @@
     return [lane == h for h in range(4)]
 
 
-def attend_unit(q, k, v_ones, bias):
-    n = q.shape[0]
+def attend_units(units):
+    n = units[0][0].shape[0]
     masks = head_masks(n)
-    zero = jnp.zeros_like(q)
-    stacked = jnp.concatenate([jnp.where(m, q, zero) for m in masks], axis=0)
-    scores = dot_t(stacked, k) + bias
-    top = jnp.max(scores, axis=-1, keepdims=True)
-    probs = jnp.exp2(scores - top).astype(BF16)
-    both = dot(probs, v_ones)
-    out = both[:n]
-    for h in range(1, 4):
-        part = both[h * n : (h + 1) * n]
-        wide = jnp.concatenate([masks[h], masks[h]], axis=1)
-        out = jnp.where(wide, part, out)
-    return (out[:, :128] / out[:, 128:]).astype(BF16)
+    zero = jnp.zeros((n, 128), BF16)
+    scores = []
+    for q, k, _, bias in units:
+        stacked = jnp.concatenate([jnp.where(m, q, zero) for m in masks], axis=0)
+        scores.append(dot_t(stacked, k) + bias)
+    tops = [jnp.max(s, axis=-1, keepdims=True) for s in scores]
+    probs = [jnp.exp2(s - t).astype(BF16) for s, t in zip(scores, tops)]
+    outs = []
+    for unit, p in zip(units, probs):
+        both = dot(p, unit[2])
+        top, low = both[:n, :128], both[:n, 128:]
+        for h in range(1, 4):
+            part = both[h * n : (h + 1) * n]
+            top = jnp.where(masks[h], part[:, :128], top)
+            low = jnp.where(masks[h], part[:, 128:], low)
+        outs.append((top / low).astype(BF16))
+    return outs
 
 
 def finish_rows(attended, stream, gain, wp, wu, wd):
@@ -202,20 +207,26 @@
     copies[1].wait()
 
     def attend(b, carry):
-        at_q = pl.multiple_of(b * 64, 64)
-        at_k = pl.multiple_of(b * 96, 32)
-        kind = jnp.where(b == 0, 0, jnp.where(b == 7, 2, 1))
+        at_q = b * 64
+        at_k = b * 96
+        kind = 0 if b == 0 else 2 if b == 7 else 1
+        outs = attend_units(
+            [
+                (
+                    q_ref[pl.ds(at_q, 64), g * 128 : (g + 1) * 128],
+                    k_s[pl.ds(at_k, 256), g * 128 : (g + 1) * 128],
+                    v_s[pl.ds(at_k, 256), g * 256 : (g + 1) * 256],
+                    bias[kind, g],
+                )
+                for g in range(4)
+            ]
+        )
         for g in range(4):
-            lanes = slice(g * 128, (g + 1) * 128)
-            a_s[pl.ds(at_q, 64), lanes] = attend_unit(
-                q_ref[pl.ds(at_q, 64), lanes],
-                k_s[pl.ds(at_k, 256), lanes],
-                v_s[pl.ds(at_k, 256), g * 256 : (g + 1) * 256],
-                bias[kind, g],
-            )
+            a_s[pl.ds(at_q, 64), g * 128 : (g + 1) * 128] = outs[g]
         return carry
 
-    lax.fori_loop(0, 8, attend, 0)
+    for b in range(8):
+        attend(b, 0)
     for c in copies[2:]:
         c.wait()
     for half in range(2):
@@ -285,22 +296,30 @@
     copies[1].wait()
 
     def attend(b, carry):
-        start = jnp.clip(2 * b - 3, 0, 8)
-        kind = jnp.where(b < 2, b, jnp.where(b < 6, 2, b - 3))
+        start = min(max(2 * b - 3, 0), 8)
+        kind = b if b < 2 else 2 if b < 6 else b - 3
+        units = []
         for g in range(2):
-            at_q = pl.multiple_of(g * 256 + b * 32, 32)
-            at_k = pl.multiple_of(g * 256 + start * 16, 16)
+            at_q = g * 256 + b * 32
+            at_k = g * 256 + start * 16
             for h in range(4):
-                lanes = slice(h * 128, (h + 1) * 128)
-                a_s[pl.ds(at_q, 32), lanes] = attend_unit(
-                    q_s[pl.ds(at_q, 32), lanes],
-                    k_s[pl.ds(at_k, 128), lanes],
-                    v_s[pl.ds(at_k, 128), h * 256 : (h + 1) * 256],
-                    bias[kind, h],
+                units.append(
+                    (
+                        q_s[pl.ds(at_q, 32), h * 128 : (h + 1) * 128],
+                        k_s[pl.ds(at_k, 128), h * 128 : (h + 1) * 128],
+                        v_s[pl.ds(at_k, 128), h * 256 : (h + 1) * 256],
+                        bias[kind, h],
+                    )
                 )
+        outs = attend_units(units)
+        for g in range(2):
+            at_q = g * 256 + b * 32
+            for h in range(4):
+                a_s[pl.ds(at_q, 32), h * 128 : (h + 1) * 128] = outs[g * 4 + h]
         return carry
 
-    lax.fori_loop(0, 8, attend, 0)
+    for b in range(8):
+        attend(b, 0)
     for c in copies[2:]:
         c.wait()
     for g in range(2):

time: 115 us -> 101 us (0.88)
  Pallas kernels: 49.5 us -> 34.6 us
    pallas_call x1, Pallas kernels: 25.1 us -> 12.1 us  [group_call(): pl.pallas_call(group_kernel, in_specs=[vmem] * 2 + [hbm] * 5, out_specs=v...]
    pallas_call x1, Pallas kernels: 14.4 us -> 12.4 us  [local_call(): pl.pallas_call(local_kernel, in_specs=[vmem] * 4 + [hbm] * 5, out_specs=v...]
  transfers between devices with their start and end apart: 5 -> 5, of which waited for: 2 -> 2; matrix products, arithmetic and copies ran while one was open for 3% -> 3% of each run, Pallas kernels for 7% -> 8%
where the time goes in v2:
time: 101 us; the launch traced here: 99.9 us
  Pallas kernels  34.6 us (34%)
  starting transfers between devices  24.1 us (24%)
  blocking collectives  17.6 us (17%)
  waiting for transfers between devices  12.5 us (12%)
  local copies, waits for them, and re-layouts  8.8 us (9%)
  other arithmetic  2.22 us (2%)
    all_to_all x1, blocking collectives, exchange(): lax.all_to_all(shaped, ('row', 'col'), 0, 0, tiled=True).reshape(128, 2048)  17.6 us
    pallas_call x1, Pallas kernels, local_call(): pl.pallas_call(local_kernel, in_specs=[vmem] * 4 + [hbm] * 5, out_specs=v...  12.4 us
    pallas_call x1, Pallas kernels, group_call(): pl.pallas_call(group_kernel, in_specs=[vmem] * 2 + [hbm] * 5, out_specs=v...  12.1 us
    all_to_all x1, starting transfers between devices, exchange(): lax.all_to_all(shaped, ('row', 'col'), 0, 0, tiled=True).reshape(128, 2048)  11.6 us
    all_to_all x1, waiting for transfers between devices, exchange(): lax.all_to_all(shaped, ('row', 'col'), 0, 0, tiled=True).reshape(128, 2048)  10.9 us
    ppermute x2, starting transfers between devices, edges(): before = lax.ppermute(tail, axis, [(i, i + 1) for i in range(ends)])  9.29 us
    unnamed x11, local copies, waits for them, and re-layouts  6.23 us
    ppermute x2, starting transfers between devices, edges(): after = lax.ppermute(head, axis, [(i + 1, i) for i in range(ends)])  3.21 us
  transfers between devices with their start and end apart: 5, of which 2 were waited for; matrix products, arithmetic and copies ran while one was open for 3% of the time, Pallas kernels for 8%

profile of v2, /device:TPU:1, one launch (start us, length us, event | category | flops | bytes accessed | tf_op | source)
XLA Modules:
  0.0 99.9 jit_solution(12966607871120737919)
XLA Ops:
  0.0 0.9 fusion.1
  0.9 4.4 %collective-permute-start = (bf16[3,16,512]{2,1,0:T(8,128)(2,1)S(1)}, bf16[3,16,512]{2,1,0:T(8,128)(2,1)S(1)}, u32[]{:S(2)}, u32[]{:S(2)}) collective-permute-start(bf16[3,16,512]{2,1,0:T(8,128)(2,1)S(1)} %get-tuple-element.8), channel_id=1, source_target_pairs={{0,16},{16,32},{32,48},{48,64},{64,80},{80,96},{96,112},{1,17},{17... | collective-permute-start | bytes 147464 | tf_op jit(solution)/shard_map/ppermute | solution.py:386
  5.3 1.3 %collective-permute-start.1 = (bf16[3,16,512]{2,1,0:T(8,128)(2,1)S(1)}, bf16[3,16,512]{2,1,0:T(8,128)(2,1)S(1)}, u32[]{:S(2)}, u32[]{:S(2)}) collective-permute-start(bf16[3,16,512]{2,1,0:T(8,128)(2,1)S(1)} %get-tuple-element.7), channel_id=1, source_target_pairs={{16,0},{32,16},{48,32},{64,48},{80,64},{96,80},{112,96},{17,1},{33... | collective-permute-start | bytes 147464 | tf_op jit(solution)/shard_map/ppermute | solution.py:387
  6.6 1.1 %copy.10 = f32[2,16,13,13]{3,1,2,0:T(8,128)S(1)} copy(f32[2,16,13,13]{1,0,3,2:T(2,128)} %param.10) | data formatting | bytes 43264 | tf_op args[3]
  7.9 0.6 pad.13.table_ref
  8.7 1.6 %collective-permute-done.1 = bf16[3,16,512]{2,1,0:T(8,128)(2,1)S(1)} collective-permute-done((bf16[3,16,512]{2,1,0:T(8,128)(2,1)S(1)}, bf16[3,16,512]{2,1,0:T(8,128)(2,1)S(1)}, u32[]{:S(2)}, u32[]{:S(2)}) %collective-permute-start.1) | collective-permute-done | bytes 49184 | tf_op jit(solution)/shard_map/ppermute | solution.py:387
  10.4 4.9 %collective-permute-start.2 = (bf16[38,3,512]{2,1,0:T(4,128)(2,1)S(1)}, bf16[38,3,512]{2,1,0:T(4,128)(2,1)S(1)}, u32[]{:S(2)}, u32[]{:S(2)}) collective-permute-start(bf16[38,3,512]{2,1,0:T(4,128)(2,1)S(1)} %get-tuple-element.5), channel_id=1, source_target_pairs={{0,1},{1,2},{2,3},{3,4},{4,5},{5,6},{6,7},{7,8},{8,9},{9,10},{10,1... | collective-permute-start | bytes 350216 | tf_op jit(solution)/shard_map/ppermute | solution.py:386
  15.3 1.9 %collective-permute-start.3 = (bf16[38,3,512]{2,1,0:T(4,128)(2,1)S(1)}, bf16[38,3,512]{2,1,0:T(4,128)(2,1)S(1)}, u32[]{:S(2)}, u32[]{:S(2)}) collective-permute-start(bf16[38,3,512]{2,1,0:T(4,128)(2,1)S(1)} %get-tuple-element.6), channel_id=1, source_target_pairs={{1,0},{2,1},{3,2},{4,3},{5,4},{6,5},{7,6},{8,7},{9,8},{10,9},{11,1... | collective-permute-start | bytes 350216 | tf_op jit(solution)/shard_map/ppermute | solution.py:387
  17.3 0.6 pad_add_fusion.place_ref
  17.9 3.0 %local_bias.1.bias_hbm = f32[3,4,256,256]{3,2,1,0:T(8,128)} custom-call(s32[2]{0:T(128)} %pad_add_fusion.place_ref, f32[16,512]{1,0:T(8,128)} %pad.13.table_ref), custom_call_target="tpu_custom_call" | custom-call | flops 4000000 | bytes 3145728 | tf_op jit(solution)/shard_map/local_bias/pallas_call | solution.py:138
  20.9 2.7 %query.1.q_ref = bf16[512,512]{1,0:T(8,128)(2,1)} custom-call(bf16[512,512]{1,0:T(8,128)(2,1)} %bitcast.20, f32[4,512]{1,0:T(4,128)} %gains_ref.5, bf16[2,512,1536]{2,1,0:T(8,128)(2,1)} %wqkv_hbm.3), custom_call_target="tpu_custom_call" | custom-call | flops 268435456 | bytes 1572864 | tf_op jit(solution)/shard_map/query/pallas_call | solution.py:88
  23.6 1.6 %maximum_maximum_fusion = bf16[38,24,512]{2,1,0:T(8,128)(2,1)} fusion(bf16[38,3,512]{2,1,0:T(4,128)(2,1)S(1)} %collective-permute-done.3, bf16[38,16,512]{2,1,0:T(8,128)(2,1)S(1)} %constant_dynamic-update-slice_fusion, bf16[38,3,512]{2,1,0:T(4,128)(2,1)S(1)} %collective-permute-done.2, bf16[24]{0:T(256)(128)(2,1)S(1)} %pad.20.clone), kind=kLoop, calls=%fused_computation | loop fusion | flops 3735552 | bytes 1790000 | tf_op jit(solution)/shard_map/concatenate | solution.py:401
  25.2 12.4 %local_layer.1 = bf16[128,2048]{1,0:T(8,128)(2,1)} custom-call(bf16[912,512]{1,0:T(8,128)(2,1)} %bitcast.26, bf16[512,512]{1,0:T(8,128)(2,1)} %bitcast.21, bf16[512,512]{1,0:T(8,128)(2,1)} %query.1.q_ref, f32[4,512]{1,0:T(4,128)} %gains_ref.5, f32[3,4,256,256]{3,2,1,0:T(8,128)} %local_bias.1.bias_hbm, bf16[2,512,1536]{2,1,0:T(8,128)(2,1)} %wqkv_hbm.3, ...), custom_call_target="tpu_custom_call" | custom-call | flops 8000000000 | bytes 12000000 | tf_op jit(solution)/shard_map/local_layer/pallas_call | solution.py:245
  37.6 1.9 %copy.15 = bf16[16,8,16,128]{3,2,1,0:T(8,128)(2,1)} copy(bf16[16,8,16,128]{3,1,2,0:T(8,128)(2,1)} %bitcast.27) | data formatting | bytes 1048576
  39.5 11.6 %all-to-all-start = ((bf16[128,16,128]{2,1,0:T(8,128)(2,1)}), bf16[128,16,128]{2,1,0:T(8,128)(2,1)S(1)}, u32[]{:S(2)}, u32[]{:S(2)}) async-start(bf16[128,16,128]{2,1,0:T(8,128)(2,1)} %bitcast.7), calls=%async_computation | async-start | bytes 1048576 | tf_op jit(solution)/shard_map/all_to_all | solution.py:393
  51.2 0.7 reshape.29.table_ref
  51.9 2.5 %group_bias.1.bias_hbm = f32[5,4,128,128]{3,2,1,0:T(8,128)} custom-call(f32[16,256]{1,0:T(8,128)} %reshape.29.table_ref), custom_call_target="tpu_custom_call" | custom-call | flops 4000000 | bytes 1300000 | tf_op jit(solution)/shard_map/group_bias/pallas_call | solution.py:171
  54.5 10.9 %all-to-all-done = bf16[128,16,128]{2,1,0:T(8,128)(2,1)S(1)} async-done(((bf16[128,16,128]{2,1,0:T(8,128)(2,1)}), bf16[128,16,128]{2,1,0:T(8,128)(2,1)S(1)}, u32[]{:S(2)}, u32[]{:S(2)}) %all-to-all-start) | async-done | bytes 524320 | tf_op jit(solution)/shard_map/all_to_all | solution.py:393
  65.3 0.9 copy.22
  66.2 12.1 %group_layer.1 = bf16[128,2048]{1,0:T(8,128)(2,1)} custom-call(bf16[128,2048]{1,0:T(8,128)(2,1)} %bitcast.28, f32[4,512]{1,0:T(4,128)} %gains_ref.5, f32[5,4,128,128]{3,2,1,0:T(8,128)} %group_bias.1.bias_hbm, bf16[2,512,1536]{2,1,0:T(8,128)(2,1)} %wqkv_hbm.3, bf16[2,512,512]{2,1,0:T(8,128)(2,1)} %wp_hbm.3, bf16[2,512,2048]{2,1,0:T(8,128)(2,1)} %wu_hbm.3, ...), custom_call_target="tpu_custom_call" | custom-call | flops 7000000000 | bytes 10000000 | tf_op jit(solution)/shard_map/group_layer/pallas_call | solution.py:337
  78.4 1.1 %copy.17 = bf16[16,8,16,128]{3,2,1,0:T(8,128)(2,1)S(1)} copy(bf16[16,8,16,128]{3,1,2,0:T(8,128)(2,1)} %bitcast.29) | data formatting | bytes 1048576
  79.5 17.6 %all_to_all.10 = bf16[128,16,128]{2,1,0:T(8,128)(2,1)S(1)} all-to-all(bf16[128,16,128]{2,1,0:T(8,128)(2,1)S(1)} %bitcast.23), channel_id=1, replica_groups=mesh['row'=8,'col'=16] {'row','col'}, dimensions={0} | all-to-all | bytes 1048576 | tf_op jit(solution)/shard_map/all_to_all | solution.py:393
  97.1 0.9 copy.21
  98.0 1.9 %place.1 = bf16[32,16,512]{2,1,0:T(8,128)(2,1)} custom-call(bf16[128,2048]{1,0:T(8,128)(2,1)} %bitcast.25), custom_call_target="tpu_custom_call" | custom-call | tf_op jit(solution)/shard_map/place/pallas_call | solution.py:370
  (18 shorter events, 0.5 us)
Async XLA Ops:
  0.0 8.6 %copy-start = (bf16[32,16,512]{2,1,0:T(8,128)(2,1)S(1)}, bf16[32,16,512]{2,1,0:T(8,128)(2,1)}, u32[]{:S(2)}) copy-start(bf16[32,16,512]{2,1,0:T(8,128)(2,1)} %param.7) | copy-start | bytes 1572868
  0.9 7.7 %collective-permute-start = (bf16[3,16,512]{2,1,0:T(8,128)(2,1)S(1)}, bf16[3,16,512]{2,1,0:T(8,128)(2,1)S(1)}, u32[]{:S(2)}, u32[]{:S(2)}) collective-permute-start(bf16[3,16,512]{2,1,0:T(8,128)(2,1)S(1)} %get-tuple-element.8), channel_id=1, source_target_pairs={{0,16},{16,32},{32,48},{48,64},{64,80},{80,96},{96,112},{1,17},{17... | collective-permute-start | bytes 147464 | tf_op jit(solution)/shard_map/ppermute | solution.py:386
  5.3 5.0 %collective-permute-start.1 = (bf16[3,16,512]{2,1,0:T(8,128)(2,1)S(1)}, bf16[3,16,512]{2,1,0:T(8,128)(2,1)S(1)}, u32[]{:S(2)}, u32[]{:S(2)}) collective-permute-start(bf16[3,16,512]{2,1,0:T(8,128)(2,1)S(1)} %get-tuple-element.7), channel_id=1, source_target_pairs={{16,0},{32,16},{48,32},{64,48},{80,64},{96,80},{112,96},{17,1},{33... | collective-permute-start | bytes 147464 | tf_op jit(solution)/shard_map/ppermute | solution.py:387
  10.4 13.2 %collective-permute-start.2 = (bf16[38,3,512]{2,1,0:T(4,128)(2,1)S(1)}, bf16[38,3,512]{2,1,0:T(4,128)(2,1)S(1)}, u32[]{:S(2)}, u32[]{:S(2)}) collective-permute-start(bf16[38,3,512]{2,1,0:T(4,128)(2,1)S(1)} %get-tuple-element.5), channel_id=1, source_target_pairs={{0,1},{1,2},{2,3},{3,4},{4,5},{5,6},{6,7},{7,8},{8,9},{9,10},{10,1... | collective-permute-start | bytes 350216 | tf_op jit(solution)/shard_map/ppermute | solution.py:386
  15.3 8.3 %collective-permute-start.3 = (bf16[38,3,512]{2,1,0:T(4,128)(2,1)S(1)}, bf16[38,3,512]{2,1,0:T(4,128)(2,1)S(1)}, u32[]{:S(2)}, u32[]{:S(2)}) collective-permute-start(bf16[38,3,512]{2,1,0:T(4,128)(2,1)S(1)} %get-tuple-element.6), channel_id=1, source_target_pairs={{1,0},{2,1},{3,2},{4,3},{5,4},{6,5},{7,6},{8,7},{9,8},{10,9},{11,1... | collective-permute-start | bytes 350216 | tf_op jit(solution)/shard_map/ppermute | solution.py:387
  39.5 25.8 %all-to-all-start = ((bf16[128,16,128]{2,1,0:T(8,128)(2,1)}), bf16[128,16,128]{2,1,0:T(8,128)(2,1)S(1)}, u32[]{:S(2)}, u32[]{:S(2)}) async-start(bf16[128,16,128]{2,1,0:T(8,128)(2,1)} %bitcast.7), calls=%async_computation | async-start | bytes 1048576 | tf_op jit(solution)/shard_map/all_to_all | solution.py:393

commit v3 on v2

--- a/solution.py
+++ b/solution.py
@@ -16,7 +16,10 @@
 NEG = -1e30
 F32 = jnp.float32
 BF16 = jnp.bfloat16
-VMEM_LIMIT = 56 * 1024 * 1024
+BIG = 24 * 1024 * 1024
+SMALL = 12 * 1024 * 1024
+VM = pl.BlockSpec(memory_space=pltpu.VMEM)
+FAR = pl.BlockSpec(memory_space=pl.ANY)
 
 
 def iota(shape, dim):
@@ -71,34 +74,32 @@
 
 
 def finish_rows(attended, stream, gain, wp, wu, wd):
-    mixed = (dot(attended, wp) + stream.astype(F32)).astype(BF16)
+    mixed = (dot(attended, wp[...]) + stream.astype(F32)).astype(BF16)
     normed = layer_norm(mixed, gain)
     acc = mixed.astype(F32)
     for c in range(4):
         hidden = gelu(dot(normed, wu[:, c * 512 : (c + 1) * 512])).astype(BF16)
         acc = acc + dot(hidden, wd[c * 512 : (c + 1) * 512, :])
-    return acc.astype(BF16)
+    return acc
 
 
 def query_kernel(x_ref, gains_ref, w_ref, q_ref):
-    q_ref[...] = (dot(layer_norm(x_ref[...], gains_ref[0:1, :]), w_ref[0]) * QSCALE).astype(BF16)
-
-
-def query_call(x, gains, qkv_weight):
+    for half in range(2):
+        rows = slice(half * 256, (half + 1) * 256)
+        normed = layer_norm(x_ref[rows, :], gains_ref[0:1, :])
+        q_ref[rows, :] = (dot(normed, w_ref[0, :, :512]) * QSCALE).astype(BF16)
+
+
+def query_call(x, gains, wqkv):
     return pl.pallas_call(
         query_kernel,
-        grid=(1,),
-        in_specs=[
-            pl.BlockSpec((512, 512), lambda i: (0, 0)),
-            pl.BlockSpec((4, 512), lambda i: (0, 0)),
-            pl.BlockSpec((1, 512, 512), lambda i: (0, 0, 0)),
-        ],
-        out_specs=pl.BlockSpec((512, 512), lambda i: (0, 0)),
-        out_shape=jax.ShapeDtypeStruct((512, 512), BF16),
-        compiler_params=pltpu.CompilerParams(vmem_limit_bytes=VMEM_LIMIT),
+        in_specs=[VM] * 3,
+        out_specs=VM,
+        out_shape=pltpu.VMEM((512, 512), BF16),
+        compiler_params=pltpu.CompilerParams(vmem_limit_bytes=SMALL),
         cost_estimate=pl.CostEstimate(flops=2 * 512 ** 3, transcendentals=0, bytes_accessed=3 * 512 * 1024),
         name="query",
-    )(x, gains, qkv_weight)
+    )(x, gains, wqkv)
 
 
 def spread(table, n):
@@ -137,10 +138,10 @@
 def local_bias_call(place, table):
     return pl.pallas_call(
         local_bias_kernel,
-        in_specs=[pl.BlockSpec(memory_space=pltpu.SMEM), pl.BlockSpec(memory_space=pltpu.VMEM)],
-        out_specs=pl.BlockSpec(memory_space=pltpu.VMEM),
-        out_shape=jax.ShapeDtypeStruct((3, 4, 256, 256), F32),
-        compiler_params=pltpu.CompilerParams(vmem_limit_bytes=VMEM_LIMIT),
+        in_specs=[pl.BlockSpec(memory_space=pltpu.SMEM), VM],
+        out_specs=VM,
+        out_shape=pltpu.VMEM((3, 4, 256, 256), F32),
+        compiler_params=pltpu.CompilerParams(vmem_limit_bytes=SMALL),
         cost_estimate=pl.CostEstimate(flops=4_000_000, transcendentals=0, bytes_accessed=3 * 1024 * 1024),
         name="local_bias",
     )(place, table)
@@ -170,41 +171,52 @@
 def group_bias_call(table):
     return pl.pallas_call(
         group_bias_kernel,
-        in_specs=[pl.BlockSpec(memory_space=pltpu.VMEM)],
-        out_specs=pl.BlockSpec(memory_space=pltpu.VMEM),
-        out_shape=jax.ShapeDtypeStruct((5, 4, 128, 128), F32),
-        compiler_params=pltpu.CompilerParams(vmem_limit_bytes=VMEM_LIMIT),
+        in_specs=[VM],
+        out_specs=VM,
+        out_shape=pltpu.VMEM((5, 4, 128, 128), F32),
+        compiler_params=pltpu.CompilerParams(vmem_limit_bytes=SMALL),
         cost_estimate=pl.CostEstimate(flops=4_000_000, transcendentals=0, bytes_accessed=1_300_000),
         name="group_bias",
     )(table)
 
 
-def local_kernel(
-    xpad_ref, x_ref, q_ref, gains_ref, bias_hbm, wqkv_hbm, wp_hbm, wu_hbm, wd_hbm, out_ref,
-    bias, wkv, wp, wu, wd, k_s, v_s, a_s, sems,
-):
-    copies = [
-        pltpu.make_async_copy(wqkv_hbm.at[0, :, pl.ds(512, 1024)], wkv, sems.at[0]),
-        pltpu.make_async_copy(bias_hbm, bias, sems.at[1]),
-        pltpu.make_async_copy(wp_hbm.at[0], wp, sems.at[2]),
-        pltpu.make_async_copy(wu_hbm.at[0], wu, sems.at[3]),
-        pltpu.make_async_copy(wd_hbm.at[0], wd, sems.at[4]),
-    ]
+def fetch_weights(layer, far, near, sems):
+    copies = [pltpu.make_async_copy(a.at[layer], b, sems.at[i]) for i, (a, b) in enumerate(zip(far, near))]
     for c in copies:
         c.start()
+    return copies
+
+
+WEIGHT_SCRATCH = [
+    pltpu.VMEM((512, 512), BF16),
+    pltpu.VMEM((512, 2048), BF16),
+    pltpu.VMEM((2048, 512), BF16),
+    pltpu.SemaphoreType.DMA((3,)),
+]
+
+
+def send_rows(done, stage, pieces):
+    for at, block, slot in pieces:
+        for f in range(4):
+            stage[pl.ds(block * 256 + slot * 4 + f, 16, stride=16), :] = done[at : at + 16, f * 128 : (f + 1) * 128]
+
+
+def local_kernel(
+    xpad_ref, x_ref, q_ref, gains_ref, bias, wqkv, wp_far, wu_far, wd_far, out_ref,
+    k_s, v_s, a_s, stage, wp, wu, wd, sems,
+):
+    copies = fetch_weights(0, (wp_far, wu_far, wd_far), (wp, wu, wd), sems)
     k_s[912:928, :] = jnp.zeros((16, 512), BF16)
     v_s[...] = jnp.ones((928, 1024), BF16)
     for g in range(4):
         v_s[912:928, g * 256 : g * 256 + 128] = jnp.zeros((16, 128), BF16)
-    copies[0].wait()
     for r in range(3):
         rows = slice(r * 304, (r + 1) * 304)
         normed = layer_norm(xpad_ref[rows, :], gains_ref[0:1, :])
-        k_s[rows, :] = dot(normed, wkv[:, :512]).astype(BF16)
-        value = dot(normed, wkv[:, 512:]).astype(BF16)
+        k_s[rows, :] = dot(normed, wqkv[0, :, 512:1024]).astype(BF16)
+        value = dot(normed, wqkv[0, :, 1024:]).astype(BF16)
         for g in range(4):
             v_s[rows, g * 256 : g * 256 + 128] = value[:, g * 128 : (g + 1) * 128]
-    copies[1].wait()
 
     def attend(b, carry):
         at_q = b * 64
@@ -227,73 +239,57 @@
 
     for b in range(8):
         attend(b, 0)
-    for c in copies[2:]:
+    for c in copies:
         c.wait()
     for half in range(2):
         rows = slice(half * 256, (half + 1) * 256)
-        done = finish_rows(a_s[rows, :], x_ref[rows, :], gains_ref[1:2, :], wp[...], wu, wd)
-        for r in range(8):
-            for g in range(2):
-                at = (2 * r + g) * 16
-                lane = (g * 2 + half) * 512
-                out_ref[r * 16 : (r + 1) * 16, lane : lane + 512] = done[at : at + 16, :]
+        done = finish_rows(a_s[rows, :], x_ref[rows, :], gains_ref[1:2, :], wp, wu, wd)
+        send_rows(done, stage, [((2 * r + g) * 16, r, g * 2 + half) for r in range(8) for g in range(2)])
+    out_ref[...] = stage[...].reshape(128, 16, 128).astype(BF16)
 
 
 def local_call(xpad, x, q, gains, bias, wqkv, wp, wu, wd):
-    vmem = pl.BlockSpec(memory_space=pltpu.VMEM)
-    hbm = pl.BlockSpec(memory_space=pl.ANY)
     return pl.pallas_call(
         local_kernel,
-        in_specs=[vmem] * 4 + [hbm] * 5,
-        out_specs=vmem,
-        out_shape=jax.ShapeDtypeStruct((128, 2048), BF16),
+        in_specs=[VM] * 6 + [FAR] * 3,
+        out_specs=VM,
+        out_shape=pltpu.VMEM((128, 16, 128), BF16),
         scratch_shapes=[
-            pltpu.VMEM((3, 4, 256, 256), F32),
-            pltpu.VMEM((512, 1024), BF16),
-            pltpu.VMEM((512, 512), BF16),
-            pltpu.VMEM((512, 2048), BF16),
-            pltpu.VMEM((2048, 512), BF16),
             pltpu.VMEM((928, 512), BF16),
             pltpu.VMEM((928, 1024), BF16),
             pltpu.VMEM((512, 512), BF16),
-            pltpu.SemaphoreType.DMA((5,)),
-        ],
-        compiler_params=pltpu.CompilerParams(vmem_limit_bytes=VMEM_LIMIT),
+            pltpu.VMEM((2048, 128), F32),
+        ]
+        + WEIGHT_SCRATCH,
+        compiler_params=pltpu.CompilerParams(vmem_limit_bytes=BIG),
         cost_estimate=pl.CostEstimate(flops=8_000_000_000, transcendentals=3_000_000, bytes_accessed=12_000_000),
         name="local_layer",
     )(xpad, x, q, gains, bias, wqkv, wp, wu, wd)
 
 
 def group_kernel(
-    in_ref, gains_ref, bias_hbm, wqkv_hbm, wp_hbm, wu_hbm, wd_hbm, out_ref,
-    bias, wqkv, wp, wu, wd, x_s, q_s, k_s, v_s, a_s, sems,
+    in_ref, gains_ref, bias, wqkv, wp_far, wu_far, wd_far, out_ref,
+    x_s, q_s, k_s, v_s, a_s, stage, wp, wu, wd, sems,
 ):
-    copies = [
-        pltpu.make_async_copy(wqkv_hbm.at[1], wqkv, sems.at[0]),
-        pltpu.make_async_copy(bias_hbm, bias, sems.at[1]),
-        pltpu.make_async_copy(wp_hbm.at[1], wp, sems.at[2]),
-        pltpu.make_async_copy(wu_hbm.at[1], wu, sems.at[3]),
-        pltpu.make_async_copy(wd_hbm.at[1], wd, sems.at[4]),
-    ]
-    for c in copies:
-        c.start()
+    copies = fetch_weights(1, (wp_far, wu_far, wd_far), (wp, wu, wd), sems)
+    stage[...] = in_ref[...].astype(F32).reshape(2048, 128)
     for g in range(2):
         for p in range(16):
             r, half = p // 2, p % 2
-            lane = (g * 2 + half) * 512
             at = g * 256 + p * 16
-            x_s[at : at + 16, :] = in_ref[r * 16 : (r + 1) * 16, lane : lane + 512]
+            for f in range(4):
+                x_s[at : at + 16, f * 128 : (f + 1) * 128] = stage[
+                    pl.ds(r * 256 + (g * 2 + half) * 4 + f, 16, stride=16), :
+                ]
     v_s[...] = jnp.ones((512, 1024), BF16)
-    copies[0].wait()
     for g in range(2):
         rows = slice(g * 256, (g + 1) * 256)
         normed = layer_norm(x_s[rows, :], gains_ref[2:3, :])
-        q_s[rows, :] = (dot(normed, wqkv[:, :512]) * QSCALE).astype(BF16)
-        k_s[rows, :] = dot(normed, wqkv[:, 512:1024]).astype(BF16)
-        value = dot(normed, wqkv[:, 1024:]).astype(BF16)
+        q_s[rows, :] = (dot(normed, wqkv[1, :, :512]) * QSCALE).astype(BF16)
+        k_s[rows, :] = dot(normed, wqkv[1, :, 512:1024]).astype(BF16)
+        value = dot(normed, wqkv[1, :, 1024:]).astype(BF16)
         for h in range(4):
             v_s[rows, h * 256 : h * 256 + 128] = value[:, h * 128 : (h + 1) * 128]
-    copies[1].wait()
 
     def attend(b, carry):
         start = min(max(2 * b - 3, 0), 8)
@@ -320,59 +316,52 @@
 
     for b in range(8):
         attend(b, 0)
-    for c in copies[2:]:
+    for c in copies:
         c.wait()
     for g in range(2):
         rows = slice(g * 256, (g + 1) * 256)
-        done = finish_rows(a_s[rows, :], x_s[rows, :], gains_ref[3:4, :], wp[...], wu, wd)
-        for p in range(16):
-            r, half = p // 2, p % 2
-            lane = (g * 2 + half) * 512
-            out_ref[r * 16 : (r + 1) * 16, lane : lane + 512] = done[p * 16 : (p + 1) * 16, :]
+        done = finish_rows(a_s[rows, :], x_s[rows, :], gains_ref[3:4, :], wp, wu, wd)
+        send_rows(done, stage, [(p * 16, p // 2, g * 2 + p % 2) for p in range(16)])
+    out_ref[...] = stage[...].reshape(128, 16, 128).astype(BF16)
 
 
 def group_call(rows, gains, bias, wqkv, wp, wu, wd):
-    vmem = pl.BlockSpec(memory_space=pltpu.VMEM)
-    hbm = pl.BlockSpec(memory_space=pl.ANY)
     return pl.pallas_call(
         group_kernel,
-        in_specs=[vmem] * 2 + [hbm] * 5,
-        out_specs=vmem,
-        out_shape=jax.ShapeDtypeStruct((128, 2048), BF16),
+        in_specs=[VM] * 4 + [FAR] * 3,
+        out_specs=VM,
+        out_shape=pltpu.VMEM((128, 16, 128), BF16),
         scratch_shapes=[
-            pltpu.VMEM((5, 4, 128, 128), F32),
-            pltpu.VMEM((512, 1536), BF16),
-            pltpu.VMEM((512, 512), BF16),
-            pltpu.VMEM((512, 2048), BF16),
-            pltpu.VMEM((2048, 512), BF16),
-            pltpu.VMEM((512, 512), BF16),
+            pltpu.VMEM((512, 512), F32),
             pltpu.VMEM((512, 512), BF16),
             pltpu.VMEM((512, 512), BF16),
             pltpu.VMEM((512, 1024), BF16),
             pltpu.VMEM((512, 512), BF16),
-            pltpu.SemaphoreType.DMA((5,)),
-        ],
-        compiler_params=pltpu.CompilerParams(vmem_limit_bytes=VMEM_LIMIT),
+            pltpu.VMEM((2048, 128), F32),
+        ]
+        + WEIGHT_SCRATCH,
+        compiler_params=pltpu.CompilerParams(vmem_limit_bytes=BIG),
         cost_estimate=pl.CostEstimate(flops=7_000_000_000, transcendentals=3_000_000, bytes_accessed=10_000_000),
         name="group_layer",
     )(rows, gains, bias, wqkv, wp, wu, wd)
 
 
-def place_kernel(in_ref, out_ref):
+def place_kernel(in_ref, out_ref, stage):
+    stage[...] = in_ref[...].astype(F32).reshape(2048, 128)
     for r in range(8):
-        for g in range(2):
-            for half in range(2):
-                lane = (g * 2 + half) * 512
-                out_ref[half * 16 + 2 * r + g] = in_ref[r * 16 : (r + 1) * 16, lane : lane + 512]
+        for slot in range(4):
+            parts = [stage[pl.ds(r * 256 + slot * 4 + f, 16, stride=16), :] for f in range(4)]
+            out_ref[slot % 2 * 16 + 2 * r + slot // 2] = jnp.concatenate(parts, axis=1).astype(BF16)
 
 
 def place_call(rows):
     return pl.pallas_call(
         place_kernel,
-        in_specs=[pl.BlockSpec(memory_space=pltpu.VMEM)],
-        out_specs=pl.BlockSpec(memory_space=pltpu.VMEM),
+        in_specs=[VM],
+        out_specs=VM,
         out_shape=jax.ShapeDtypeStruct((TR, TC, D), BF16),
-        compiler_params=pltpu.CompilerParams(vmem_limit_bytes=VMEM_LIMIT),
+        scratch_shapes=[pltpu.VMEM((2048, 128), F32)],
+        compiler_params=pltpu.CompilerParams(vmem_limit_bytes=SMALL),
         name="place",
     )(rows)
 
@@ -389,8 +378,7 @@
 
 
 def exchange(rows):
-    shaped = rows.reshape(128, 16, 128)
-    return lax.all_to_all(shaped, ("row", "col"), 0, 0, tiled=True).reshape(128, 2048)
+    return lax.all_to_all(rows, ("row", "col"), 0, 0, tiled=True)
 
 
 def body(tokens, norm_gains, qkv_weight, rel_bias, proj_weight, up_weight, down_weight):
@@ -407,13 +395,16 @@
     group_table = jnp.pad(table[1], ((0, 0), (1, 2), (0, 3))).reshape(HEADS, 256)
     place = jnp.stack([lax.axis_index("row") * TR, lax.axis_index("col") * TC]).astype(jnp.int32)
 
-    q = query_call(x, norm_gains, qkv_weight)
+    near = lambda a: pltpu.with_memory_space_constraint(a, pltpu.VMEM)
+    wqkv, wp, wu, wd = near(qkv_weight), proj_weight, up_weight, down_weight
+    x = near(x)
+    q = query_call(x, norm_gains, wqkv)
     local_bias = local_bias_call(place, local_table)
     group_bias = group_bias_call(group_table)
-    sent = local_call(xpad, x, q, norm_gains, local_bias, qkv_weight, proj_weight, up_weight, down_weight)
+    sent = local_call(near(xpad), x, q, norm_gains, local_bias, wqkv, wp, wu, wd)
     got = exchange(sent)
-    back = group_call(got, norm_gains, group_bias, qkv_weight, proj_weight, up_weight, down_weight)
-    return place_call(exchange(back))
+    back = group_call(near(got), norm_gains, group_bias, wqkv, wp, wu, wd)
+    return place_call(near(exchange(back)))
 
 
 def solution(mesh):

time: 101 us -> 98.1 us (0.971)
  Pallas kernels: 34.6 us -> 23.7 us
  local copies, waits for them, and re-layouts: 8.8 us -> 13.6 us
  waiting for transfers between devices: 12.5 us -> 16.6 us
  other arithmetic: 2.22 us -> 0.72 us
  starting transfers between devices: 24.1 us -> 25.2 us
    pallas_call x5, Pallas kernels: 31.6 us -> 22.5 us  [the longest x1 10.6 us: group_call(): pl.pallas_call(group_kernel, in_specs=[VM] * 4 + [FAR] * 3, out_specs=VM,...]
    unnamed x11 -> x31, local copies, waits for them, and re-layouts: 6.23 us -> 12.2 us
    ppermute x2, waiting for transfers between devices: 1.6 us -> 4.81 us  [edges(): after = lax.ppermute(head, axis, [(i + 1, i) for i in range(ends)])]
    pallas_call x1, Pallas kernels: 3 us -> 1.13 us  [local_bias_call(): pl.pallas_call(local_bias_kernel, in_specs=[pl.BlockSpec(memory_space=plt...]
  transfers between devices with their start and end apart: 5 -> 5, of which waited for: 2 -> 3; matrix products, arithmetic and copies ran while one was open for 3% -> 2% of each run, Pallas kernels for 8% -> 3%
where the time goes in v3:
time: 98.1 us; the launch traced here: 97.6 us
  starting transfers between devices  25.2 us (26%)
  Pallas kernels  23.7 us (24%)
  blocking collectives  17.5 us (18%)
  waiting for transfers between devices  16.6 us (17%)
  local copies, waits for them, and re-layouts  13.6 us (14%)
    all_to_all x1, blocking collectives, exchange(): return lax.all_to_all(rows, ('row', 'col'), 0, 0, tiled=True)  17.5 us
    all_to_all x1, starting transfers between devices, exchange(): return lax.all_to_all(rows, ('row', 'col'), 0, 0, tiled=True)  12.4 us
    unnamed x31, local copies, waits for them, and re-layouts  12.2 us
    all_to_all x1, waiting for transfers between devices, exchange(): return lax.all_to_all(rows, ('row', 'col'), 0, 0, tiled=True)  11.8 us
    pallas_call x1, Pallas kernels, group_call(): pl.pallas_call(group_kernel, in_specs=[VM] * 4 + [FAR] * 3, out_specs=VM,...  10.6 us
    ppermute x2, starting transfers between devices, edges(): before = lax.ppermute(tail, axis, [(i, i + 1) for i in range(ends)])  9.55 us
    pallas_call x1, Pallas kernels, local_call(): pl.pallas_call(local_kernel, in_specs=[VM] * 6 + [FAR] * 3, out_specs=VM,...  9.4 us
    ppermute x2, waiting for transfers between devices, edges(): after = lax.ppermute(head, axis, [(i + 1, i) for i in range(ends)])  4.81 us
  transfers between devices with their start and end apart: 5, of which 3 were waited for; matrix products, arithmetic and copies ran while one was open for 2% of the time, Pallas kernels for 3%

profile of v3, /device:TPU:1, one launch (start us, length us, event | category | flops | bytes accessed | tf_op | source)
XLA Modules:
  0.0 97.6 jit_solution(5877169362951320713)
XLA Ops:
  0.0 0.9 fusion.1
  0.9 4.4 %collective-permute-start = (bf16[3,16,512]{2,1,0:T(8,128)(2,1)S(1)}, bf16[3,16,512]{2,1,0:T(8,128)(2,1)S(1)}, u32[]{:S(2)}, u32[]{:S(2)}) collective-permute-start(bf16[3,16,512]{2,1,0:T(8,128)(2,1)S(1)} %get-tuple-element.8), channel_id=1, source_target_pairs={{0,16},{16,32},{32,48},{48,64},{64,80},{80,96},{96,112},{1,17},{17... | collective-permute-start | bytes 147464 | tf_op jit(solution)/shard_map/ppermute | solution.py:375
  5.3 1.3 %collective-permute-start.1 = (bf16[3,16,512]{2,1,0:T(8,128)(2,1)S(1)}, bf16[3,16,512]{2,1,0:T(8,128)(2,1)S(1)}, u32[]{:S(2)}, u32[]{:S(2)}) collective-permute-start(bf16[3,16,512]{2,1,0:T(8,128)(2,1)S(1)} %get-tuple-element.7), channel_id=1, source_target_pairs={{16,0},{32,16},{48,32},{64,48},{80,64},{96,80},{112,96},{17,1},{33... | collective-permute-start | bytes 147464 | tf_op jit(solution)/shard_map/ppermute | solution.py:376
  6.6 1.1 %copy.10 = f32[2,16,13,13]{3,1,2,0:T(8,128)S(1)} copy(f32[2,16,13,13]{1,0,3,2:T(2,128)} %param.10) | data formatting | bytes 43264 | tf_op args[3]
  8.1 2.2 %collective-permute-done.1 = bf16[3,16,512]{2,1,0:T(8,128)(2,1)S(1)} collective-permute-done((bf16[3,16,512]{2,1,0:T(8,128)(2,1)S(1)}, bf16[3,16,512]{2,1,0:T(8,128)(2,1)S(1)}, u32[]{:S(2)}, u32[]{:S(2)}) %collective-permute-start.1) | collective-permute-done | bytes 49184 | tf_op jit(solution)/shard_map/ppermute | solution.py:376
  10.4 5.2 %collective-permute-start.2 = (bf16[38,3,512]{2,1,0:T(4,128)(2,1)S(1)}, bf16[38,3,512]{2,1,0:T(4,128)(2,1)S(1)}, u32[]{:S(2)}, u32[]{:S(2)}) collective-permute-start(bf16[38,3,512]{2,1,0:T(4,128)(2,1)S(1)} %get-tuple-element.5), channel_id=1, source_target_pairs={{0,1},{1,2},{2,3},{3,4},{4,5},{5,6},{6,7},{7,8},{8,9},{9,10},{10,1... | collective-permute-start | bytes 350216 | tf_op jit(solution)/shard_map/ppermute | solution.py:375
  15.6 1.9 %collective-permute-start.3 = (bf16[38,3,512]{2,1,0:T(4,128)(2,1)S(1)}, bf16[38,3,512]{2,1,0:T(4,128)(2,1)S(1)}, u32[]{:S(2)}, u32[]{:S(2)}) collective-permute-start(bf16[38,3,512]{2,1,0:T(4,128)(2,1)S(1)} %get-tuple-element.6), channel_id=1, source_target_pairs={{1,0},{2,1},{3,2},{4,3},{5,4},{6,5},{7,6},{8,7},{9,8},{10,9},{11,1... | collective-permute-start | bytes 350216 | tf_op jit(solution)/shard_map/ppermute | solution.py:376
  17.6 1.1 %local_bias.1.bias = f32[3,4,256,256]{3,2,1,0:T(8,128)S(1)} custom-call(s32[2]{0:T(128)S(1)} %pad_add_fusion.place_ref, f32[16,512]{1,0:T(8,128)S(1)} %pad.13.table_ref), custom_call_target="tpu_custom_call" | custom-call | flops 4000000 | bytes 3145728 | tf_op jit(solution)/shard_map/local_bias/pallas_call | solution.py:139
  18.8 0.7 query.1.q_ref
  19.6 2.6 %collective-permute-done.3 = bf16[38,3,512]{2,1,0:T(4,128)(2,1)S(1)} collective-permute-done((bf16[38,3,512]{2,1,0:T(4,128)(2,1)S(1)}, bf16[38,3,512]{2,1,0:T(4,128)(2,1)S(1)}, u32[]{:S(2)}, u32[]{:S(2)}) %collective-permute-start.3) | collective-permute-done | bytes 116768 | tf_op jit(solution)/shard_map/ppermute | solution.py:376
  22.8 2.2 %copy-done.9 = bf16[2,2048,512]{2,1,0:T(8,128)(2,1)S(1)} copy-done((bf16[2,2048,512]{2,1,0:T(8,128)(2,1)S(1)}, bf16[2,2048,512]{2,1,0:T(8,128)(2,1)}, u32[]{:S(2)}) %copy-start.9) | copy-done | bytes 4194328
  25.0 9.4 %local_layer.1 = bf16[128,16,128]{2,1,0:T(8,128)(2,1)S(1)} custom-call(bf16[912,512]{1,0:T(8,128)(2,1)S(1)} %bitcast.10, bf16[512,512]{1,0:T(8,128)(2,1)S(1)} %bitcast.9, bf16[512,512]{1,0:T(8,128)(2,1)S(1)} %query.1.q_ref, f32[4,512]{1,0:T(4,128)S(1)} %copy-done.6, f32[3,4,256,256]{3,2,1,0:T(8,128)S(1)} %local_bias.1.bias, ...), custom_call_target="tpu_custom_call" | custom-call | flops 8000000000 | bytes 12000000 | tf_op jit(solution)/shard_map/local_layer/pallas_call | solution.py:252
  34.4 0.8 copy-done.5
  35.2 12.4 %all-to-all-start = ((bf16[128,16,128]{2,1,0:T(8,128)(2,1)}), bf16[128,16,128]{2,1,0:T(8,128)(2,1)}, u32[]{:S(2)}, u32[]{:S(2)}) async-start(bf16[128,16,128]{2,1,0:T(8,128)(2,1)} %copy-done.5), calls=%async_computation | async-start | bytes 1048576 | tf_op jit(solution)/shard_map/all_to_all | solution.py:381
  47.8 0.7 group_bias.1.bias
  48.5 1.1 %copy-done.3 = f32[5,4,128,128]{3,2,1,0:T(8,128)} copy-done((f32[5,4,128,128]{3,2,1,0:T(8,128)}, f32[5,4,128,128]{3,2,1,0:T(8,128)S(1)}, u32[]{:S(2)}) %copy-start.3) | copy-done | bytes 1310744
  49.6 11.8 %all-to-all-done.in_ref = bf16[128,16,128]{2,1,0:T(8,128)(2,1)} async-done(((bf16[128,16,128]{2,1,0:T(8,128)(2,1)}), bf16[128,16,128]{2,1,0:T(8,128)(2,1)}, u32[]{:S(2)}, u32[]{:S(2)}) %all-to-all-start) | async-done | bytes 524320 | tf_op jit(solution)/shard_map/all_to_all | solution.py:381
  61.4 1.3 %copy-done.4 = f32[5,4,128,128]{3,2,1,0:T(8,128)S(1)} copy-done((f32[5,4,128,128]{3,2,1,0:T(8,128)S(1)}, f32[5,4,128,128]{3,2,1,0:T(8,128)}, u32[]{:S(2)}) %copy-start.4) | copy-done | bytes 1310744
  62.7 2.2 %copy-done.8 = bf16[2,512,2048]{2,1,0:T(8,128)(2,1)S(1)} copy-done((bf16[2,512,2048]{2,1,0:T(8,128)(2,1)S(1)}, bf16[2,512,2048]{2,1,0:T(8,128)(2,1)}, u32[]{:S(2)}) %copy-start.8) | copy-done | bytes 4194328
  64.9 2.2 %copy-done.10 = bf16[2,2048,512]{2,1,0:T(8,128)(2,1)S(1)} copy-done((bf16[2,2048,512]{2,1,0:T(8,128)(2,1)S(1)}, bf16[2,2048,512]{2,1,0:T(8,128)(2,1)}, u32[]{:S(2)}) %copy-start.10) | copy-done | bytes 4194328
  67.1 1.2 %copy-done.12 = bf16[2,512,512]{2,1,0:T(8,128)(2,1)S(1)} copy-done((bf16[2,512,512]{2,1,0:T(8,128)(2,1)S(1)}, bf16[2,512,512]{2,1,0:T(8,128)(2,1)}, u32[]{:S(2)}) %copy-start.12) | copy-done | bytes 1048600
  68.3 10.6 %group_layer.1 = bf16[128,16,128]{2,1,0:T(8,128)(2,1)S(1)} custom-call(bf16[128,16,128]{2,1,0:T(8,128)(2,1)} %all-to-all-done.in_ref, f32[4,512]{1,0:T(4,128)S(1)} %copy-done.6, f32[5,4,128,128]{3,2,1,0:T(8,128)S(1)} %copy-done.4, bf16[2,512,1536]{2,1,0:T(8,128)(2,1)S(1)} %copy-done, bf16[2,512,512]{2,1,0:T(8,128)(2,1)S(1)} %copy-done.12, ...), custom_call_target="tpu_custom_call" | custom-call | flops 7000000000 | bytes 10000000 | tf_op jit(solution)/shard_map/group_layer/pallas_call | solution.py:329
  78.9 17.5 %all_to_all.10.in_ref = bf16[128,16,128]{2,1,0:T(8,128)(2,1)S(1)} all-to-all(bf16[128,16,128]{2,1,0:T(8,128)(2,1)S(1)} %group_layer.1), channel_id=1, replica_groups=mesh['row'=8,'col'=16] {'row','col'}, dimensions={0} | all-to-all | bytes 1048576 | tf_op jit(solution)/shard_map/all_to_all | solution.py:381
  96.4 1.2 %place.1 = bf16[32,16,512]{2,1,0:T(8,128)(2,1)} custom-call(bf16[128,16,128]{2,1,0:T(8,128)(2,1)S(1)} %all_to_all.10.in_ref), custom_call_target="tpu_custom_call" | custom-call | tf_op jit(solution)/shard_map/place/pallas_call | solution.py:358
  (38 shorter events, 1.4 us)
Async XLA Ops:
  0.0 8.0 %copy-start.1 = (bf16[32,16,512]{2,1,0:T(8,128)(2,1)S(1)}, bf16[32,16,512]{2,1,0:T(8,128)(2,1)}, u32[]{:S(2)}) copy-start(bf16[32,16,512]{2,1,0:T(8,128)(2,1)} %param.7) | copy-start | bytes 1572868
  0.9 7.1 %collective-permute-start = (bf16[3,16,512]{2,1,0:T(8,128)(2,1)S(1)}, bf16[3,16,512]{2,1,0:T(8,128)(2,1)S(1)}, u32[]{:S(2)}, u32[]{:S(2)}) collective-permute-start(bf16[3,16,512]{2,1,0:T(8,128)(2,1)S(1)} %get-tuple-element.8), channel_id=1, source_target_pairs={{0,16},{16,32},{32,48},{48,64},{64,80},{80,96},{96,112},{1,17},{17... | collective-permute-start | bytes 147464 | tf_op jit(solution)/shard_map/ppermute | solution.py:375
  5.3 5.0 %collective-permute-start.1 = (bf16[3,16,512]{2,1,0:T(8,128)(2,1)S(1)}, bf16[3,16,512]{2,1,0:T(8,128)(2,1)S(1)}, u32[]{:S(2)}, u32[]{:S(2)}) collective-permute-start(bf16[3,16,512]{2,1,0:T(8,128)(2,1)S(1)} %get-tuple-element.7), channel_id=1, source_target_pairs={{16,0},{32,16},{48,32},{64,48},{80,64},{96,80},{112,96},{17,1},{33... | collective-permute-start | bytes 147464 | tf_op jit(solution)/shard_map/ppermute | solution.py:376
  10.3 8.5 %copy-start = (bf16[2,512,1536]{2,1,0:T(8,128)(2,1)S(1)}, bf16[2,512,1536]{2,1,0:T(8,128)(2,1)}, u32[]{:S(2)}) copy-start(bf16[2,512,1536]{2,1,0:T(8,128)(2,1)} %wqkv.3) | copy-start | bytes 9437188
  10.3 8.5 %copy-start.2 = (bf16[32,16,512]{2,1,0:T(8,128)(2,1)S(1)}, bf16[32,16,512]{2,1,0:T(8,128)(2,1)}, u32[]{:S(2)}) copy-start(bf16[32,16,512]{2,1,0:T(8,128)(2,1)} %param.7) | copy-start | bytes 1572868
  10.3 8.5 %copy-start.6 = (f32[4,512]{1,0:T(4,128)S(1)}, f32[4,512]{1,0:T(4,128)}, u32[]{:S(2)}) copy-start(f32[4,512]{1,0:T(4,128)} %gains_ref.5) | copy-start | bytes 24580
  10.4 9.1 %collective-permute-start.2 = (bf16[38,3,512]{2,1,0:T(4,128)(2,1)S(1)}, bf16[38,3,512]{2,1,0:T(4,128)(2,1)S(1)}, u32[]{:S(2)}, u32[]{:S(2)}) collective-permute-start(bf16[38,3,512]{2,1,0:T(4,128)(2,1)S(1)} %get-tuple-element.5), channel_id=1, source_target_pairs={{0,1},{1,2},{2,3},{3,4},{4,5},{5,6},{6,7},{7,8},{8,9},{9,10},{10,1... | collective-permute-start | bytes 350216 | tf_op jit(solution)/shard_map/ppermute | solution.py:375
  15.6 6.5 %collective-permute-start.3 = (bf16[38,3,512]{2,1,0:T(4,128)(2,1)S(1)}, bf16[38,3,512]{2,1,0:T(4,128)(2,1)S(1)}, u32[]{:S(2)}, u32[]{:S(2)}) collective-permute-start(bf16[38,3,512]{2,1,0:T(4,128)(2,1)S(1)} %get-tuple-element.6), channel_id=1, source_target_pairs={{1,0},{2,1},{3,2},{4,3},{5,4},{6,5},{7,6},{8,7},{9,8},{10,9},{11,1... | collective-permute-start | bytes 350216 | tf_op jit(solution)/shard_map/ppermute | solution.py:376
  18.8 4.0 %copy-start.7 = (bf16[2,512,2048]{2,1,0:T(8,128)(2,1)S(1)}, bf16[2,512,2048]{2,1,0:T(8,128)(2,1)}, u32[]{:S(2)}) copy-start(bf16[2,512,2048]{2,1,0:T(8,128)(2,1)} %wu_far.3) | copy-start | bytes 12582916
  19.6 3.3 %copy-start.11 = (bf16[2,512,512]{2,1,0:T(8,128)(2,1)S(1)}, bf16[2,512,512]{2,1,0:T(8,128)(2,1)}, u32[]{:S(2)}) copy-start(bf16[2,512,512]{2,1,0:T(8,128)(2,1)} %wp_far.3) | copy-start | bytes 3145732
  22.8 2.2 %copy-start.9 = (bf16[2,2048,512]{2,1,0:T(8,128)(2,1)S(1)}, bf16[2,2048,512]{2,1,0:T(8,128)(2,1)}, u32[]{:S(2)}) copy-start(bf16[2,2048,512]{2,1,0:T(8,128)(2,1)} %wd_far.3) | copy-start | bytes 12582916
  34.4 0.8 copy-start.5
  35.2 26.2 %all-to-all-start = ((bf16[128,16,128]{2,1,0:T(8,128)(2,1)}), bf16[128,16,128]{2,1,0:T(8,128)(2,1)}, u32[]{:S(2)}, u32[]{:S(2)}) async-start(bf16[128,16,128]{2,1,0:T(8,128)(2,1)} %copy-done.5), calls=%async_computation | async-start | bytes 1048576 | tf_op jit(solution)/shard_map/all_to_all | solution.py:381
  48.5 1.1 %copy-start.3 = (f32[5,4,128,128]{3,2,1,0:T(8,128)}, f32[5,4,128,128]{3,2,1,0:T(8,128)S(1)}, u32[]{:S(2)}) copy-start(f32[5,4,128,128]{3,2,1,0:T(8,128)S(1)} %group_bias.1.bias) | copy-start | bytes 3932164
  61.4 1.3 %copy-start.4 = (f32[5,4,128,128]{3,2,1,0:T(8,128)S(1)}, f32[5,4,128,128]{3,2,1,0:T(8,128)}, u32[]{:S(2)}) copy-start(f32[5,4,128,128]{3,2,1,0:T(8,128)} %copy-done.3) | copy-start | bytes 3932164
  62.7 2.2 %copy-start.8 = (bf16[2,512,2048]{2,1,0:T(8,128)(2,1)S(1)}, bf16[2,512,2048]{2,1,0:T(8,128)(2,1)}, u32[]{:S(2)}) copy-start(bf16[2,512,2048]{2,1,0:T(8,128)(2,1)} %wu_far.3) | copy-start | bytes 12582916
  64.9 2.2 %copy-start.10 = (bf16[2,2048,512]{2,1,0:T(8,128)(2,1)S(1)}, bf16[2,2048,512]{2,1,0:T(8,128)(2,1)}, u32[]{:S(2)}) copy-start(bf16[2,2048,512]{2,1,0:T(8,128)(2,1)} %wd_far.3) | copy-start | bytes 12582916
  67.1 1.2 %copy-start.12 = (bf16[2,512,512]{2,1,0:T(8,128)(2,1)S(1)}, bf16[2,512,512]{2,1,0:T(8,128)(2,1)}, u32[]{:S(2)}) copy-start(bf16[2,512,512]{2,1,0:T(8,128)(2,1)} %wp_far.3) | copy-start | bytes 3145732

commit v4 on v3

--- a/solution.py
+++ b/solution.py
@@ -19,7 +19,7 @@
 BIG = 24 * 1024 * 1024
 SMALL = 12 * 1024 * 1024
 VM = pl.BlockSpec(memory_space=pltpu.VMEM)
-FAR = pl.BlockSpec(memory_space=pl.ANY)
+FAR = pl.BlockSpec(memory_space=pltpu.HBM)
 
 
 def iota(shape, dim):
@@ -173,7 +173,7 @@
         group_bias_kernel,
         in_specs=[VM],
         out_specs=VM,
-        out_shape=pltpu.VMEM((5, 4, 128, 128), F32),
+        out_shape=pltpu.HBM((5, 4, 128, 128), F32),
         compiler_params=pltpu.CompilerParams(vmem_limit_bytes=SMALL),
         cost_estimate=pl.CostEstimate(flops=4_000_000, transcendentals=0, bytes_accessed=1_300_000),
         name="group_bias",
@@ -253,7 +253,7 @@
         local_kernel,
         in_specs=[VM] * 6 + [FAR] * 3,
         out_specs=VM,
-        out_shape=pltpu.VMEM((128, 16, 128), BF16),
+        out_shape=pltpu.HBM((128, 16, 128), BF16),
         scratch_shapes=[
             pltpu.VMEM((928, 512), BF16),
             pltpu.VMEM((928, 1024), BF16),
@@ -268,9 +268,11 @@
 
 
 def group_kernel(
-    in_ref, gains_ref, bias, wqkv, wp_far, wu_far, wd_far, out_ref,
-    x_s, q_s, k_s, v_s, a_s, stage, wp, wu, wd, sems,
+    in_ref, gains_ref, bias_far, wqkv, wp_far, wu_far, wd_far, out_ref,
+    x_s, q_s, k_s, v_s, a_s, stage, wp, wu, wd, sems, bias, bias_sem,
 ):
+    bias_copy = pltpu.make_async_copy(bias_far, bias, bias_sem)
+    bias_copy.start()
     copies = fetch_weights(1, (wp_far, wu_far, wd_far), (wp, wu, wd), sems)
     stage[...] = in_ref[...].astype(F32).reshape(2048, 128)
     for g in range(2):
@@ -290,6 +292,8 @@
         value = dot(normed, wqkv[1, :, 1024:]).astype(BF16)
         for h in range(4):
             v_s[rows, h * 256 : h * 256 + 128] = value[:, h * 128 : (h + 1) * 128]
+
+    bias_copy.wait()
 
     def attend(b, carry):
         start = min(max(2 * b - 3, 0), 8)
@@ -328,7 +332,7 @@
 def group_call(rows, gains, bias, wqkv, wp, wu, wd):
     return pl.pallas_call(
         group_kernel,
-        in_specs=[VM] * 4 + [FAR] * 3,
+        in_specs=[VM, VM, FAR, VM] + [FAR] * 3,
         out_specs=VM,
         out_shape=pltpu.VMEM((128, 16, 128), BF16),
         scratch_shapes=[
@@ -339,7 +343,8 @@
             pltpu.VMEM((512, 512), BF16),
             pltpu.VMEM((2048, 128), F32),
         ]
-        + WEIGHT_SCRATCH,
+        + WEIGHT_SCRATCH
+        + [pltpu.VMEM((5, 4, 128, 128), F32), pltpu.SemaphoreType.DMA(())],
         compiler_params=pltpu.CompilerParams(vmem_limit_bytes=BIG),
         cost_estimate=pl.CostEstimate(flops=7_000_000_000, transcendentals=3_000_000, bytes_accessed=10_000_000),
         name="group_layer",
@@ -396,7 +401,8 @@
     place = jnp.stack([lax.axis_index("row") * TR, lax.axis_index("col") * TC]).astype(jnp.int32)
 
     near = lambda a: pltpu.with_memory_space_constraint(a, pltpu.VMEM)
-    wqkv, wp, wu, wd = near(qkv_weight), proj_weight, up_weight, down_weight
+    far = lambda a: pltpu.with_memory_space_constraint(a, pltpu.HBM)
+    wqkv, wp, wu, wd = near(qkv_weight), far(proj_weight), far(up_weight), far(down_weight)
     x = near(x)
     q = query_call(x, norm_gains, wqkv)
     local_bias = local_bias_call(place, local_table)

time: 98.1 us -> 92 us (0.938)
  local copies, waits for them, and re-layouts: 13.6 us -> 3.96 us
  Pallas kernels: 23.7 us -> 27.4 us
    unnamed x31 -> x15, local copies, waits for them, and re-layouts: 12.2 us -> 2.6 us
    pallas_call x1, Pallas kernels: 9.4 us -> 12.1 us  [local_call(): pl.pallas_call(local_kernel, in_specs=[VM] * 6 + [FAR] * 3, out_specs=VM,...]
    pallas_call x1, Pallas kernels: 0.71 us -> 1.79 us  [group_bias_call(): pl.pallas_call(group_bias_kernel, in_specs=[VM], out_specs=VM, out_shape=...]
  transfers between devices with their start and end apart: 5 -> 5, of which waited for: 3 -> 3; matrix products, arithmetic and copies ran while one was open for 2% -> 2% of each run, Pallas kernels for 3% -> 4%
where the time goes in v4:
time: 92 us; the launch traced here: 91.6 us
  Pallas kernels  27.4 us (30%)
  starting transfers between devices  25.2 us (27%)
  blocking collectives  17.5 us (19%)
  waiting for transfers between devices  16.6 us (18%)
  local copies, waits for them, and re-layouts  3.96 us (4%)
    all_to_all x1, blocking collectives, exchange(): return lax.all_to_all(rows, ('row', 'col'), 0, 0, tiled=True)  17.5 us
    all_to_all x1, starting transfers between devices, exchange(): return lax.all_to_all(rows, ('row', 'col'), 0, 0, tiled=True)  12.4 us
    pallas_call x1, Pallas kernels, local_call(): pl.pallas_call(local_kernel, in_specs=[VM] * 6 + [FAR] * 3, out_specs=VM,...  12.1 us
    all_to_all x1, waiting for transfers between devices, exchange(): return lax.all_to_all(rows, ('row', 'col'), 0, 0, tiled=True)  11.8 us
    pallas_call x1, Pallas kernels, group_call(): pl.pallas_call(group_kernel, in_specs=[VM, VM, FAR, VM] + [FAR] * 3, out_...  10.5 us
    ppermute x2, starting transfers between devices, edges(): before = lax.ppermute(tail, axis, [(i, i + 1) for i in range(ends)])  9.55 us
    ppermute x2, waiting for transfers between devices, edges(): after = lax.ppermute(head, axis, [(i + 1, i) for i in range(ends)])  4.83 us
    ppermute x2, starting transfers between devices, edges(): after = lax.ppermute(head, axis, [(i + 1, i) for i in range(ends)])  3.21 us
  transfers between devices with their start and end apart: 5, of which 3 were waited for; matrix products, arithmetic and copies ran while one was open for 2% of the time, Pallas kernels for 4%

profile of v4, /device:TPU:1, one launch (start us, length us, event | category | flops | bytes accessed | tf_op | source)
XLA Modules:
  0.0 91.6 jit_solution(6063237374473232181)
XLA Ops:
  0.0 0.9 fusion.1
  0.9 4.4 %collective-permute-start = (bf16[3,16,512]{2,1,0:T(8,128)(2,1)S(1)}, bf16[3,16,512]{2,1,0:T(8,128)(2,1)S(1)}, u32[]{:S(2)}, u32[]{:S(2)}) collective-permute-start(bf16[3,16,512]{2,1,0:T(8,128)(2,1)S(1)} %get-tuple-element.8), channel_id=1, source_target_pairs={{0,16},{16,32},{32,48},{48,64},{64,80},{80,96},{96,112},{1,17},{17... | collective-permute-start | bytes 147464 | tf_op jit(solution)/shard_map/ppermute | solution.py:380
  5.3 1.3 %collective-permute-start.1 = (bf16[3,16,512]{2,1,0:T(8,128)(2,1)S(1)}, bf16[3,16,512]{2,1,0:T(8,128)(2,1)S(1)}, u32[]{:S(2)}, u32[]{:S(2)}) collective-permute-start(bf16[3,16,512]{2,1,0:T(8,128)(2,1)S(1)} %get-tuple-element.7), channel_id=1, source_target_pairs={{16,0},{32,16},{48,32},{64,48},{80,64},{96,80},{112,96},{17,1},{33... | collective-permute-start | bytes 147464 | tf_op jit(solution)/shard_map/ppermute | solution.py:381
  6.6 1.1 %copy.10 = f32[2,16,13,13]{3,1,2,0:T(8,128)S(1)} copy(f32[2,16,13,13]{1,0,3,2:T(2,128)} %param.10) | data formatting | bytes 43264 | tf_op args[3]
  7.8 0.1 reshape.14
  7.9 0.1 pad.20.clone
  8.1 2.2 %collective-permute-done.1 = bf16[3,16,512]{2,1,0:T(8,128)(2,1)S(1)} collective-permute-done((bf16[3,16,512]{2,1,0:T(8,128)(2,1)S(1)}, bf16[3,16,512]{2,1,0:T(8,128)(2,1)S(1)}, u32[]{:S(2)}, u32[]{:S(2)}) %collective-permute-start.1) | collective-permute-done | bytes 49184 | tf_op jit(solution)/shard_map/ppermute | solution.py:381
  10.3 0.1 fusion
  10.4 5.2 %collective-permute-start.2 = (bf16[38,3,512]{2,1,0:T(4,128)(2,1)S(1)}, bf16[38,3,512]{2,1,0:T(4,128)(2,1)S(1)}, u32[]{:S(2)}, u32[]{:S(2)}) collective-permute-start(bf16[38,3,512]{2,1,0:T(4,128)(2,1)S(1)} %get-tuple-element.5), channel_id=1, source_target_pairs={{0,1},{1,2},{2,3},{3,4},{4,5},{5,6},{6,7},{7,8},{8,9},{9,10},{10,1... | collective-permute-start | bytes 350216 | tf_op jit(solution)/shard_map/ppermute | solution.py:380
  15.6 1.9 %collective-permute-start.3 = (bf16[38,3,512]{2,1,0:T(4,128)(2,1)S(1)}, bf16[38,3,512]{2,1,0:T(4,128)(2,1)S(1)}, u32[]{:S(2)}, u32[]{:S(2)}) collective-permute-start(bf16[38,3,512]{2,1,0:T(4,128)(2,1)S(1)} %get-tuple-element.6), channel_id=1, source_target_pairs={{1,0},{2,1},{3,2},{4,3},{5,4},{6,5},{7,6},{8,7},{9,8},{10,9},{11,1... | collective-permute-start | bytes 350216 | tf_op jit(solution)/shard_map/ppermute | solution.py:381
  17.6 0.1 pad_add_fusion.place_ref
  17.6 1.1 %local_bias.1.bias = f32[3,4,256,256]{3,2,1,0:T(8,128)S(1)} custom-call(s32[2]{0:T(128)S(1)} %pad_add_fusion.place_ref, f32[16,512]{1,0:T(8,128)S(1)} %pad.13.table_ref), custom_call_target="tpu_custom_call" | custom-call | flops 4000000 | bytes 3145728 | tf_op jit(solution)/shard_map/local_bias/pallas_call | solution.py:139
  18.8 0.7 query.1.q_ref
  19.6 2.6 %collective-permute-done.3 = bf16[38,3,512]{2,1,0:T(4,128)(2,1)S(1)} collective-permute-done((bf16[38,3,512]{2,1,0:T(4,128)(2,1)S(1)}, bf16[38,3,512]{2,1,0:T(4,128)(2,1)S(1)}, u32[]{:S(2)}, u32[]{:S(2)}) %collective-permute-start.3) | collective-permute-done | bytes 116768 | tf_op jit(solution)/shard_map/ppermute | solution.py:381
  22.2 0.6 maximum_maximum_fusion
  22.8 12.1 %local_layer.1 = bf16[128,16,128]{2,1,0:T(8,128)(2,1)} custom-call(bf16[912,512]{1,0:T(8,128)(2,1)S(1)} %bitcast.10, bf16[512,512]{1,0:T(8,128)(2,1)S(1)} %bitcast.9, bf16[512,512]{1,0:T(8,128)(2,1)S(1)} %query.1.q_ref, f32[4,512]{1,0:T(4,128)S(1)} %copy-done.4, f32[3,4,256,256]{3,2,1,0:T(8,128)S(1)} %local_bias.1.bias, bf16[2,512,1536]{2,1,0:T(8,128)(2,1)S(1)} %copy-done, ...), custom_call_target="tpu_custom_call" | custom-call | flops 8000000000 | bytes 12000000 | tf_op jit(solution)/shard_map/local_layer/pallas_call | solution.py:252
  34.9 12.4 %all-to-all-start = ((bf16[128,16,128]{2,1,0:T(8,128)(2,1)}), bf16[128,16,128]{2,1,0:T(8,128)(2,1)}, u32[]{:S(2)}, u32[]{:S(2)}) async-start(bf16[128,16,128]{2,1,0:T(8,128)(2,1)} %local_layer.1), calls=%async_computation | async-start | bytes 1048576 | tf_op jit(solution)/shard_map/all_to_all | solution.py:386
  47.4 0.1 reshape.15.table_ref
  47.5 1.8 %group_bias.1.bias_far = f32[5,4,128,128]{3,2,1,0:T(8,128)} custom-call(f32[16,256]{1,0:T(8,128)S(1)} %reshape.15.table_ref), custom_call_target="tpu_custom_call" | custom-call | flops 4000000 | bytes 1300000 | tf_op jit(solution)/shard_map/group_bias/pallas_call | solution.py:172
  49.3 11.8 %all-to-all-done.in_ref = bf16[128,16,128]{2,1,0:T(8,128)(2,1)} async-done(((bf16[128,16,128]{2,1,0:T(8,128)(2,1)}), bf16[128,16,128]{2,1,0:T(8,128)(2,1)}, u32[]{:S(2)}, u32[]{:S(2)}) %all-to-all-start) | async-done | bytes 524320 | tf_op jit(solution)/shard_map/all_to_all | solution.py:386
  61.1 1.3 %copy-done.3 = f32[5,4,128,128]{3,2,1,0:T(8,128)S(1)} copy-done((f32[5,4,128,128]{3,2,1,0:T(8,128)S(1)}, f32[5,4,128,128]{3,2,1,0:T(8,128)}, u32[]{:S(2)}) %copy-start.3) | copy-done | bytes 1310744
  62.4 10.5 %group_layer.1 = bf16[128,16,128]{2,1,0:T(8,128)(2,1)S(1)} custom-call(bf16[128,16,128]{2,1,0:T(8,128)(2,1)} %all-to-all-done.in_ref, f32[4,512]{1,0:T(4,128)S(1)} %copy-done.4, f32[5,4,128,128]{3,2,1,0:T(8,128)S(1)} %copy-done.3, bf16[2,512,1536]{2,1,0:T(8,128)(2,1)S(1)} %copy-done, bf16[2,512,512]{2,1,0:T(8,128)(2,1)} %wp_far.3, ...), custom_call_target="tpu_custom_call" | custom-call | flops 7000000000 | bytes 10000000 | tf_op jit(solution)/shard_map/group_layer/pallas_call | solution.py:333
  72.9 17.5 %all_to_all.10.in_ref = bf16[128,16,128]{2,1,0:T(8,128)(2,1)S(1)} all-to-all(bf16[128,16,128]{2,1,0:T(8,128)(2,1)S(1)} %group_layer.1), channel_id=1, replica_groups=mesh['row'=8,'col'=16] {'row','col'}, dimensions={0} | all-to-all | bytes 1048576 | tf_op jit(solution)/shard_map/all_to_all | solution.py:386
  90.5 1.2 %place.1 = bf16[32,16,512]{2,1,0:T(8,128)(2,1)} custom-call(bf16[128,16,128]{2,1,0:T(8,128)(2,1)S(1)} %all_to_all.10.in_ref), custom_call_target="tpu_custom_call" | custom-call | tf_op jit(solution)/shard_map/place/pallas_call | solution.py:363
  (22 shorter events, 0.2 us)
Async XLA Ops:
  0.0 8.0 %copy-start.1 = (bf16[32,16,512]{2,1,0:T(8,128)(2,1)S(1)}, bf16[32,16,512]{2,1,0:T(8,128)(2,1)}, u32[]{:S(2)}) copy-start(bf16[32,16,512]{2,1,0:T(8,128)(2,1)} %param.7) | copy-start | bytes 1572868
  0.9 7.1 %collective-permute-start = (bf16[3,16,512]{2,1,0:T(8,128)(2,1)S(1)}, bf16[3,16,512]{2,1,0:T(8,128)(2,1)S(1)}, u32[]{:S(2)}, u32[]{:S(2)}) collective-permute-start(bf16[3,16,512]{2,1,0:T(8,128)(2,1)S(1)} %get-tuple-element.8), channel_id=1, source_target_pairs={{0,16},{16,32},{32,48},{48,64},{64,80},{80,96},{96,112},{1,17},{17... | collective-permute-start | bytes 147464 | tf_op jit(solution)/shard_map/ppermute | solution.py:380
  5.3 5.0 %collective-permute-start.1 = (bf16[3,16,512]{2,1,0:T(8,128)(2,1)S(1)}, bf16[3,16,512]{2,1,0:T(8,128)(2,1)S(1)}, u32[]{:S(2)}, u32[]{:S(2)}) collective-permute-start(bf16[3,16,512]{2,1,0:T(8,128)(2,1)S(1)} %get-tuple-element.7), channel_id=1, source_target_pairs={{16,0},{32,16},{48,32},{64,48},{80,64},{96,80},{112,96},{17,1},{33... | collective-permute-start | bytes 147464 | tf_op jit(solution)/shard_map/ppermute | solution.py:381
  10.3 8.5 %copy-start = (bf16[2,512,1536]{2,1,0:T(8,128)(2,1)S(1)}, bf16[2,512,1536]{2,1,0:T(8,128)(2,1)}, u32[]{:S(2)}) copy-start(bf16[2,512,1536]{2,1,0:T(8,128)(2,1)} %wqkv.3) | copy-start | bytes 9437188
  10.3 8.5 %copy-start.2 = (bf16[32,16,512]{2,1,0:T(8,128)(2,1)S(1)}, bf16[32,16,512]{2,1,0:T(8,128)(2,1)}, u32[]{:S(2)}) copy-start(bf16[32,16,512]{2,1,0:T(8,128)(2,1)} %param.7) | copy-start | bytes 1572868
  10.3 8.5 %copy-start.4 = (f32[4,512]{1,0:T(4,128)S(1)}, f32[4,512]{1,0:T(4,128)}, u32[]{:S(2)}) copy-start(f32[4,512]{1,0:T(4,128)} %gains_ref.5) | copy-start | bytes 24580
  10.4 9.1 %collective-permute-start.2 = (bf16[38,3,512]{2,1,0:T(4,128)(2,1)S(1)}, bf16[38,3,512]{2,1,0:T(4,128)(2,1)S(1)}, u32[]{:S(2)}, u32[]{:S(2)}) collective-permute-start(bf16[38,3,512]{2,1,0:T(4,128)(2,1)S(1)} %get-tuple-element.5), channel_id=1, source_target_pairs={{0,1},{1,2},{2,3},{3,4},{4,5},{5,6},{6,7},{7,8},{8,9},{9,10},{10,1... | collective-permute-start | bytes 350216 | tf_op jit(solution)/shard_map/ppermute | solution.py:380
  15.6 6.5 %collective-permute-start.3 = (bf16[38,3,512]{2,1,0:T(4,128)(2,1)S(1)}, bf16[38,3,512]{2,1,0:T(4,128)(2,1)S(1)}, u32[]{:S(2)}, u32[]{:S(2)}) collective-permute-start(bf16[38,3,512]{2,1,0:T(4,128)(2,1)S(1)} %get-tuple-element.6), channel_id=1, source_target_pairs={{1,0},{2,1},{3,2},{4,3},{5,4},{6,5},{7,6},{8,7},{9,8},{10,9},{11,1... | collective-permute-start | bytes 350216 | tf_op jit(solution)/shard_map/ppermute | solution.py:381
  34.9 26.2 %all-to-all-start = ((bf16[128,16,128]{2,1,0:T(8,128)(2,1)}), bf16[128,16,128]{2,1,0:T(8,128)(2,1)}, u32[]{:S(2)}, u32[]{:S(2)}) async-start(bf16[128,16,128]{2,1,0:T(8,128)(2,1)} %local_layer.1), calls=%async_computation | async-start | bytes 1048576 | tf_op jit(solution)/shard_map/all_to_all | solution.py:386
  61.1 1.3 %copy-start.3 = (f32[5,4,128,128]{3,2,1,0:T(8,128)S(1)}, f32[5,4,128,128]{3,2,1,0:T(8,128)}, u32[]{:S(2)}) copy-start(f32[5,4,128,128]{3,2,1,0:T(8,128)} %group_bias.1.bias_far) | copy-start | bytes 3932164

commit v5 on v3

--- a/solution.py
+++ b/solution.py
@@ -19,7 +19,7 @@
 BIG = 24 * 1024 * 1024
 SMALL = 12 * 1024 * 1024
 VM = pl.BlockSpec(memory_space=pltpu.VMEM)
-FAR = pl.BlockSpec(memory_space=pl.ANY)
+FAR = pl.BlockSpec(memory_space=pltpu.HBM)
 
 
 def iota(shape, dim):
@@ -77,9 +77,9 @@
     mixed = (dot(attended, wp[...]) + stream.astype(F32)).astype(BF16)
     normed = layer_norm(mixed, gain)
     acc = mixed.astype(F32)
-    for c in range(4):
-        hidden = gelu(dot(normed, wu[:, c * 512 : (c + 1) * 512])).astype(BF16)
-        acc = acc + dot(hidden, wd[c * 512 : (c + 1) * 512, :])
+    for c in range(2):
+        hidden = gelu(dot(normed, wu[:, c * 1024 : (c + 1) * 1024])).astype(BF16)
+        acc = acc + dot(hidden, wd[c * 1024 : (c + 1) * 1024, :])
     return acc
 
 
@@ -241,10 +241,8 @@
         attend(b, 0)
     for c in copies:
         c.wait()
-    for half in range(2):
-        rows = slice(half * 256, (half + 1) * 256)
-        done = finish_rows(a_s[rows, :], x_ref[rows, :], gains_ref[1:2, :], wp, wu, wd)
-        send_rows(done, stage, [((2 * r + g) * 16, r, g * 2 + half) for r in range(8) for g in range(2)])
+    done = finish_rows(a_s[...], x_ref[...], gains_ref[1:2, :], wp, wu, wd)
+    send_rows(done, stage, [(i * 16, i % 16 // 2, i % 2 * 2 + i // 16) for i in range(32)])
     out_ref[...] = stage[...].reshape(128, 16, 128).astype(BF16)
 
 
@@ -318,10 +316,8 @@
         attend(b, 0)
     for c in copies:
         c.wait()
-    for g in range(2):
-        rows = slice(g * 256, (g + 1) * 256)
-        done = finish_rows(a_s[rows, :], x_s[rows, :], gains_ref[3:4, :], wp, wu, wd)
-        send_rows(done, stage, [(p * 16, p // 2, g * 2 + p % 2) for p in range(16)])
+    done = finish_rows(a_s[...], x_s[...], gains_ref[3:4, :], wp, wu, wd)
+    send_rows(done, stage, [(i * 16, i % 16 // 2, i // 16 * 2 + i % 2) for i in range(32)])
     out_ref[...] = stage[...].reshape(128, 16, 128).astype(BF16)
 
 
@@ -396,14 +392,16 @@
     place = jnp.stack([lax.axis_index("row") * TR, lax.axis_index("col") * TC]).astype(jnp.int32)
 
     near = lambda a: pltpu.with_memory_space_constraint(a, pltpu.VMEM)
-    wqkv, wp, wu, wd = near(qkv_weight), proj_weight, up_weight, down_weight
+    far = lambda a: pltpu.with_memory_space_constraint(a, pltpu.HBM)
+    wqkv, wp, wu, wd = near(qkv_weight), far(proj_weight), far(up_weight), far(down_weight)
     x = near(x)
     q = query_call(x, norm_gains, wqkv)
     local_bias = local_bias_call(place, local_table)
     group_bias = group_bias_call(group_table)
+    xpad, group_bias = lax.optimization_barrier((xpad, group_bias))
     sent = local_call(near(xpad), x, q, norm_gains, local_bias, wqkv, wp, wu, wd)
     got = exchange(sent)
-    back = group_call(near(got), norm_gains, group_bias, wqkv, wp, wu, wd)
+    back = group_call(near(got), norm_gains, near(group_bias), wqkv, wp, wu, wd)
     return place_call(near(exchange(back)))
 
 

time: 98.1 us -> 88.6 us (0.903)
  blocking collectives: 17.5 us -> 47.6 us
  waiting for transfers between devices: 16.6 us -> 2.65 us
  starting transfers between devices: 25.2 us -> 12.5 us
  local copies, waits for them, and re-layouts: 13.6 us -> 2.59 us
  Pallas kernels: 23.7 us -> 22 us
    all_to_all x1 -> x2, blocking collectives: 17.5 us -> 47.6 us  [exchange(): return lax.all_to_all(rows, ('row', 'col'), 0, 0, tiled=True)]
    all_to_all x1 -> x0, starting transfers between devices: 12.4 us -> none  [exchange(): return lax.all_to_all(rows, ('row', 'col'), 0, 0, tiled=True)]
    all_to_all x1 -> x0, waiting for transfers between devices: 11.8 us -> none  [exchange(): return lax.all_to_all(rows, ('row', 'col'), 0, 0, tiled=True)]
    unnamed x31 -> x11, local copies, waits for them, and re-layouts: 12.2 us -> 1.28 us
    pallas_call x1, Pallas kernels: 10.6 us -> 8.06 us  [group_call(): pl.pallas_call(group_kernel, in_specs=[VM] * 4 + [FAR] * 3, out_specs=VM,...]
    ppermute x2, waiting for transfers between devices: 4.81 us -> 2.64 us  [edges(): after = lax.ppermute(head, axis, [(i + 1, i) for i in range(ends)])]
  transfers between devices with their start and end apart: 5 -> 4, of which waited for: 3 -> 1; matrix products, arithmetic and copies ran while one was open for 2% -> 2% of each run, Pallas kernels for 3% -> 3%
where the time goes in v5:
time: 88.6 us; the launch traced here: 88.3 us
  blocking collectives  47.6 us (54%)
  Pallas kernels  22 us (25%)
  starting transfers between devices  12.5 us (14%)
  waiting for transfers between devices  2.65 us (3%)
  local copies, waits for them, and re-layouts  2.59 us (3%)
    all_to_all x2, blocking collectives, exchange(): return lax.all_to_all(rows, ('row', 'col'), 0, 0, tiled=True)  47.6 us
    pallas_call x1, Pallas kernels, local_call(): pl.pallas_call(local_kernel, in_specs=[VM] * 6 + [FAR] * 3, out_specs=VM,...  10.2 us
    ppermute x2, starting transfers between devices, edges(): before = lax.ppermute(tail, axis, [(i, i + 1) for i in range(ends)])  9.32 us
    pallas_call x1, Pallas kernels, group_call(): pl.pallas_call(group_kernel, in_specs=[VM] * 4 + [FAR] * 3, out_specs=VM,...  8.06 us
    ppermute x2, starting transfers between devices, edges(): after = lax.ppermute(head, axis, [(i + 1, i) for i in range(ends)])  3.2 us
    ppermute x2, waiting for transfers between devices, edges(): after = lax.ppermute(head, axis, [(i + 1, i) for i in range(ends)])  2.64 us
  transfers between devices with their start and end apart: 4, of which 1 were waited for; matrix products, arithmetic and copies ran while one was open for 2% of the time, Pallas kernels for 3%

profile of v5, /device:TPU:1, one launch (start us, length us, event | category | flops | bytes accessed | tf_op | source)
XLA Modules:
  0.0 88.3 jit_solution(3466125684670348253)
XLA Ops:
  0.0 0.8 fusion.1
  0.8 1.3 %collective-permute-start.1 = (bf16[3,16,512]{2,1,0:T(8,128)(2,1)S(1)}, bf16[3,16,512]{2,1,0:T(8,128)(2,1)S(1)}, u32[]{:S(2)}, u32[]{:S(2)}) collective-permute-start(bf16[3,16,512]{2,1,0:T(8,128)(2,1)S(1)} %get-tuple-element.11), channel_id=1, source_target_pairs={{16,0},{32,16},{48,32},{64,48},{80,64},{96,80},{112,96},{17,1},{33... | collective-permute-start | bytes 147464 | tf_op jit(solution)/shard_map/ppermute | solution.py:372
  2.1 5.0 %collective-permute-start = (bf16[3,16,512]{2,1,0:T(8,128)(2,1)S(1)}, bf16[3,16,512]{2,1,0:T(8,128)(2,1)S(1)}, u32[]{:S(2)}, u32[]{:S(2)}) collective-permute-start(bf16[3,16,512]{2,1,0:T(8,128)(2,1)S(1)} %get-tuple-element.12), channel_id=1, source_target_pairs={{0,16},{16,32},{32,48},{48,64},{64,80},{80,96},{96,112},{1,17},{17... | collective-permute-start | bytes 147464 | tf_op jit(solution)/shard_map/ppermute | solution.py:371
  7.1 1.1 %copy.10 = f32[2,16,13,13]{3,1,2,0:T(8,128)S(1)} copy(f32[2,16,13,13]{1,0,3,2:T(2,128)} %param.10) | data formatting | bytes 43264 | tf_op args[3]
  8.4 0.1 reshape.15
  8.6 0.1 reshape.13.table_ref
  8.7 0.1 pad.20.clone
  8.8 0.7 group_bias.1.bias
  9.6 0.0 collective-permute-done.1
  9.6 0.0 copy-start
  9.6 0.0 copy-start.2
  9.6 0.1 fusion
  9.8 4.3 %collective-permute-start.2 = (bf16[38,3,512]{2,1,0:T(4,128)(2,1)S(1)}, bf16[38,3,512]{2,1,0:T(4,128)(2,1)S(1)}, u32[]{:S(2)}, u32[]{:S(2)}) collective-permute-start(bf16[38,3,512]{2,1,0:T(4,128)(2,1)S(1)} %get-tuple-element.9), channel_id=1, source_target_pairs={{0,1},{1,2},{2,3},{3,4},{4,5},{5,6},{6,7},{7,8},{8,9},{9,10},{10,1... | collective-permute-start | bytes 350216 | tf_op jit(solution)/shard_map/ppermute | solution.py:371
  14.1 1.9 %collective-permute-start.3 = (bf16[38,3,512]{2,1,0:T(4,128)(2,1)S(1)}, bf16[38,3,512]{2,1,0:T(4,128)(2,1)S(1)}, u32[]{:S(2)}, u32[]{:S(2)}) collective-permute-start(bf16[38,3,512]{2,1,0:T(4,128)(2,1)S(1)} %get-tuple-element.10), channel_id=1, source_target_pairs={{1,0},{2,1},{3,2},{4,3},{5,4},{6,5},{7,6},{8,7},{9,8},{10,9},{11,1... | collective-permute-start | bytes 350216 | tf_op jit(solution)/shard_map/ppermute | solution.py:372
  16.0 0.1 pad_add_fusion.place_ref
  16.1 1.1 %local_bias.1.bias = f32[3,4,256,256]{3,2,1,0:T(8,128)S(1)} custom-call(s32[2]{0:T(128)S(1)} %pad_add_fusion.place_ref, f32[16,512]{1,0:T(8,128)S(1)} %pad.14.table_ref), custom_call_target="tpu_custom_call" | custom-call | flops 4000000 | bytes 3145728 | tf_op jit(solution)/shard_map/local_bias/pallas_call | solution.py:139
  17.3 0.7 query.1.q_ref
  18.0 2.6 %collective-permute-done.3 = bf16[38,3,512]{2,1,0:T(4,128)(2,1)S(1)} collective-permute-done((bf16[38,3,512]{2,1,0:T(4,128)(2,1)S(1)}, bf16[38,3,512]{2,1,0:T(4,128)(2,1)S(1)}, u32[]{:S(2)}, u32[]{:S(2)}) %collective-permute-start.3) | collective-permute-done | bytes 116768 | tf_op jit(solution)/shard_map/ppermute | solution.py:372
  20.6 0.6 maximum_maximum_fusion
  21.3 10.2 %local_layer.1 = bf16[128,16,128]{2,1,0:T(8,128)(2,1)S(1)} custom-call(bf16[912,512]{1,0:T(8,128)(2,1)S(1)} %bitcast.10, bf16[512,512]{1,0:T(8,128)(2,1)S(1)} %bitcast.9, bf16[512,512]{1,0:T(8,128)(2,1)S(1)} %query.1.q_ref, f32[4,512]{1,0:T(4,128)S(1)} %copy-done.2, f32[3,4,256,256]{3,2,1,0:T(8,128)S(1)} %local_bias.1.bias, ...), custom_call_target="tpu_custom_call" | custom-call | flops 8000000000 | bytes 12000000 | tf_op jit(solution)/shard_map/local_layer/pallas_call | solution.py:250
  31.4 30.1 %all_to_all.10.in_ref = bf16[128,16,128]{2,1,0:T(8,128)(2,1)S(1)} all-to-all(bf16[128,16,128]{2,1,0:T(8,128)(2,1)S(1)} %local_layer.1), channel_id=1, replica_groups=mesh['row'=8,'col'=16] {'row','col'}, dimensions={0} | all-to-all | bytes 1048576 | tf_op jit(solution)/shard_map/all_to_all | solution.py:377
  61.5 8.1 %group_layer.1 = bf16[128,16,128]{2,1,0:T(8,128)(2,1)S(1)} custom-call(bf16[128,16,128]{2,1,0:T(8,128)(2,1)S(1)} %all_to_all.10.in_ref, f32[4,512]{1,0:T(4,128)S(1)} %copy-done.2, f32[5,4,128,128]{3,2,1,0:T(8,128)S(1)} %group_bias.1.bias, bf16[2,512,1536]{2,1,0:T(8,128)(2,1)S(1)} %copy-done, bf16[2,512,512]{2,1,0:T(8,128)(2,1)} %wp_far.3, ...), custom_call_target="tpu_custom_call" | custom-call | flops 7000000000 | bytes 10000000 | tf_op jit(solution)/shard_map/group_layer/pallas_call | solution.py:325
  69.6 17.5 %all_to_all.11.in_ref = bf16[128,16,128]{2,1,0:T(8,128)(2,1)S(1)} all-to-all(bf16[128,16,128]{2,1,0:T(8,128)(2,1)S(1)} %group_layer.1), channel_id=1, replica_groups=mesh['row'=8,'col'=16] {'row','col'}, dimensions={0} | all-to-all | bytes 1048576 | tf_op jit(solution)/shard_map/all_to_all | solution.py:377
  87.2 1.2 %place.1 = bf16[32,16,512]{2,1,0:T(8,128)(2,1)} custom-call(bf16[128,16,128]{2,1,0:T(8,128)(2,1)S(1)} %all_to_all.11.in_ref), custom_call_target="tpu_custom_call" | custom-call | tf_op jit(solution)/shard_map/place/pallas_call | solution.py:354
  (17 shorter events, 0.2 us)
Async XLA Ops:
  0.8 8.8 %collective-permute-start.1 = (bf16[3,16,512]{2,1,0:T(8,128)(2,1)S(1)}, bf16[3,16,512]{2,1,0:T(8,128)(2,1)S(1)}, u32[]{:S(2)}, u32[]{:S(2)}) collective-permute-start(bf16[3,16,512]{2,1,0:T(8,128)(2,1)S(1)} %get-tuple-element.11), channel_id=1, source_target_pairs={{16,0},{32,16},{48,32},{64,48},{80,64},{96,80},{112,96},{17,1},{33... | collective-permute-start | bytes 147464 | tf_op jit(solution)/shard_map/ppermute | solution.py:372
  2.1 7.4 %collective-permute-start = (bf16[3,16,512]{2,1,0:T(8,128)(2,1)S(1)}, bf16[3,16,512]{2,1,0:T(8,128)(2,1)S(1)}, u32[]{:S(2)}, u32[]{:S(2)}) collective-permute-start(bf16[3,16,512]{2,1,0:T(8,128)(2,1)S(1)} %get-tuple-element.12), channel_id=1, source_target_pairs={{0,16},{16,32},{32,48},{48,64},{64,80},{80,96},{96,112},{1,17},{17... | collective-permute-start | bytes 147464 | tf_op jit(solution)/shard_map/ppermute | solution.py:371
  8.3 1.3 %copy-start.1 = (bf16[32,16,512]{2,1,0:T(8,128)(2,1)S(1)}, bf16[32,16,512]{2,1,0:T(8,128)(2,1)}, u32[]{:S(2)}) copy-start(bf16[32,16,512]{2,1,0:T(8,128)(2,1)} %param.7) | copy-start | bytes 1572868
  9.6 7.6 %copy-start = (bf16[2,512,1536]{2,1,0:T(8,128)(2,1)S(1)}, bf16[2,512,1536]{2,1,0:T(8,128)(2,1)}, u32[]{:S(2)}) copy-start(bf16[2,512,1536]{2,1,0:T(8,128)(2,1)} %wqkv.3) | copy-start | bytes 9437188
  9.6 7.6 %copy-start.2 = (f32[4,512]{1,0:T(4,128)S(1)}, f32[4,512]{1,0:T(4,128)}, u32[]{:S(2)}) copy-start(f32[4,512]{1,0:T(4,128)} %gains_ref.5) | copy-start | bytes 24580
  9.8 8.2 %collective-permute-start.2 = (bf16[38,3,512]{2,1,0:T(4,128)(2,1)S(1)}, bf16[38,3,512]{2,1,0:T(4,128)(2,1)S(1)}, u32[]{:S(2)}, u32[]{:S(2)}) collective-permute-start(bf16[38,3,512]{2,1,0:T(4,128)(2,1)S(1)} %get-tuple-element.9), channel_id=1, source_target_pairs={{0,1},{1,2},{2,3},{3,4},{4,5},{5,6},{6,7},{7,8},{8,9},{9,10},{10,1... | collective-permute-start | bytes 350216 | tf_op jit(solution)/shard_map/ppermute | solution.py:371
  14.1 6.5 %collective-permute-start.3 = (bf16[38,3,512]{2,1,0:T(4,128)(2,1)S(1)}, bf16[38,3,512]{2,1,0:T(4,128)(2,1)S(1)}, u32[]{:S(2)}, u32[]{:S(2)}) collective-permute-start(bf16[38,3,512]{2,1,0:T(4,128)(2,1)S(1)} %get-tuple-element.10), channel_id=1, source_target_pairs={{1,0},{2,1},{3,2},{4,3},{5,4},{6,5},{7,6},{8,7},{9,8},{10,9},{11,1... | collective-permute-start | bytes 350216 | tf_op jit(solution)/shard_map/ppermute | solution.py:372

commit v6 on v5

--- a/solution.py
+++ b/solution.py
@@ -364,12 +364,11 @@
 
 def edges(cells, axis, dim):
     count = lax.axis_size(axis)
-    ends = count - 1
     size = cells.shape[dim]
     head = lax.slice_in_dim(cells, 0, 3, axis=dim)
     tail = lax.slice_in_dim(cells, size - 3, size, axis=dim)
-    before = lax.ppermute(tail, axis, [(i, i + 1) for i in range(ends)])
-    after = lax.ppermute(head, axis, [(i + 1, i) for i in range(ends)])
+    before = lax.ppermute(tail, axis, [(i, (i + 1) % count) for i in range(count)])
+    after = lax.ppermute(head, axis, [((i + 1) % count, i) for i in range(count)])
     return before, after
 
 
@@ -379,10 +378,10 @@
 
 def body(tokens, norm_gains, qkv_weight, rel_bias, proj_weight, up_weight, down_weight):
     x = tokens.reshape(TR * TC, D)
-    top, bottom = edges(tokens, "row", 0)
-    tall = jnp.concatenate([top, tokens, bottom], axis=0)
-    left, right = edges(tall, "col", 1)
-    xpad = jnp.concatenate([left, tall, right, jnp.zeros((TR + 6, 2, D), BF16)], axis=1)
+    left, right = edges(tokens, "col", 1)
+    wide = jnp.concatenate([left, tokens, right, jnp.zeros((TR, 2, D), BF16)], axis=1)
+    top, bottom = edges(wide, "row", 0)
+    xpad = jnp.concatenate([top, wide, bottom], axis=0)
     xpad = xpad.reshape((TR + 6) * 24, D)
 
     table = rel_bias * LOG2E

time: 88.6 us -> 78.7 us (0.89)
  blocking collectives: 47.6 us -> 39.5 us
  starting transfers between devices: 12.5 us -> 9.21 us
    all_to_all x2, blocking collectives: 47.6 us -> 39.5 us  [exchange(): return lax.all_to_all(rows, ('row', 'col'), 0, 0, tiled=True)]
    ppermute x4, starting transfers between devices: 12.5 us -> 9.21 us  [the longest x2 4.83 us: edges(): lax.ppermute(head, axis, [((i + 1) % count, i) for i in range(count)])]
    slice x1, local copies, waits for them, and re-layouts: 0.13 us -> 1.19 us  [edges(): tail = lax.slice_in_dim(cells, size - 3, size, axis=dim)]
    unnamed x11 -> x9, local copies, waits for them, and re-layouts: 1.28 us -> 1.96 us
  transfers between devices with their start and end apart: 4 -> 4, of which waited for: 1 -> 2; matrix products, arithmetic and copies ran while one was open for 2% -> 2% of each run, Pallas kernels for 3% -> 3%
where the time goes in v6:
time: 78.7 us; the launch traced here: 78.5 us
  blocking collectives  39.5 us (50%)
  Pallas kernels  22 us (28%)
  starting transfers between devices  9.21 us (12%)
  waiting for transfers between devices  3.5 us (4%)
  local copies, waits for them, and re-layouts  3.45 us (4%)
    all_to_all x2, blocking collectives, exchange(): return lax.all_to_all(rows, ('row', 'col'), 0, 0, tiled=True)  39.5 us
    pallas_call x1, Pallas kernels, local_call(): pl.pallas_call(local_kernel, in_specs=[VM] * 6 + [FAR] * 3, out_specs=VM,...  10.2 us
    pallas_call x1, Pallas kernels, group_call(): pl.pallas_call(group_kernel, in_specs=[VM] * 4 + [FAR] * 3, out_specs=VM,...  8.06 us
    ppermute x2, starting transfers between devices, edges(): lax.ppermute(head, axis, [((i + 1) % count, i) for i in range(count)])  4.83 us
    ppermute x2, starting transfers between devices, edges(): lax.ppermute(tail, axis, [(i, (i + 1) % count) for i in range(count)])  4.38 us
    ppermute x2, waiting for transfers between devices, edges(): lax.ppermute(head, axis, [((i + 1) % count, i) for i in range(count)])  2.74 us
    unnamed x9, local copies, waits for them, and re-layouts  1.96 us
  transfers between devices with their start and end apart: 4, of which 2 were waited for; matrix products, arithmetic and copies ran while one was open for 2% of the time, Pallas kernels for 3%

profile of v6, /device:TPU:1, one launch (start us, length us, event | category | flops | bytes accessed | tf_op | source)
XLA Modules:
  0.0 78.5 jit_solution(14812623361418174214)
XLA Ops:
  0.0 1.2 %fusion = (bf16[32,3,512]{2,1,0:T(4,128)(2,1)S(1)}, bf16[32,3,512]{2,1,0:T(4,128)(2,1)S(1)}) fusion(bf16[32,16,512]{2,1,0:T(8,128)(2,1)} %param.7), kind=kLoop, calls=%fused_computation.9 | loop fusion | bytes 393216 | tf_op jit(solution)/shard_map/slice | solution.py:369
  1.2 2.7 %collective-permute-start = (bf16[32,3,512]{2,1,0:T(4,128)(2,1)S(1)}, bf16[32,3,512]{2,1,0:T(4,128)(2,1)S(1)}, u32[]{:S(2)}, u32[]{:S(2)}) collective-permute-start(bf16[32,3,512]{2,1,0:T(4,128)(2,1)S(1)} %get-tuple-element.11), channel_id=1, source_target_pairs={{0,1},{1,2},{2,3},{3,4},{4,5},{5,6},{6,7},{7,8},{8,9},{9,10},{10,1... | collective-permute-start | bytes 294920 | tf_op jit(solution)/shard_map/ppermute | solution.py:370
  3.9 1.1 %copy.10 = f32[2,16,13,13]{3,1,2,0:T(8,128)S(1)} copy(f32[2,16,13,13]{1,0,3,2:T(2,128)} %param.10) | data formatting | bytes 43264 | tf_op args[3]
  5.1 0.8 collective-permute-done
  5.8 2.7 %collective-permute-done.1 = bf16[32,3,512]{2,1,0:T(4,128)(2,1)S(1)} collective-permute-done((bf16[32,3,512]{2,1,0:T(4,128)(2,1)S(1)}, bf16[32,3,512]{2,1,0:T(4,128)(2,1)S(1)}, u32[]{:S(2)}, u32[]{:S(2)}) %collective-permute-start.1) | collective-permute-done | bytes 98336 | tf_op jit(solution)/shard_map/ppermute | solution.py:371
  8.6 0.1 pad_maximum_fusion.4
  8.7 1.7 %collective-permute-start.2 = (bf16[3,24,512]{2,1,0:T(8,128)(2,1)S(1)}, bf16[3,24,512]{2,1,0:T(8,128)(2,1)S(1)}, u32[]{:S(2)}, u32[]{:S(2)}) collective-permute-start(bf16[3,24,512]{2,1,0:T(8,128)(2,1)S(1)} %get-tuple-element.9), channel_id=1, source_target_pairs={{0,16},{16,32},{32,48},{48,64},{64,80},{80,96},{96,112},{112,0},{1... | collective-permute-start | bytes 221192 | tf_op jit(solution)/shard_map/ppermute | solution.py:370
  10.4 4.8 %collective-permute-start.3 = (bf16[3,24,512]{2,1,0:T(8,128)(2,1)S(1)}, bf16[3,24,512]{2,1,0:T(8,128)(2,1)S(1)}, u32[]{:S(2)}, u32[]{:S(2)}) collective-permute-start(bf16[3,24,512]{2,1,0:T(8,128)(2,1)S(1)} %get-tuple-element.10), channel_id=1, source_target_pairs={{16,0},{32,16},{48,32},{64,48},{80,64},{96,80},{112,96},{0,112},{1... | collective-permute-start | bytes 221192 | tf_op jit(solution)/shard_map/ppermute | solution.py:371
  15.2 0.1 pad_add_fusion.place_ref
  15.4 0.1 reshape.15
  15.6 0.1 reshape.13.table_ref
  15.7 0.7 group_bias.1.bias
  16.4 0.0 copy-start.1
  16.4 0.0 copy-start.2
  16.4 1.1 %local_bias.1.bias = f32[3,4,256,256]{3,2,1,0:T(8,128)S(1)} custom-call(s32[2]{0:T(128)S(1)} %pad_add_fusion.place_ref, f32[16,512]{1,0:T(8,128)S(1)} %pad.14.table_ref), custom_call_target="tpu_custom_call" | custom-call | flops 4000000 | bytes 3145728 | tf_op jit(solution)/shard_map/local_bias/pallas_call | solution.py:139
  17.6 0.7 copy-done.1
  18.3 0.7 query.1.q_ref
  19.0 0.0 collective-permute-done.2
  19.0 0.5 pad_maximum_fusion
  19.6 10.2 %local_layer.1 = bf16[128,16,128]{2,1,0:T(8,128)(2,1)S(1)} custom-call(bf16[912,512]{1,0:T(8,128)(2,1)S(1)} %bitcast.10, bf16[512,512]{1,0:T(8,128)(2,1)S(1)} %bitcast.9, bf16[512,512]{1,0:T(8,128)(2,1)S(1)} %query.1.q_ref, f32[4,512]{1,0:T(4,128)S(1)} %copy-done.2, f32[3,4,256,256]{3,2,1,0:T(8,128)S(1)} %local_bias.1.bias, ...), custom_call_target="tpu_custom_call" | custom-call | flops 8000000000 | bytes 12000000 | tf_op jit(solution)/shard_map/local_layer/pallas_call | solution.py:250
  29.7 22.0 %all_to_all.10.in_ref = bf16[128,16,128]{2,1,0:T(8,128)(2,1)S(1)} all-to-all(bf16[128,16,128]{2,1,0:T(8,128)(2,1)S(1)} %local_layer.1), channel_id=1, replica_groups=mesh['row'=8,'col'=16] {'row','col'}, dimensions={0} | all-to-all | bytes 1048576 | tf_op jit(solution)/shard_map/all_to_all | solution.py:376
  51.8 8.1 %group_layer.1 = bf16[128,16,128]{2,1,0:T(8,128)(2,1)S(1)} custom-call(bf16[128,16,128]{2,1,0:T(8,128)(2,1)S(1)} %all_to_all.10.in_ref, f32[4,512]{1,0:T(4,128)S(1)} %copy-done.2, f32[5,4,128,128]{3,2,1,0:T(8,128)S(1)} %group_bias.1.bias, bf16[2,512,1536]{2,1,0:T(8,128)(2,1)S(1)} %copy-done.1, bf16[2,512,512]{2,1,0:T(8,128)(2,1)} %wp_far.3, ...), custom_call_target="tpu_custom_call" | custom-call | flops 7000000000 | bytes 10000000 | tf_op jit(solution)/shard_map/group_layer/pallas_call | solution.py:325
  59.8 17.5 %all_to_all.11.in_ref = bf16[128,16,128]{2,1,0:T(8,128)(2,1)S(1)} all-to-all(bf16[128,16,128]{2,1,0:T(8,128)(2,1)S(1)} %group_layer.1), channel_id=1, replica_groups=mesh['row'=8,'col'=16] {'row','col'}, dimensions={0} | all-to-all | bytes 1048576 | tf_op jit(solution)/shard_map/all_to_all | solution.py:376
  77.4 1.2 %place.1 = bf16[32,16,512]{2,1,0:T(8,128)(2,1)} custom-call(bf16[128,16,128]{2,1,0:T(8,128)(2,1)S(1)} %all_to_all.11.in_ref), custom_call_target="tpu_custom_call" | custom-call | tf_op jit(solution)/shard_map/place/pallas_call | solution.py:354
  (13 shorter events, 0.2 us)
Async XLA Ops:
  0.0 8.6 %copy-start = (bf16[32,16,512]{2,1,0:T(8,128)(2,1)S(1)}, bf16[32,16,512]{2,1,0:T(8,128)(2,1)}, u32[]{:S(2)}) copy-start(bf16[32,16,512]{2,1,0:T(8,128)(2,1)} %param.7) | copy-start | bytes 1572868
  1.2 4.6 %collective-permute-start = (bf16[32,3,512]{2,1,0:T(4,128)(2,1)S(1)}, bf16[32,3,512]{2,1,0:T(4,128)(2,1)S(1)}, u32[]{:S(2)}, u32[]{:S(2)}) collective-permute-start(bf16[32,3,512]{2,1,0:T(4,128)(2,1)S(1)} %get-tuple-element.11), channel_id=1, source_target_pairs={{0,1},{1,2},{2,3},{3,4},{4,5},{5,6},{6,7},{7,8},{8,9},{9,10},{10,1... | collective-permute-start | bytes 294920 | tf_op jit(solution)/shard_map/ppermute | solution.py:370
  3.9 4.7 %collective-permute-start.1 = (bf16[32,3,512]{2,1,0:T(4,128)(2,1)S(1)}, bf16[32,3,512]{2,1,0:T(4,128)(2,1)S(1)}, u32[]{:S(2)}, u32[]{:S(2)}) collective-permute-start(bf16[32,3,512]{2,1,0:T(4,128)(2,1)S(1)} %get-tuple-element.12), channel_id=1, source_target_pairs={{1,0},{2,1},{3,2},{4,3},{5,4},{6,5},{7,6},{8,7},{9,8},{10,9},{11,1... | collective-permute-start | bytes 294920 | tf_op jit(solution)/shard_map/ppermute | solution.py:371
  8.7 10.3 %collective-permute-start.2 = (bf16[3,24,512]{2,1,0:T(8,128)(2,1)S(1)}, bf16[3,24,512]{2,1,0:T(8,128)(2,1)S(1)}, u32[]{:S(2)}, u32[]{:S(2)}) collective-permute-start(bf16[3,24,512]{2,1,0:T(8,128)(2,1)S(1)} %get-tuple-element.9), channel_id=1, source_target_pairs={{0,16},{16,32},{32,48},{48,64},{64,80},{80,96},{96,112},{112,0},{1... | collective-permute-start | bytes 221192 | tf_op jit(solution)/shard_map/ppermute | solution.py:370
  10.4 8.6 %collective-permute-start.3 = (bf16[3,24,512]{2,1,0:T(8,128)(2,1)S(1)}, bf16[3,24,512]{2,1,0:T(8,128)(2,1)S(1)}, u32[]{:S(2)}, u32[]{:S(2)}) collective-permute-start(bf16[3,24,512]{2,1,0:T(8,128)(2,1)S(1)} %get-tuple-element.10), channel_id=1, source_target_pairs={{16,0},{32,16},{48,32},{64,48},{80,64},{96,80},{112,96},{0,112},{1... | collective-permute-start | bytes 221192 | tf_op jit(solution)/shard_map/ppermute | solution.py:371
  16.4 1.9 %copy-start.1 = (bf16[2,512,1536]{2,1,0:T(8,128)(2,1)S(1)}, bf16[2,512,1536]{2,1,0:T(8,128)(2,1)}, u32[]{:S(2)}) copy-start(bf16[2,512,1536]{2,1,0:T(8,128)(2,1)} %wqkv.3) | copy-start | bytes 9437188
  16.4 1.9 %copy-start.2 = (f32[4,512]{1,0:T(4,128)S(1)}, f32[4,512]{1,0:T(4,128)}, u32[]{:S(2)}) copy-start(f32[4,512]{1,0:T(4,128)} %gains_ref.5) | copy-start | bytes 24580

commit v7 on v6

--- a/solution.py
+++ b/solution.py
@@ -201,68 +201,121 @@
             stage[pl.ds(block * 256 + slot * 4 + f, 16, stride=16), :] = done[at : at + 16, f * 128 : (f + 1) * 128]
 
 
-def local_kernel(
-    xpad_ref, x_ref, q_ref, gains_ref, bias, wqkv, wp_far, wu_far, wd_far, out_ref,
-    k_s, v_s, a_s, stage, wp, wu, wd, sems,
+def put_values(v_s, rows, value):
+    for g in range(4):
+        v_s[rows, g * 256 : g * 256 + 128] = value[:, g * 128 : (g + 1) * 128]
+
+
+def block_units(q, k, v, bias):
+    return [
+        (
+            q[:, g * 128 : (g + 1) * 128],
+            k[:, g * 128 : (g + 1) * 128],
+            v[:, g * 256 : (g + 1) * 256],
+            bias[g],
+        )
+        for g in range(4)
+    ]
+
+
+def inner_kernel(
+    wide_ref, q_ref, gains_ref, bias, wqkv, wp_far, wu_far, wd_far,
+    a_ref, k_s, v_s, wp, wu, wd, sems,
 ):
     copies = fetch_weights(0, (wp_far, wu_far, wd_far), (wp, wu, wd), sems)
-    k_s[912:928, :] = jnp.zeros((16, 512), BF16)
     v_s[...] = jnp.ones((928, 1024), BF16)
-    for g in range(4):
-        v_s[912:928, g * 256 : g * 256 + 128] = jnp.zeros((16, 128), BF16)
-    for r in range(3):
-        rows = slice(r * 304, (r + 1) * 304)
-        normed = layer_norm(xpad_ref[rows, :], gains_ref[0:1, :])
+    for r in range(2):
+        rows = slice(64 + r * 400, 64 + min((r + 1) * 400, 784))
+        normed = layer_norm(wide_ref[r * 400 : min((r + 1) * 400, 784), :], gains_ref[0:1, :])
         k_s[rows, :] = dot(normed, wqkv[0, :, 512:1024]).astype(BF16)
-        value = dot(normed, wqkv[0, :, 1024:]).astype(BF16)
+        put_values(v_s, rows, dot(normed, wqkv[0, :, 1024:]).astype(BF16))
+    for b in range(1, 7):
+        keys = slice(96 * b, 96 * b + 256)
+        rows = slice(64 * b, 64 * b + 64)
+        outs = attend_units(block_units(q_ref[rows, :], k_s[keys, :], v_s[keys, :], bias[1]))
         for g in range(4):
-            v_s[rows, g * 256 : g * 256 + 128] = value[:, g * 128 : (g + 1) * 128]
-
-    def attend(b, carry):
-        at_q = b * 64
-        at_k = b * 96
-        kind = 0 if b == 0 else 2 if b == 7 else 1
-        outs = attend_units(
-            [
-                (
-                    q_ref[pl.ds(at_q, 64), g * 128 : (g + 1) * 128],
-                    k_s[pl.ds(at_k, 256), g * 128 : (g + 1) * 128],
-                    v_s[pl.ds(at_k, 256), g * 256 : (g + 1) * 256],
-                    bias[kind, g],
-                )
-                for g in range(4)
-            ]
-        )
-        for g in range(4):
-            a_s[pl.ds(at_q, 64), g * 128 : (g + 1) * 128] = outs[g]
-        return carry
-
-    for b in range(8):
-        attend(b, 0)
+            a_ref[rows, g * 128 : (g + 1) * 128] = outs[g]
+    a_ref[0:64, :] = jnp.zeros((64, 512), BF16)
+    a_ref[448:512, :] = jnp.zeros((64, 512), BF16)
     for c in copies:
         c.wait()
-    done = finish_rows(a_s[...], x_ref[...], gains_ref[1:2, :], wp, wu, wd)
+
+
+def inner_call(wide, q, gains, bias, wqkv, wp, wu, wd):
+    return pl.pallas_call(
+        inner_kernel,
+        in_specs=[VM] * 5 + [FAR] * 3,
+        out_specs=[VM] * 6,
+        out_shape=[
+            pltpu.VMEM((512, 512), BF16),
+            pltpu.VMEM((928, 512), BF16),
+            pltpu.VMEM((928, 1024), BF16),
+            pltpu.VMEM((512, 512), BF16),
+            pltpu.VMEM((512, 2048), BF16),
+            pltpu.VMEM((2048, 512), BF16),
+        ],
+        scratch_shapes=[pltpu.SemaphoreType.DMA((3,))],
+        compiler_params=pltpu.CompilerParams(vmem_limit_bytes=BIG),
+        cost_estimate=pl.CostEstimate(flops=4_000_000_000, transcendentals=2_000_000, bytes_accessed=8_000_000),
+        name="inner_blocks",
+    )(wide, q, gains, bias, wqkv, wp, wu, wd)
+
+
+def local_kernel(
+    edge_ref, x_ref, q_ref, gains_ref, bias, wqkv, a_ref, k_s, v_s, wp, wu, wd, out_ref, k_e, v_e, stage
+):
+    normed = layer_norm(edge_ref[...], gains_ref[0:1, :])
+    gap = jnp.zeros((8, 512), F32)
+    v_e[...] = jnp.ones((512, 1024), BF16)
+    for lane, is_key in ((512, True), (1024, False)):
+        fresh = dot(normed, wqkv[0, :, lane : lane + 512])
+        if is_key:
+            own = lambda a, b: k_s[a:b, :]
+        else:
+            own = lambda a, b: jnp.concatenate([v_s[a:b, g * 256 : g * 256 + 128] for g in range(4)], axis=1)
+        above = (jnp.concatenate([fresh[64:72], gap], axis=0) + own(64, 80).astype(F32)).astype(BF16)
+        below = (jnp.concatenate([gap, fresh[72:80]], axis=0) + own(832, 848).astype(F32)).astype(BF16)
+        pieces = [
+            (0, fresh[:64].astype(BF16)),
+            (64, above),
+            (80, own(80, 256)),
+            (256, own(672, 832)),
+            (416, below),
+            (432, fresh[80:144].astype(BF16)),
+            (496, jnp.zeros((16, 512), BF16)),
+        ]
+        for at, piece in pieces:
+            rows = slice(at, at + piece.shape[0])
+            if is_key:
+                k_e[rows, :] = piece
+            else:
+                put_values(v_e, rows, piece)
+    units = block_units(q_ref[0:64, :], k_e[:256, :], v_e[:256, :], bias[0])
+    units += block_units(q_ref[448:512, :], k_e[256:, :], v_e[256:, :], bias[2])
+    outs = attend_units(units)
+    attended = jnp.concatenate(
+        [jnp.concatenate(outs[:4], axis=1), a_ref[64:448, :], jnp.concatenate(outs[4:], axis=1)], axis=0
+    )
+    done = finish_rows(attended, x_ref[...], gains_ref[1:2, :], wp, wu, wd)
     send_rows(done, stage, [(i * 16, i % 16 // 2, i % 2 * 2 + i // 16) for i in range(32)])
     out_ref[...] = stage[...].reshape(128, 16, 128).astype(BF16)
 
 
-def local_call(xpad, x, q, gains, bias, wqkv, wp, wu, wd):
+def local_call(edge, x, q, gains, bias, wqkv, inner):
     return pl.pallas_call(
         local_kernel,
-        in_specs=[VM] * 6 + [FAR] * 3,
+        in_specs=[VM] * 12,
         out_specs=VM,
         out_shape=pltpu.VMEM((128, 16, 128), BF16),
         scratch_shapes=[
-            pltpu.VMEM((928, 512), BF16),
-            pltpu.VMEM((928, 1024), BF16),
-            pltpu.VMEM((512, 512), BF16),
+            pltpu.VMEM((512, 512), BF16),
+            pltpu.VMEM((512, 1024), BF16),
             pltpu.VMEM((2048, 128), F32),
-        ]
-        + WEIGHT_SCRATCH,
+        ],
         compiler_params=pltpu.CompilerParams(vmem_limit_bytes=BIG),
-        cost_estimate=pl.CostEstimate(flops=8_000_000_000, transcendentals=3_000_000, bytes_accessed=12_000_000),
+        cost_estimate=pl.CostEstimate(flops=4_000_000_000, transcendentals=2_000_000, bytes_accessed=8_000_000),
         name="local_layer",
-    )(xpad, x, q, gains, bias, wqkv, wp, wu, wd)
+    )(edge, x, q, gains, bias, wqkv, *inner)
 
 
 def group_kernel(
@@ -378,12 +431,6 @@
 
 def body(tokens, norm_gains, qkv_weight, rel_bias, proj_weight, up_weight, down_weight):
     x = tokens.reshape(TR * TC, D)
-    left, right = edges(tokens, "col", 1)
-    wide = jnp.concatenate([left, tokens, right, jnp.zeros((TR, 2, D), BF16)], axis=1)
-    top, bottom = edges(wide, "row", 0)
-    xpad = jnp.concatenate([top, wide, bottom], axis=0)
-    xpad = xpad.reshape((TR + 6) * 24, D)
-
     table = rel_bias * LOG2E
     local_table = jnp.pad(table[0], ((0, 0), (0, 0), (0, 11))).reshape(HEADS, 312)
     local_table = jnp.pad(local_table, ((0, 0), (0, 200)))
@@ -397,8 +444,14 @@
     q = query_call(x, norm_gains, wqkv)
     local_bias = local_bias_call(place, local_table)
     group_bias = group_bias_call(group_table)
-    xpad, group_bias = lax.optimization_barrier((xpad, group_bias))
-    sent = local_call(near(xpad), x, q, norm_gains, local_bias, wqkv, wp, wu, wd)
+    left, right = edges(tokens, "col", 1)
+    left, right, q, local_bias, group_bias = lax.optimization_barrier((left, right, q, local_bias, group_bias))
+    wide = jnp.concatenate([left, tokens, right, jnp.zeros((TR, 2, D), BF16)], axis=1)
+    top, bottom = edges(wide, "row", 0)
+    padded = jnp.pad(wide.reshape(TR * 24, D), ((8, 8), (0, 0)))
+    edge = jnp.concatenate([top.reshape(72, D), bottom.reshape(72, D)], axis=0)
+    inner = inner_call(near(padded), near(q), norm_gains, near(local_bias), wqkv, wp, wu, wd)
+    sent = local_call(near(edge), x, near(q), norm_gains, near(local_bias), wqkv, inner)
     got = exchange(sent)
     back = group_call(near(got), norm_gains, near(group_bias), wqkv, wp, wu, wd)
     return place_call(near(exchange(back)))

time: 78.7 us -> 73.9 us (0.939)
  waiting for transfers between devices: 3.5 us -> 0.01 us
  Pallas kernels: 22 us -> 20.1 us
    ppermute x2, waiting for transfers between devices: 2.74 us -> 0.01 us  [edges(): lax.ppermute(head, axis, [((i + 1) % count, i) for i in range(count)])]
    pallas_call x1 -> x2, Pallas kernels: 10.2 us -> 8.27 us  [the longest x1 4.56 us: local_call(): pl.pallas_call(local_kernel, in_specs=[VM] * 12, out_specs=VM, out_shape=...]
    ppermute x2, starting transfers between devices: 4.83 us -> 6.33 us  [edges(): lax.ppermute(head, axis, [((i + 1) % count, i) for i in range(count)])]
    ppermute x2, starting transfers between devices: 4.38 us -> 2.96 us  [edges(): lax.ppermute(tail, axis, [(i, (i + 1) % count) for i in range(count)])]
    slice x1, local copies, waits for them, and re-layouts: 1.19 us -> 0.01 us  [edges(): tail = lax.slice_in_dim(cells, size - 3, size, axis=dim)]
    slice x0 -> x1, local copies, waits for them, and re-layouts: none -> 1.13 us  [edges(): head = lax.slice_in_dim(cells, 0, 3, axis=dim)]
  transfers between devices with their start and end apart: 4 -> 4, of which waited for: 2 -> 0; matrix products, arithmetic and copies ran while one was open for 2% -> 2% of each run, Pallas kernels for 3% -> 9%
where the time goes in v7:
time: 73.9 us; the launch traced here: 73.7 us
  blocking collectives  40 us (54%)
  Pallas kernels  20.1 us (27%)
  starting transfers between devices  9.29 us (13%)
  local copies, waits for them, and re-layouts  3.55 us (5%)
    all_to_all x2, blocking collectives, exchange(): return lax.all_to_all(rows, ('row', 'col'), 0, 0, tiled=True)  40 us
    pallas_call x1, Pallas kernels, group_call(): pl.pallas_call(group_kernel, in_specs=[VM] * 4 + [FAR] * 3, out_specs=VM,...  8.08 us
    ppermute x2, starting transfers between devices, edges(): lax.ppermute(head, axis, [((i + 1) % count, i) for i in range(count)])  6.33 us
    pallas_call x1, Pallas kernels, local_call(): pl.pallas_call(local_kernel, in_specs=[VM] * 12, out_specs=VM, out_shape=...  4.56 us
    pallas_call x1, Pallas kernels, inner_call(): pl.pallas_call(inner_kernel, in_specs=[VM] * 5 + [FAR] * 3, out_specs=[VM...  3.72 us
    ppermute x2, starting transfers between devices, edges(): lax.ppermute(tail, axis, [(i, (i + 1) % count) for i in range(count)])  2.96 us
    unnamed x9, local copies, waits for them, and re-layouts  2 us
  transfers between devices with their start and end apart: 4, of which 0 were waited for; matrix products, arithmetic and copies ran while one was open for 2% of the time, Pallas kernels for 9%

profile of v7, /device:TPU:1, one launch (start us, length us, event | category | flops | bytes accessed | tf_op | source)
XLA Modules:
  0.0 73.7 jit_solution(16407699783965901473)
XLA Ops:
  0.0 1.1 %fusion.1 = (bf16[32,3,512]{2,1,0:T(4,128)(2,1)S(1)}, bf16[32,3,512]{2,1,0:T(4,128)(2,1)S(1)}) fusion(bf16[32,16,512]{2,1,0:T(8,128)(2,1)} %param.7), kind=kLoop, calls=%fused_computation.7 | loop fusion | bytes 393216 | tf_op jit(solution)/shard_map/slice | solution.py:421
  1.1 1.5 %collective-permute-start.1 = (bf16[32,3,512]{2,1,0:T(4,128)(2,1)S(1)}, bf16[32,3,512]{2,1,0:T(4,128)(2,1)S(1)}, u32[]{:S(2)}, u32[]{:S(2)}) collective-permute-start(bf16[32,3,512]{2,1,0:T(4,128)(2,1)S(1)} %get-tuple-element.29), channel_id=1, source_target_pairs={{1,0},{2,1},{3,2},{4,3},{5,4},{6,5},{7,6},{8,7},{9,8},{10,9},{11,1... | collective-permute-start | bytes 294920 | tf_op jit(solution)/shard_map/ppermute | solution.py:424
  2.6 1.3 %collective-permute-start = (bf16[32,3,512]{2,1,0:T(4,128)(2,1)S(1)}, bf16[32,3,512]{2,1,0:T(4,128)(2,1)S(1)}, u32[]{:S(2)}, u32[]{:S(2)}) collective-permute-start(bf16[32,3,512]{2,1,0:T(4,128)(2,1)S(1)} %get-tuple-element.30), channel_id=1, source_target_pairs={{0,1},{1,2},{2,3},{3,4},{4,5},{5,6},{6,7},{7,8},{8,9},{9,10},{10,1... | collective-permute-start | bytes 294920 | tf_op jit(solution)/shard_map/ppermute | solution.py:423
  3.9 1.1 %copy.10 = f32[2,16,13,13]{3,1,2,0:T(8,128)S(1)} copy(f32[2,16,13,13]{1,0,3,2:T(2,128)} %param.10) | data formatting | bytes 43264 | tf_op args[3]
  5.2 0.1 reshape.20.table_ref
  5.3 0.1 reshape.19
  5.4 0.0 copy-start.1
  5.5 0.7 group_bias.1.bias
  6.2 0.1 pad.25.clone
  6.3 0.1 pad_add_fusion.place_ref
  6.3 1.1 %local_bias.1.bias = f32[3,4,256,256]{3,2,1,0:T(8,128)S(1)} custom-call(s32[2]{0:T(128)S(1)} %pad_add_fusion.place_ref, f32[16,512]{1,0:T(8,128)S(1)} %pad.17.table_ref), custom_call_target="tpu_custom_call" | custom-call | flops 4000000 | bytes 3145728 | tf_op jit(solution)/shard_map/local_bias/pallas_call | solution.py:139
  7.5 0.8 %copy-done = bf16[2,512,1536]{2,1,0:T(8,128)(2,1)S(1)} copy-done((bf16[2,512,1536]{2,1,0:T(8,128)(2,1)S(1)}, bf16[2,512,1536]{2,1,0:T(8,128)(2,1)}, u32[]{:S(2)}) %copy-start) | copy-done | bytes 3145752
  8.3 0.7 query.1.q_ref
  9.0 0.0 collective-permute-done.1
  9.0 0.5 maximum_maximum_fusion
  9.6 1.7 %collective-permute-start.2 = (bf16[3,24,512]{2,1,0:T(8,128)(2,1)S(1)}, bf16[3,24,512]{2,1,0:T(8,128)(2,1)S(1)}, u32[]{:S(2)}, u32[]{:S(2)}) collective-permute-start(bf16[3,24,512]{2,1,0:T(8,128)(2,1)S(1)} %get-tuple-element.27), channel_id=1, source_target_pairs={{0,16},{16,32},{32,48},{48,64},{64,80},{80,96},{96,112},{112,0},{1... | collective-permute-start | bytes 221192 | tf_op jit(solution)/shard_map/ppermute | solution.py:423
  11.3 4.8 %collective-permute-start.3 = (bf16[3,24,512]{2,1,0:T(8,128)(2,1)S(1)}, bf16[3,24,512]{2,1,0:T(8,128)(2,1)S(1)}, u32[]{:S(2)}, u32[]{:S(2)}) collective-permute-start(bf16[3,24,512]{2,1,0:T(8,128)(2,1)S(1)} %get-tuple-element.28), channel_id=1, source_target_pairs={{16,0},{32,16},{48,32},{64,48},{80,64},{96,80},{112,96},{0,112},{1... | collective-permute-start | bytes 221192 | tf_op jit(solution)/shard_map/ppermute | solution.py:424
  16.1 0.1 pad.19.wide_ref
  16.1 3.7 %inner_blocks.1 = (bf16[512,512]{1,0:T(8,128)(2,1)S(1)}, bf16[928,512]{1,0:T(8,128)(2,1)S(1)}, bf16[928,1024]{1,0:T(8,128)(2,1)S(1)}, bf16[512,512]{1,0:T(8,128)...) custom-call(bf16[784,512]{1,0:T(8,128)(2,1)S(1)} %pad.19.wide_ref, ...), custom_call_target="tpu_custom_call" | custom-call | flops 4000000000 | bytes 8000000 | tf_op jit(solution)/shard_map/inner_blocks/pallas_call | solution.py:245
  19.9 4.6 %local_layer.1 = bf16[128,16,128]{2,1,0:T(8,128)(2,1)S(1)} custom-call(bf16[144,512]{1,0:T(8,128)(2,1)S(1)} %pad_maximum_fusion.edge_ref, bf16[512,512]{1,0:T(8,128)(2,1)S(1)} %bitcast.11, bf16[512,512]{1,0:T(8,128)(2,1)S(1)} %query.1.q_ref, f32[4,512]{1,0:T(4,128)S(1)} %copy-done.2, f32[3,4,256,256]{3,2,1,0:T(8,128)S(1)} %local_bias.1.bias, ...), custom_call_target="tpu_custom_call" | custom-call | flops 4000000000 | bytes 8000000 | tf_op jit(solution)/shard_map/local_layer/pallas_call | solution.py:305
  24.5 22.4 %all_to_all.10.in_ref = bf16[128,16,128]{2,1,0:T(8,128)(2,1)S(1)} all-to-all(bf16[128,16,128]{2,1,0:T(8,128)(2,1)S(1)} %local_layer.1), channel_id=1, replica_groups=mesh['row'=8,'col'=16] {'row','col'}, dimensions={0} | all-to-all | bytes 1048576 | tf_op jit(solution)/shard_map/all_to_all | solution.py:429
  46.9 8.1 %group_layer.1 = bf16[128,16,128]{2,1,0:T(8,128)(2,1)S(1)} custom-call(bf16[128,16,128]{2,1,0:T(8,128)(2,1)S(1)} %all_to_all.10.in_ref, f32[4,512]{1,0:T(4,128)S(1)} %copy-done.2, f32[5,4,128,128]{3,2,1,0:T(8,128)S(1)} %group_bias.1.bias, bf16[2,512,1536]{2,1,0:T(8,128)(2,1)S(1)} %copy-done, bf16[2,512,512]{2,1,0:T(8,128)(2,1)} %wp_far.3, ...), custom_call_target="tpu_custom_call" | custom-call | flops 7000000000 | bytes 10000000 | tf_op jit(solution)/shard_map/group_layer/pallas_call | solution.py:378
  55.0 17.5 %all_to_all.11.in_ref = bf16[128,16,128]{2,1,0:T(8,128)(2,1)S(1)} all-to-all(bf16[128,16,128]{2,1,0:T(8,128)(2,1)S(1)} %group_layer.1), channel_id=1, replica_groups=mesh['row'=8,'col'=16] {'row','col'}, dimensions={0} | all-to-all | bytes 1048576 | tf_op jit(solution)/shard_map/all_to_all | solution.py:429
  72.5 1.2 %place.1 = bf16[32,16,512]{2,1,0:T(8,128)(2,1)} custom-call(bf16[128,16,128]{2,1,0:T(8,128)(2,1)S(1)} %all_to_all.11.in_ref), custom_call_target="tpu_custom_call" | custom-call | tf_op jit(solution)/shard_map/place/pallas_call | solution.py:407
  (17 shorter events, 0.2 us)
Async XLA Ops:
  1.1 7.9 %collective-permute-start.1 = (bf16[32,3,512]{2,1,0:T(4,128)(2,1)S(1)}, bf16[32,3,512]{2,1,0:T(4,128)(2,1)S(1)}, u32[]{:S(2)}, u32[]{:S(2)}) collective-permute-start(bf16[32,3,512]{2,1,0:T(4,128)(2,1)S(1)} %get-tuple-element.29), channel_id=1, source_target_pairs={{1,0},{2,1},{3,2},{4,3},{5,4},{6,5},{7,6},{8,7},{9,8},{10,9},{11,1... | collective-permute-start | bytes 294920 | tf_op jit(solution)/shard_map/ppermute | solution.py:424
  2.6 6.4 %collective-permute-start = (bf16[32,3,512]{2,1,0:T(4,128)(2,1)S(1)}, bf16[32,3,512]{2,1,0:T(4,128)(2,1)S(1)}, u32[]{:S(2)}, u32[]{:S(2)}) collective-permute-start(bf16[32,3,512]{2,1,0:T(4,128)(2,1)S(1)} %get-tuple-element.30), channel_id=1, source_target_pairs={{0,1},{1,2},{2,3},{3,4},{4,5},{5,6},{6,7},{7,8},{8,9},{9,10},{10,1... | collective-permute-start | bytes 294920 | tf_op jit(solution)/shard_map/ppermute | solution.py:423
  5.4 2.0 %copy-start.1 = (bf16[32,16,512]{2,1,0:T(8,128)(2,1)S(1)}, bf16[32,16,512]{2,1,0:T(8,128)(2,1)}, u32[]{:S(2)}) copy-start(bf16[32,16,512]{2,1,0:T(8,128)(2,1)} %param.7) | copy-start | bytes 1572868
  6.3 1.9 %copy-start = (bf16[2,512,1536]{2,1,0:T(8,128)(2,1)S(1)}, bf16[2,512,1536]{2,1,0:T(8,128)(2,1)}, u32[]{:S(2)}) copy-start(bf16[2,512,1536]{2,1,0:T(8,128)(2,1)} %wqkv.5) | copy-start | bytes 9437188
  6.3 1.9 %copy-start.2 = (f32[4,512]{1,0:T(4,128)S(1)}, f32[4,512]{1,0:T(4,128)}, u32[]{:S(2)}) copy-start(f32[4,512]{1,0:T(4,128)} %gains_ref.7) | copy-start | bytes 24580
  9.6 10.3 %collective-permute-start.2 = (bf16[3,24,512]{2,1,0:T(8,128)(2,1)S(1)}, bf16[3,24,512]{2,1,0:T(8,128)(2,1)S(1)}, u32[]{:S(2)}, u32[]{:S(2)}) collective-permute-start(bf16[3,24,512]{2,1,0:T(8,128)(2,1)S(1)} %get-tuple-element.27), channel_id=1, source_target_pairs={{0,16},{16,32},{32,48},{48,64},{64,80},{80,96},{96,112},{112,0},{1... | collective-permute-start | bytes 221192 | tf_op jit(solution)/shard_map/ppermute | solution.py:423
  11.3 8.6 %collective-permute-start.3 = (bf16[3,24,512]{2,1,0:T(8,128)(2,1)S(1)}, bf16[3,24,512]{2,1,0:T(8,128)(2,1)S(1)}, u32[]{:S(2)}, u32[]{:S(2)}) collective-permute-start(bf16[3,24,512]{2,1,0:T(8,128)(2,1)S(1)} %get-tuple-element.28), channel_id=1, source_target_pairs={{16,0},{32,16},{48,32},{64,48},{80,64},{96,80},{112,96},{0,112},{1... | collective-permute-start | bytes 221192 | tf_op jit(solution)/shard_map/ppermute | solution.py:424

commit v8 on v7

--- a/solution.py
+++ b/solution.py
@@ -87,7 +87,7 @@
     for half in range(2):
         rows = slice(half * 256, (half + 1) * 256)
         normed = layer_norm(x_ref[rows, :], gains_ref[0:1, :])
-        q_ref[rows, :] = (dot(normed, w_ref[0, :, :512]) * QSCALE).astype(BF16)
+        q_ref[rows, :] = (dot(normed, w_ref[:, :512]) * QSCALE).astype(BF16)
 
 
 def query_call(x, gains, wqkv):
@@ -107,7 +107,27 @@
     return pltpu.roll(base, 0, 1, stride=1, stride_axis=0)
 
 
-def local_bias_kernel(place_ref, table_ref, bias_ref):
+def flatten_table(table_ref, pad, layer, width, stride, offset):
+    flat = jnp.zeros((HEADS, width), F32)
+    rest = jnp.zeros((HEADS, width - 128), F32)
+    for y in range(13):
+        pad[y, :, 0:13] = table_ref[layer, y] * LOG2E
+        row = jnp.concatenate([pad[y], rest], axis=1)
+        at = stride * y + offset
+        flat = flat + (pltpu.roll(row, at, 1) if at else row)
+    return flat
+
+
+def bias_kernel(place_ref, table_ref, w_far, local_ref, group_ref, w_near, pad, sem):
+    fetch = pltpu.make_async_copy(w_far.at[0], w_near, sem)
+    fetch.start()
+    pad[...] = jnp.zeros((13, HEADS, 128), F32)
+    local_bias(place_ref, flatten_table(table_ref, pad, 0, 512, 24, 0), local_ref)
+    group_bias(flatten_table(table_ref, pad, 1, 256, 16, 16), group_ref)
+    fetch.wait()
+
+
+def local_bias(place_ref, flat, bias_ref):
     first_row = place_ref[0]
     first_col = place_ref[1]
     row = iota((64, 256), 0)
@@ -126,7 +146,7 @@
         row_a = jnp.clip(row_q - 3, 0, MAP - 7)
         row_k = first_row + 4 * block - 3 + kr
         oks.append(col_ok & (row_k >= row_a) & (row_k <= row_a + 6))
-    rolled = [pltpu.roll(table_ref[...], 512 - (24 * (3 - i) + 3), 1) for i in range(4)]
+    rolled = [pltpu.roll(flat, 512 - (24 * (3 - i) + 3), 1) for i in range(4)]
     for n in range(HEADS):
         parts = [spread(rolled[i], n)[:, :256] for i in range(4)]
         full = jnp.concatenate(parts, axis=0)
@@ -135,19 +155,7 @@
             bias_ref[c, n // 4, at : at + 64, :] = jnp.where(oks[c], full, NEG)
 
 
-def local_bias_call(place, table):
-    return pl.pallas_call(
-        local_bias_kernel,
-        in_specs=[pl.BlockSpec(memory_space=pltpu.SMEM), VM],
-        out_specs=VM,
-        out_shape=pltpu.VMEM((3, 4, 256, 256), F32),
-        compiler_params=pltpu.CompilerParams(vmem_limit_bytes=SMALL),
-        cost_estimate=pl.CostEstimate(flops=4_000_000, transcendentals=0, bytes_accessed=3 * 1024 * 1024),
-        name="local_bias",
-    )(place, table)
-
-
-def group_bias_kernel(table_ref, bias_ref):
+def group_bias(flat, bias_ref):
     row = iota((32, 128), 0)
     lane = iota((32, 128), 1)
     qi = row // 16
@@ -157,7 +165,7 @@
     col_a = jnp.clip(qj - 3, 0, 9)
     col_ok = (kc >= col_a) & (kc <= col_a + 6)
     classes = ((0, 0), (1, 0), (2, 1), (6, 8), (7, 8))
-    rolled = [pltpu.roll(table_ref[...], 256 - (step * 16 + 6), 1) for step in range(8)]
+    rolled = [pltpu.roll(flat, 256 - (step * 16 + 6), 1) for step in range(8)]
     for n in range(HEADS):
         at = (n % 4) * 32
         for c, (block, start) in enumerate(classes):
@@ -168,16 +176,21 @@
             bias_ref[c, n // 4, at : at + 32, :] = jnp.where(ok, jnp.concatenate(parts, axis=0), NEG)
 
 
-def group_bias_call(table):
-    return pl.pallas_call(
-        group_bias_kernel,
-        in_specs=[VM],
-        out_specs=VM,
-        out_shape=pltpu.VMEM((5, 4, 128, 128), F32),
+def bias_call(place, table, wqkv):
+    return pl.pallas_call(
+        bias_kernel,
+        in_specs=[pl.BlockSpec(memory_space=pltpu.SMEM), VM, FAR],
+        out_specs=[VM] * 3,
+        out_shape=[
+            pltpu.VMEM((3, 4, 256, 256), F32),
+            pltpu.VMEM((5, 4, 128, 128), F32),
+            pltpu.VMEM((512, 1536), BF16),
+        ],
+        scratch_shapes=[pltpu.VMEM((13, HEADS, 128), F32), pltpu.SemaphoreType.DMA(())],
         compiler_params=pltpu.CompilerParams(vmem_limit_bytes=SMALL),
-        cost_estimate=pl.CostEstimate(flops=4_000_000, transcendentals=0, bytes_accessed=1_300_000),
-        name="group_bias",
-    )(table)
+        cost_estimate=pl.CostEstimate(flops=8_000_000, transcendentals=0, bytes_accessed=5 * 1024 * 1024),
+        name="biases",
+    )(place, table, wqkv)
 
 
 def fetch_weights(layer, far, near, sems):
@@ -227,8 +240,8 @@
     for r in range(2):
         rows = slice(64 + r * 400, 64 + min((r + 1) * 400, 784))
         normed = layer_norm(wide_ref[r * 400 : min((r + 1) * 400, 784), :], gains_ref[0:1, :])
-        k_s[rows, :] = dot(normed, wqkv[0, :, 512:1024]).astype(BF16)
-        put_values(v_s, rows, dot(normed, wqkv[0, :, 1024:]).astype(BF16))
+        k_s[rows, :] = dot(normed, wqkv[:, 512:1024]).astype(BF16)
+        put_values(v_s, rows, dot(normed, wqkv[:, 1024:]).astype(BF16))
     for b in range(1, 7):
         keys = slice(96 * b, 96 * b + 256)
         rows = slice(64 * b, 64 * b + 64)
@@ -262,13 +275,16 @@
 
 
 def local_kernel(
-    edge_ref, x_ref, q_ref, gains_ref, bias, wqkv, a_ref, k_s, v_s, wp, wu, wd, out_ref, k_e, v_e, stage
+    edge_ref, x_ref, q_ref, gains_ref, bias, wqkv, w_far, a_ref, k_s, v_s, wp, wu, wd, out_ref, w_next,
+    k_e, v_e, stage, sem,
 ):
+    fetch = pltpu.make_async_copy(w_far.at[1], w_next, sem)
+    fetch.start()
     normed = layer_norm(edge_ref[...], gains_ref[0:1, :])
     gap = jnp.zeros((8, 512), F32)
     v_e[...] = jnp.ones((512, 1024), BF16)
     for lane, is_key in ((512, True), (1024, False)):
-        fresh = dot(normed, wqkv[0, :, lane : lane + 512])
+        fresh = dot(normed, wqkv[:, lane : lane + 512])
         if is_key:
             own = lambda a, b: k_s[a:b, :]
         else:
@@ -299,23 +315,25 @@
     done = finish_rows(attended, x_ref[...], gains_ref[1:2, :], wp, wu, wd)
     send_rows(done, stage, [(i * 16, i % 16 // 2, i % 2 * 2 + i // 16) for i in range(32)])
     out_ref[...] = stage[...].reshape(128, 16, 128).astype(BF16)
-
-
-def local_call(edge, x, q, gains, bias, wqkv, inner):
+    fetch.wait()
+
+
+def local_call(edge, x, q, gains, bias, wqkv, w_far, inner):
     return pl.pallas_call(
         local_kernel,
-        in_specs=[VM] * 12,
-        out_specs=VM,
-        out_shape=pltpu.VMEM((128, 16, 128), BF16),
+        in_specs=[VM] * 6 + [FAR] + [VM] * 6,
+        out_specs=[VM, VM],
+        out_shape=[pltpu.VMEM((128, 16, 128), BF16), pltpu.VMEM((512, 1536), BF16)],
         scratch_shapes=[
             pltpu.VMEM((512, 512), BF16),
             pltpu.VMEM((512, 1024), BF16),
             pltpu.VMEM((2048, 128), F32),
+            pltpu.SemaphoreType.DMA(()),
         ],
         compiler_params=pltpu.CompilerParams(vmem_limit_bytes=BIG),
         cost_estimate=pl.CostEstimate(flops=4_000_000_000, transcendentals=2_000_000, bytes_accessed=8_000_000),
         name="local_layer",
-    )(edge, x, q, gains, bias, wqkv, *inner)
+    )(edge, x, q, gains, bias, wqkv, w_far, *inner)
 
 
 def group_kernel(
@@ -336,37 +354,33 @@
     for g in range(2):
         rows = slice(g * 256, (g + 1) * 256)
         normed = layer_norm(x_s[rows, :], gains_ref[2:3, :])
-        q_s[rows, :] = (dot(normed, wqkv[1, :, :512]) * QSCALE).astype(BF16)
-        k_s[rows, :] = dot(normed, wqkv[1, :, 512:1024]).astype(BF16)
-        value = dot(normed, wqkv[1, :, 1024:]).astype(BF16)
+        q_s[rows, :] = (dot(normed, wqkv[:, :512]) * QSCALE).astype(BF16)
+        k_s[rows, :] = dot(normed, wqkv[:, 512:1024]).astype(BF16)
+        value = dot(normed, wqkv[:, 1024:]).astype(BF16)
         for h in range(4):
             v_s[rows, h * 256 : h * 256 + 128] = value[:, h * 128 : (h + 1) * 128]
 
-    def attend(b, carry):
-        start = min(max(2 * b - 3, 0), 8)
-        kind = b if b < 2 else 2 if b < 6 else b - 3
-        units = []
-        for g in range(2):
-            at_q = g * 256 + b * 32
-            at_k = g * 256 + start * 16
-            for h in range(4):
-                units.append(
-                    (
-                        q_s[pl.ds(at_q, 32), h * 128 : (h + 1) * 128],
-                        k_s[pl.ds(at_k, 128), h * 128 : (h + 1) * 128],
-                        v_s[pl.ds(at_k, 128), h * 256 : (h + 1) * 256],
-                        bias[kind, h],
-                    )
-                )
-        outs = attend_units(units)
-        for g in range(2):
-            at_q = g * 256 + b * 32
-            for h in range(4):
-                a_s[pl.ds(at_q, 32), h * 128 : (h + 1) * 128] = outs[g * 4 + h]
-        return carry
-
-    for b in range(8):
-        attend(b, 0)
+    for b0 in range(0, 8, 2):
+        for gs in ((0, 1),):
+            units, places = [], []
+            for b in range(b0, b0 + 2):
+                start = min(max(2 * b - 3, 0), 8)
+                kind = b if b < 2 else 2 if b < 6 else b - 3
+                for g in gs:
+                    at_q = g * 256 + b * 32
+                    at_k = g * 256 + start * 16
+                    for h in range(4):
+                        units.append(
+                            (
+                                q_s[at_q : at_q + 32, h * 128 : (h + 1) * 128],
+                                k_s[at_k : at_k + 128, h * 128 : (h + 1) * 128],
+                                v_s[at_k : at_k + 128, h * 256 : (h + 1) * 256],
+                                bias[kind, h],
+                            )
+                        )
+                        places.append((at_q, h))
+            for (at_q, h), out in zip(places, attend_units(units)):
+                a_s[at_q : at_q + 32, h * 128 : (h + 1) * 128] = out
     for c in copies:
         c.wait()
     done = finish_rows(a_s[...], x_s[...], gains_ref[3:4, :], wp, wu, wd)
@@ -431,29 +445,25 @@
 
 def body(tokens, norm_gains, qkv_weight, rel_bias, proj_weight, up_weight, down_weight):
     x = tokens.reshape(TR * TC, D)
-    table = rel_bias * LOG2E
-    local_table = jnp.pad(table[0], ((0, 0), (0, 0), (0, 11))).reshape(HEADS, 312)
-    local_table = jnp.pad(local_table, ((0, 0), (0, 200)))
-    group_table = jnp.pad(table[1], ((0, 0), (1, 2), (0, 3))).reshape(HEADS, 256)
     place = jnp.stack([lax.axis_index("row") * TR, lax.axis_index("col") * TC]).astype(jnp.int32)
 
     near = lambda a: pltpu.with_memory_space_constraint(a, pltpu.VMEM)
     far = lambda a: pltpu.with_memory_space_constraint(a, pltpu.HBM)
-    wqkv, wp, wu, wd = near(qkv_weight), far(proj_weight), far(up_weight), far(down_weight)
+    w_far, wp, wu, wd = far(qkv_weight), far(proj_weight), far(up_weight), far(down_weight)
     x = near(x)
-    q = query_call(x, norm_gains, wqkv)
-    local_bias = local_bias_call(place, local_table)
-    group_bias = group_bias_call(group_table)
+    local_bias, group_bias, wqkv = bias_call(place, near(rel_bias.transpose(0, 2, 1, 3)), w_far)
+    q = query_call(x, norm_gains, near(wqkv))
     left, right = edges(tokens, "col", 1)
     left, right, q, local_bias, group_bias = lax.optimization_barrier((left, right, q, local_bias, group_bias))
+    wqkv, local_bias = near(wqkv), near(local_bias)
     wide = jnp.concatenate([left, tokens, right, jnp.zeros((TR, 2, D), BF16)], axis=1)
     top, bottom = edges(wide, "row", 0)
     padded = jnp.pad(wide.reshape(TR * 24, D), ((8, 8), (0, 0)))
     edge = jnp.concatenate([top.reshape(72, D), bottom.reshape(72, D)], axis=0)
-    inner = inner_call(near(padded), near(q), norm_gains, near(local_bias), wqkv, wp, wu, wd)
-    sent = local_call(near(edge), x, near(q), norm_gains, near(local_bias), wqkv, inner)
+    inner = inner_call(near(padded), near(q), norm_gains, local_bias, wqkv, wp, wu, wd)
+    sent, wqkv_next = local_call(near(edge), x, near(q), norm_gains, local_bias, wqkv, w_far, inner)
     got = exchange(sent)
-    back = group_call(near(got), norm_gains, near(group_bias), wqkv, wp, wu, wd)
+    back = group_call(near(got), norm_gains, near(group_bias), near(wqkv_next), wp, wu, wd)
     return place_call(near(exchange(back)))
 
 

time: 73.9 us -> 73.4 us (level)
  local copies, waits for them, and re-layouts: 3.55 us -> 2.42 us
    pallas_call x3 -> x2, Pallas kernels: 6.4 us -> 7.38 us  [the longest x1 4.72 us: local_call(): pl.pallas_call(local_kernel, in_specs=[VM] * 6 + [FAR] + [VM] * 6, out_sp...]
    unnamed x9 -> x5, local copies, waits for them, and re-layouts: 2 us -> 1.15 us
  transfers between devices with their start and end apart: 4 -> 4, of which waited for: 0 -> 0; matrix products, arithmetic and copies ran while one was open for 2% -> 2% of each run, Pallas kernels for 9% -> 10%
where the time goes in v8:
time: 73.4 us; the launch traced here: 73.2 us
  blocking collectives  40.3 us (55%)
  Pallas kernels  20.4 us (28%)
  starting transfers between devices  9.3 us (13%)
  local copies, waits for them, and re-layouts  2.42 us (3%)
    all_to_all x2, blocking collectives, exchange(): return lax.all_to_all(rows, ('row', 'col'), 0, 0, tiled=True)  40.3 us
    pallas_call x1, Pallas kernels, group_call(): pl.pallas_call(group_kernel, in_specs=[VM] * 4 + [FAR] * 3, out_specs=VM,...  7.43 us
    ppermute x2, starting transfers between devices, edges(): lax.ppermute(head, axis, [((i + 1) % count, i) for i in range(count)])  6.33 us
    pallas_call x1, Pallas kernels, local_call(): pl.pallas_call(local_kernel, in_specs=[VM] * 6 + [FAR] + [VM] * 6, out_sp...  4.72 us
    pallas_call x1, Pallas kernels, inner_call(): pl.pallas_call(inner_kernel, in_specs=[VM] * 5 + [FAR] * 3, out_specs=[VM...  3.73 us
    ppermute x2, starting transfers between devices, edges(): lax.ppermute(tail, axis, [(i, (i + 1) % count) for i in range(count)])  2.97 us
    pallas_call x1, Pallas kernels, bias_call(): pl.pallas_call(bias_kernel, in_specs=[pl.BlockSpec(memory_space=pltpu.SME...  2.66 us
  transfers between devices with their start and end apart: 4, of which 0 were waited for; matrix products, arithmetic and copies ran while one was open for 2% of the time, Pallas kernels for 10%

profile of v8, /device:TPU:1, one launch (start us, length us, event | category | flops | bytes accessed | tf_op | source)
XLA Modules:
  0.0 73.2 jit_solution(15792442370478903750)
XLA Ops:
  0.0 1.1 %fusion.1 = (bf16[32,3,512]{2,1,0:T(4,128)(2,1)S(1)}, bf16[32,3,512]{2,1,0:T(4,128)(2,1)S(1)}) fusion(bf16[32,16,512]{2,1,0:T(8,128)(2,1)} %param.7), kind=kLoop, calls=%fused_computation.4 | loop fusion | bytes 393216 | tf_op jit(solution)/shard_map/slice | solution.py:435
  1.1 1.5 %collective-permute-start.1 = (bf16[32,3,512]{2,1,0:T(4,128)(2,1)S(1)}, bf16[32,3,512]{2,1,0:T(4,128)(2,1)S(1)}, u32[]{:S(2)}, u32[]{:S(2)}) collective-permute-start(bf16[32,3,512]{2,1,0:T(4,128)(2,1)S(1)} %get-tuple-element.39), channel_id=1, source_target_pairs={{1,0},{2,1},{3,2},{4,3},{5,4},{6,5},{7,6},{8,7},{9,8},{10,9},{11,1... | collective-permute-start | bytes 294920 | tf_op jit(solution)/shard_map/ppermute | solution.py:438
  2.6 1.3 %collective-permute-start = (bf16[32,3,512]{2,1,0:T(4,128)(2,1)S(1)}, bf16[32,3,512]{2,1,0:T(4,128)(2,1)S(1)}, u32[]{:S(2)}, u32[]{:S(2)}) collective-permute-start(bf16[32,3,512]{2,1,0:T(4,128)(2,1)S(1)} %get-tuple-element.40), channel_id=1, source_target_pairs={{0,1},{1,2},{2,3},{3,4},{4,5},{5,6},{6,7},{7,8},{8,9},{9,10},{10,1... | collective-permute-start | bytes 294920 | tf_op jit(solution)/shard_map/ppermute | solution.py:437
  3.9 1.1 %copy.8 = f32[2,16,13,13]{3,1,2,0:T(8,128)S(1)} copy(f32[2,16,13,13]{1,0,3,2:T(2,128)} %param.10) | data formatting | bytes 43264 | tf_op args[3]
  5.0 0.1 pad.10.clone
  5.1 0.1 pad_add_fusion.place_ref
  5.2 2.7 %biases.1 = (f32[3,4,256,256]{3,2,1,0:T(8,128)S(1)}, f32[5,4,128,128]{3,2,1,0:T(8,128)S(1)}, bf16[512,1536]{1,0:T(8,128)(2,1)S(1)}) custom-call(s32[2]{0:T(128)S(1)} %pad_add_fusion.place_ref, f32[2,13,16,13]{3,2,1,0:T(8,128)S(1)} %bitcast.9, bf16[2,512,1536]{2,1,0:T(8,128)(2,1)} %w_far.3), custom_call_target="tpu_custom_call" | custom-call | flops 8000000 | bytes 5242880 | tf_op jit(solution)/shard_map/biases/pallas_call | solution.py:180
  7.9 0.0 copy-done
  7.9 0.0 copy-done.1
  7.9 0.7 query.1.q_ref
  8.6 0.0 collective-permute-done.1
  8.6 0.0 collective-permute-done
  8.6 0.5 maximum_maximum_fusion
  9.2 1.7 %collective-permute-start.2 = (bf16[3,24,512]{2,1,0:T(8,128)(2,1)S(1)}, bf16[3,24,512]{2,1,0:T(8,128)(2,1)S(1)}, u32[]{:S(2)}, u32[]{:S(2)}) collective-permute-start(bf16[3,24,512]{2,1,0:T(8,128)(2,1)S(1)} %get-tuple-element.37), channel_id=1, source_target_pairs={{0,16},{16,32},{32,48},{48,64},{64,80},{80,96},{96,112},{112,0},{1... | collective-permute-start | bytes 221192 | tf_op jit(solution)/shard_map/ppermute | solution.py:437
  10.9 4.8 %collective-permute-start.3 = (bf16[3,24,512]{2,1,0:T(8,128)(2,1)S(1)}, bf16[3,24,512]{2,1,0:T(8,128)(2,1)S(1)}, u32[]{:S(2)}, u32[]{:S(2)}) collective-permute-start(bf16[3,24,512]{2,1,0:T(8,128)(2,1)S(1)} %get-tuple-element.38), channel_id=1, source_target_pairs={{16,0},{32,16},{48,32},{64,48},{80,64},{96,80},{112,96},{0,112},{1... | collective-permute-start | bytes 221192 | tf_op jit(solution)/shard_map/ppermute | solution.py:438
  15.7 0.1 pad.4.wide_ref
  15.8 3.7 %inner_blocks.1 = (bf16[512,512]{1,0:T(8,128)(2,1)S(1)}, bf16[928,512]{1,0:T(8,128)(2,1)S(1)}, bf16[928,1024]{1,0:T(8,128)(2,1)S(1)}, bf16[512,512]{1,0:T(8,128)...) custom-call(bf16[784,512]{1,0:T(8,128)(2,1)S(1)} %pad.4.wide_ref, ...), custom_call_target="tpu_custom_call" | custom-call | flops 4000000000 | bytes 8000000 | tf_op jit(solution)/shard_map/inner_blocks/pallas_call | solution.py:258
  19.5 0.0 collective-permute-done.2
  19.5 0.0 collective-permute-done.3
  19.5 4.7 %local_layer.1 = (bf16[128,16,128]{2,1,0:T(8,128)(2,1)S(1)}, bf16[512,1536]{1,0:T(8,128)(2,1)S(1)}) custom-call(bf16[144,512]{1,0:T(8,128)(2,1)S(1)} %pad_maximum_fusion.edge_ref, bf16[512,512]{1,0:T(8,128)(2,1)S(1)} %bitcast.8, bf16[512,512]{1,0:T(8,128)(2,1)S(1)} %query.1.q_ref, f32[4,512]{1,0:T(4,128)S(1)} %copy-done.1, ...), custom_call_target="tpu_custom_call" | custom-call | flops 4000000000 | bytes 8000000 | tf_op jit(solution)/shard_map/local_layer/pallas_call | solution.py:322
  24.3 22.8 %all_to_all.10.in_ref = bf16[128,16,128]{2,1,0:T(8,128)(2,1)S(1)} all-to-all(bf16[128,16,128]{2,1,0:T(8,128)(2,1)S(1)} %get-tuple-element.34), channel_id=1, replica_groups=mesh['row'=8,'col'=16] {'row','col'}, dimensions={0} | all-to-all | bytes 1048576 | tf_op jit(solution)/shard_map/all_to_all | solution.py:443
  47.0 7.4 %group_layer.1 = bf16[128,16,128]{2,1,0:T(8,128)(2,1)S(1)} custom-call(bf16[128,16,128]{2,1,0:T(8,128)(2,1)S(1)} %all_to_all.10.in_ref, f32[4,512]{1,0:T(4,128)S(1)} %copy-done.1, f32[5,4,128,128]{3,2,1,0:T(8,128)S(1)} %get-tuple-element.35.bias, bf16[512,1536]{1,0:T(8,128)(2,1)S(1)} %get-tuple-element.36.wqkv, bf16[2,512,512]{2,1,0:T(8,128)(2,1)} %wp_far.3, ...), custom_call_target="tpu_custom_call" | custom-call | flops 7000000000 | bytes 10000000 | tf_op jit(solution)/shard_map/group_layer/pallas_call | solution.py:392
  54.5 17.5 %all_to_all.11.in_ref = bf16[128,16,128]{2,1,0:T(8,128)(2,1)S(1)} all-to-all(bf16[128,16,128]{2,1,0:T(8,128)(2,1)S(1)} %group_layer.1), channel_id=1, replica_groups=mesh['row'=8,'col'=16] {'row','col'}, dimensions={0} | all-to-all | bytes 1048576 | tf_op jit(solution)/shard_map/all_to_all | solution.py:443
  72.0 1.2 %place.1 = bf16[32,16,512]{2,1,0:T(8,128)(2,1)} custom-call(bf16[128,16,128]{2,1,0:T(8,128)(2,1)S(1)} %all_to_all.11.in_ref), custom_call_target="tpu_custom_call" | custom-call | tf_op jit(solution)/shard_map/place/pallas_call | solution.py:421
  (5 shorter events, 0.0 us)
Async XLA Ops:
  1.1 7.5 %collective-permute-start.1 = (bf16[32,3,512]{2,1,0:T(4,128)(2,1)S(1)}, bf16[32,3,512]{2,1,0:T(4,128)(2,1)S(1)}, u32[]{:S(2)}, u32[]{:S(2)}) collective-permute-start(bf16[32,3,512]{2,1,0:T(4,128)(2,1)S(1)} %get-tuple-element.39), channel_id=1, source_target_pairs={{1,0},{2,1},{3,2},{4,3},{5,4},{6,5},{7,6},{8,7},{9,8},{10,9},{11,1... | collective-permute-start | bytes 294920 | tf_op jit(solution)/shard_map/ppermute | solution.py:438
  2.6 6.0 %collective-permute-start = (bf16[32,3,512]{2,1,0:T(4,128)(2,1)S(1)}, bf16[32,3,512]{2,1,0:T(4,128)(2,1)S(1)}, u32[]{:S(2)}, u32[]{:S(2)}) collective-permute-start(bf16[32,3,512]{2,1,0:T(4,128)(2,1)S(1)} %get-tuple-element.40), channel_id=1, source_target_pairs={{0,1},{1,2},{2,3},{3,4},{4,5},{5,6},{6,7},{7,8},{8,9},{9,10},{10,1... | collective-permute-start | bytes 294920 | tf_op jit(solution)/shard_map/ppermute | solution.py:437
  5.2 2.7 %copy-start = (bf16[32,16,512]{2,1,0:T(8,128)(2,1)S(1)}, bf16[32,16,512]{2,1,0:T(8,128)(2,1)}, u32[]{:S(2)}) copy-start(bf16[32,16,512]{2,1,0:T(8,128)(2,1)} %param.7) | copy-start | bytes 1572868
  5.2 2.7 %copy-start.1 = (f32[4,512]{1,0:T(4,128)S(1)}, f32[4,512]{1,0:T(4,128)}, u32[]{:S(2)}) copy-start(f32[4,512]{1,0:T(4,128)} %gains_ref.7) | copy-start | bytes 24580
  9.2 10.3 %collective-permute-start.2 = (bf16[3,24,512]{2,1,0:T(8,128)(2,1)S(1)}, bf16[3,24,512]{2,1,0:T(8,128)(2,1)S(1)}, u32[]{:S(2)}, u32[]{:S(2)}) collective-permute-start(bf16[3,24,512]{2,1,0:T(8,128)(2,1)S(1)} %get-tuple-element.37), channel_id=1, source_target_pairs={{0,16},{16,32},{32,48},{48,64},{64,80},{80,96},{96,112},{112,0},{1... | collective-permute-start | bytes 221192 | tf_op jit(solution)/shard_map/ppermute | solution.py:437
  10.9 8.7 %collective-permute-start.3 = (bf16[3,24,512]{2,1,0:T(8,128)(2,1)S(1)}, bf16[3,24,512]{2,1,0:T(8,128)(2,1)S(1)}, u32[]{:S(2)}, u32[]{:S(2)}) collective-permute-start(bf16[3,24,512]{2,1,0:T(8,128)(2,1)S(1)} %get-tuple-element.38), channel_id=1, source_target_pairs={{16,0},{32,16},{48,32},{64,48},{80,64},{96,80},{112,96},{0,112},{1... | collective-permute-start | bytes 221192 | tf_op jit(solution)/shard_map/ppermute | solution.py:438

commit v9 on v8

--- a/solution.py
+++ b/solution.py
@@ -409,21 +409,34 @@
     )(rows, gains, bias, wqkv, wp, wu, wd)
 
 
-def place_kernel(in_ref, out_ref, stage):
-    stage[...] = in_ref[...].astype(F32).reshape(2048, 128)
-    for r in range(8):
-        for slot in range(4):
-            parts = [stage[pl.ds(r * 256 + slot * 4 + f, 16, stride=16), :] for f in range(4)]
-            out_ref[slot % 2 * 16 + 2 * r + slot // 2] = jnp.concatenate(parts, axis=1).astype(BF16)
+def place_kernel(in_ref, out_far, stage, out, sems):
+    copies = []
+    for part in range(4):
+        rows = slice(part * 512, (part + 1) * 512)
+        stage[rows, :] = in_ref[part * 32 : (part + 1) * 32].astype(F32).reshape(512, 128)
+        for r in (2 * part, 2 * part + 1):
+            for slot in range(4):
+                pieces = [stage[pl.ds(r * 256 + slot * 4 + f, 16, stride=16), :] for f in range(4)]
+                out[slot % 2 * 16 + 2 * r + slot // 2] = jnp.concatenate(pieces, axis=1).astype(BF16)
+        for half in range(2):
+            at = pl.ds(half * 16 + part * 4, 4)
+            copies.append(pltpu.make_async_copy(out.at[at], out_far.at[at], sems.at[part * 2 + half]))
+            copies[-1].start()
+    for c in copies:
+        c.wait()
 
 
 def place_call(rows):
     return pl.pallas_call(
         place_kernel,
         in_specs=[VM],
-        out_specs=VM,
+        out_specs=FAR,
         out_shape=jax.ShapeDtypeStruct((TR, TC, D), BF16),
-        scratch_shapes=[pltpu.VMEM((2048, 128), F32)],
+        scratch_shapes=[
+            pltpu.VMEM((2048, 128), F32),
+            pltpu.VMEM((TR, TC, D), BF16),
+            pltpu.SemaphoreType.DMA((8,)),
+        ],
         compiler_params=pltpu.CompilerParams(vmem_limit_bytes=SMALL),
         name="place",
     )(rows)

time: 73.4 us -> 73.5 us (level)
  no operation moved by 1% of the time
where the time goes in v9:
time: 73.5 us; the launch traced here: 73.3 us
  blocking collectives  40.3 us (55%)
  Pallas kernels  20.3 us (28%)
  starting transfers between devices  9.3 us (13%)
  local copies, waits for them, and re-layouts  2.42 us (3%)
    all_to_all x2, blocking collectives, exchange(): return lax.all_to_all(rows, ('row', 'col'), 0, 0, tiled=True)  40.3 us
    pallas_call x1, Pallas kernels, group_call(): pl.pallas_call(group_kernel, in_specs=[VM] * 4 + [FAR] * 3, out_specs=VM,...  7.43 us
    ppermute x2, starting transfers between devices, edges(): lax.ppermute(head, axis, [((i + 1) % count, i) for i in range(count)])  6.33 us
    pallas_call x1, Pallas kernels, local_call(): pl.pallas_call(local_kernel, in_specs=[VM] * 6 + [FAR] + [VM] * 6, out_sp...  4.72 us
    pallas_call x1, Pallas kernels, inner_call(): pl.pallas_call(inner_kernel, in_specs=[VM] * 5 + [FAR] * 3, out_specs=[VM...  3.73 us
    ppermute x2, starting transfers between devices, edges(): lax.ppermute(tail, axis, [(i, (i + 1) % count) for i in range(count)])  2.97 us
    pallas_call x1, Pallas kernels, bias_call(): pl.pallas_call(bias_kernel, in_specs=[pl.BlockSpec(memory_space=pltpu.SME...  2.66 us
  transfers between devices with their start and end apart: 4, of which 0 were waited for; matrix products, arithmetic and copies ran while one was open for 2% of the time, Pallas kernels for 10%

profile of v9, /device:TPU:1, one launch (start us, length us, event | category | flops | bytes accessed | tf_op | source)
XLA Modules:
  0.0 73.3 jit_solution(4463997210688082437)
XLA Ops:
  0.0 1.1 %fusion.1 = (bf16[32,3,512]{2,1,0:T(4,128)(2,1)S(1)}, bf16[32,3,512]{2,1,0:T(4,128)(2,1)S(1)}) fusion(bf16[32,16,512]{2,1,0:T(8,128)(2,1)} %param.7), kind=kLoop, calls=%fused_computation.4 | loop fusion | bytes 393216 | tf_op jit(solution)/shard_map/slice | solution.py:448
  1.1 1.5 %collective-permute-start.1 = (bf16[32,3,512]{2,1,0:T(4,128)(2,1)S(1)}, bf16[32,3,512]{2,1,0:T(4,128)(2,1)S(1)}, u32[]{:S(2)}, u32[]{:S(2)}) collective-permute-start(bf16[32,3,512]{2,1,0:T(4,128)(2,1)S(1)} %get-tuple-element.39), channel_id=1, source_target_pairs={{1,0},{2,1},{3,2},{4,3},{5,4},{6,5},{7,6},{8,7},{9,8},{10,9},{11,1... | collective-permute-start | bytes 294920 | tf_op jit(solution)/shard_map/ppermute | solution.py:451
  2.6 1.3 %collective-permute-start = (bf16[32,3,512]{2,1,0:T(4,128)(2,1)S(1)}, bf16[32,3,512]{2,1,0:T(4,128)(2,1)S(1)}, u32[]{:S(2)}, u32[]{:S(2)}) collective-permute-start(bf16[32,3,512]{2,1,0:T(4,128)(2,1)S(1)} %get-tuple-element.40), channel_id=1, source_target_pairs={{0,1},{1,2},{2,3},{3,4},{4,5},{5,6},{6,7},{7,8},{8,9},{9,10},{10,1... | collective-permute-start | bytes 294920 | tf_op jit(solution)/shard_map/ppermute | solution.py:450
  3.9 1.1 %copy.8 = f32[2,16,13,13]{3,1,2,0:T(8,128)S(1)} copy(f32[2,16,13,13]{1,0,3,2:T(2,128)} %param.10) | data formatting | bytes 43264 | tf_op args[3]
  5.0 0.1 pad.10.clone
  5.1 0.1 pad_add_fusion.place_ref
  5.2 2.7 %biases.1 = (f32[3,4,256,256]{3,2,1,0:T(8,128)S(1)}, f32[5,4,128,128]{3,2,1,0:T(8,128)S(1)}, bf16[512,1536]{1,0:T(8,128)(2,1)S(1)}) custom-call(s32[2]{0:T(128)S(1)} %pad_add_fusion.place_ref, f32[2,13,16,13]{3,2,1,0:T(8,128)S(1)} %bitcast.9, bf16[2,512,1536]{2,1,0:T(8,128)(2,1)} %w_far.3), custom_call_target="tpu_custom_call" | custom-call | flops 8000000 | bytes 5242880 | tf_op jit(solution)/shard_map/biases/pallas_call | solution.py:180
  7.9 0.0 copy-done
  7.9 0.0 copy-done.1
  7.9 0.7 query.1.q_ref
  8.6 0.0 collective-permute-done.1
  8.6 0.0 collective-permute-done
  8.6 0.5 maximum_maximum_fusion
  9.2 1.7 %collective-permute-start.2 = (bf16[3,24,512]{2,1,0:T(8,128)(2,1)S(1)}, bf16[3,24,512]{2,1,0:T(8,128)(2,1)S(1)}, u32[]{:S(2)}, u32[]{:S(2)}) collective-permute-start(bf16[3,24,512]{2,1,0:T(8,128)(2,1)S(1)} %get-tuple-element.37), channel_id=1, source_target_pairs={{0,16},{16,32},{32,48},{48,64},{64,80},{80,96},{96,112},{112,0},{1... | collective-permute-start | bytes 221192 | tf_op jit(solution)/shard_map/ppermute | solution.py:450
  10.9 4.8 %collective-permute-start.3 = (bf16[3,24,512]{2,1,0:T(8,128)(2,1)S(1)}, bf16[3,24,512]{2,1,0:T(8,128)(2,1)S(1)}, u32[]{:S(2)}, u32[]{:S(2)}) collective-permute-start(bf16[3,24,512]{2,1,0:T(8,128)(2,1)S(1)} %get-tuple-element.38), channel_id=1, source_target_pairs={{16,0},{32,16},{48,32},{64,48},{80,64},{96,80},{112,96},{0,112},{1... | collective-permute-start | bytes 221192 | tf_op jit(solution)/shard_map/ppermute | solution.py:451
  15.7 0.1 pad.4.wide_ref
  15.8 3.7 %inner_blocks.1 = (bf16[512,512]{1,0:T(8,128)(2,1)S(1)}, bf16[928,512]{1,0:T(8,128)(2,1)S(1)}, bf16[928,1024]{1,0:T(8,128)(2,1)S(1)}, bf16[512,512]{1,0:T(8,128)...) custom-call(bf16[784,512]{1,0:T(8,128)(2,1)S(1)} %pad.4.wide_ref, ...), custom_call_target="tpu_custom_call" | custom-call | flops 4000000000 | bytes 8000000 | tf_op jit(solution)/shard_map/inner_blocks/pallas_call | solution.py:258
  19.5 0.0 collective-permute-done.2
  19.5 0.0 collective-permute-done.3
  19.5 4.7 %local_layer.1 = (bf16[128,16,128]{2,1,0:T(8,128)(2,1)S(1)}, bf16[512,1536]{1,0:T(8,128)(2,1)S(1)}) custom-call(bf16[144,512]{1,0:T(8,128)(2,1)S(1)} %pad_maximum_fusion.edge_ref, bf16[512,512]{1,0:T(8,128)(2,1)S(1)} %bitcast.8, bf16[512,512]{1,0:T(8,128)(2,1)S(1)} %query.1.q_ref, f32[4,512]{1,0:T(4,128)S(1)} %copy-done.1, ...), custom_call_target="tpu_custom_call" | custom-call | flops 4000000000 | bytes 8000000 | tf_op jit(solution)/shard_map/local_layer/pallas_call | solution.py:322
  24.3 22.8 %all_to_all.10.in_ref = bf16[128,16,128]{2,1,0:T(8,128)(2,1)S(1)} all-to-all(bf16[128,16,128]{2,1,0:T(8,128)(2,1)S(1)} %get-tuple-element.34), channel_id=1, replica_groups=mesh['row'=8,'col'=16] {'row','col'}, dimensions={0} | all-to-all | bytes 1048576 | tf_op jit(solution)/shard_map/all_to_all | solution.py:456
  47.0 7.4 %group_layer.1 = bf16[128,16,128]{2,1,0:T(8,128)(2,1)S(1)} custom-call(bf16[128,16,128]{2,1,0:T(8,128)(2,1)S(1)} %all_to_all.10.in_ref, f32[4,512]{1,0:T(4,128)S(1)} %copy-done.1, f32[5,4,128,128]{3,2,1,0:T(8,128)S(1)} %get-tuple-element.35.bias, bf16[512,1536]{1,0:T(8,128)(2,1)S(1)} %get-tuple-element.36.wqkv, bf16[2,512,512]{2,1,0:T(8,128)(2,1)} %wp_far.3, ...), custom_call_target="tpu_custom_call" | custom-call | flops 7000000000 | bytes 10000000 | tf_op jit(solution)/shard_map/group_layer/pallas_call | solution.py:392
  54.5 17.5 %all_to_all.11.in_ref = bf16[128,16,128]{2,1,0:T(8,128)(2,1)S(1)} all-to-all(bf16[128,16,128]{2,1,0:T(8,128)(2,1)S(1)} %group_layer.1), channel_id=1, replica_groups=mesh['row'=8,'col'=16] {'row','col'}, dimensions={0} | all-to-all | bytes 1048576 | tf_op jit(solution)/shard_map/all_to_all | solution.py:456
  72.0 1.1 %place.1 = bf16[32,16,512]{2,1,0:T(8,128)(2,1)} custom-call(bf16[128,16,128]{2,1,0:T(8,128)(2,1)S(1)} %all_to_all.11.in_ref), custom_call_target="tpu_custom_call" | custom-call | tf_op jit(solution)/shard_map/place/pallas_call | solution.py:430
  (5 shorter events, 0.0 us)
Async XLA Ops:
  1.1 7.5 %collective-permute-start.1 = (bf16[32,3,512]{2,1,0:T(4,128)(2,1)S(1)}, bf16[32,3,512]{2,1,0:T(4,128)(2,1)S(1)}, u32[]{:S(2)}, u32[]{:S(2)}) collective-permute-start(bf16[32,3,512]{2,1,0:T(4,128)(2,1)S(1)} %get-tuple-element.39), channel_id=1, source_target_pairs={{1,0},{2,1},{3,2},{4,3},{5,4},{6,5},{7,6},{8,7},{9,8},{10,9},{11,1... | collective-permute-start | bytes 294920 | tf_op jit(solution)/shard_map/ppermute | solution.py:451
  2.6 6.0 %collective-permute-start = (bf16[32,3,512]{2,1,0:T(4,128)(2,1)S(1)}, bf16[32,3,512]{2,1,0:T(4,128)(2,1)S(1)}, u32[]{:S(2)}, u32[]{:S(2)}) collective-permute-start(bf16[32,3,512]{2,1,0:T(4,128)(2,1)S(1)} %get-tuple-element.40), channel_id=1, source_target_pairs={{0,1},{1,2},{2,3},{3,4},{4,5},{5,6},{6,7},{7,8},{8,9},{9,10},{10,1... | collective-permute-start | bytes 294920 | tf_op jit(solution)/shard_map/ppermute | solution.py:450
  5.2 2.7 %copy-start = (bf16[32,16,512]{2,1,0:T(8,128)(2,1)S(1)}, bf16[32,16,512]{2,1,0:T(8,128)(2,1)}, u32[]{:S(2)}) copy-start(bf16[32,16,512]{2,1,0:T(8,128)(2,1)} %param.7) | copy-start | bytes 1572868
  5.2 2.7 %copy-start.1 = (f32[4,512]{1,0:T(4,128)S(1)}, f32[4,512]{1,0:T(4,128)}, u32[]{:S(2)}) copy-start(f32[4,512]{1,0:T(4,128)} %gains_ref.7) | copy-start | bytes 24580
  9.2 10.3 %collective-permute-start.2 = (bf16[3,24,512]{2,1,0:T(8,128)(2,1)S(1)}, bf16[3,24,512]{2,1,0:T(8,128)(2,1)S(1)}, u32[]{:S(2)}, u32[]{:S(2)}) collective-permute-start(bf16[3,24,512]{2,1,0:T(8,128)(2,1)S(1)} %get-tuple-element.37), channel_id=1, source_target_pairs={{0,16},{16,32},{32,48},{48,64},{64,80},{80,96},{96,112},{112,0},{1... | collective-permute-start | bytes 221192 | tf_op jit(solution)/shard_map/ppermute | solution.py:450
  10.9 8.7 %collective-permute-start.3 = (bf16[3,24,512]{2,1,0:T(8,128)(2,1)S(1)}, bf16[3,24,512]{2,1,0:T(8,128)(2,1)S(1)}, u32[]{:S(2)}, u32[]{:S(2)}) collective-permute-start(bf16[3,24,512]{2,1,0:T(8,128)(2,1)S(1)} %get-tuple-element.38), channel_id=1, source_target_pairs={{16,0},{32,16},{48,32},{64,48},{80,64},{96,80},{112,96},{0,112},{1... | collective-permute-start | bytes 221192 | tf_op jit(solution)/shard_map/ppermute | solution.py:451
